TPU v7x, 32 devices: a whole 2x2x4 slice. The times are simulated.
32 devices in a mesh: dp: 16 (over z, y, core), tensor: 2 (over x).
Axes of the slice: x: 2, y: 2, z: 4, core: 2. Of those that a mesh axis runs over, the one named last changes fastest.
Arguments:
- inputs: bfloat16 [4096, 1024], P('dp', 'tensor'), may hold values from -6 to 6
- cotangent: bfloat16 [4096, 1024], P('dp', 'tensor'), may hold values from -6 to 6
- attn_gain: float32 [1024], replicated, may hold values from 0.5 to 1.5
- expert_gain: float32 [1024], replicated, may hold values from 0.5 to 1.5
- query_weight: bfloat16 [1024, 1024], P(None, 'tensor'), may hold values from -0.5 to 0.5
- key_weight: bfloat16 [1024, 512], P(None, 'tensor'), may hold values from -0.5 to 0.5
- value_weight: bfloat16 [1024, 512], P(None, 'tensor'), may hold values from -0.1875 to 0.1875
- output_weight: bfloat16 [1024, 1024], P('tensor'), may hold values from -1.5 to 1.5
- router_weight: bfloat16 [1024, 32], replicated, may hold values from -0.09375 to 0.09375
- gate_weight: bfloat16 [32, 1024, 512], P(None, 'dp', 'tensor'), may hold values from -0.1875 to 0.1875
- up_weight: bfloat16 [32, 1024, 512], P(None, 'dp', 'tensor'), may hold values from -0.1875 to 0.1875
- down_weight: bfloat16 [32, 512, 1024], P(None, 'tensor', 'dp'), may hold values from -2 to 2
- routes: int32 [4096, 8], P('dp'), may hold values from 0 to 31, all different within a row
- lengths: int32 [16, 4], replicated, may hold values from 1 to 128, 224 in all within a row
- placement: int32 [16], replicated, may hold values from 0 to 15, each once
Outputs:
- outputs: bfloat16 [4096, 1024], P('dp', 'tensor')
- input_grad: float32 [4096, 1024], P('dp', 'tensor')
- attn_gain_grad: float32 [1024], P('dp')
- expert_gain_grad: float32 [1024], P('dp')
- query_weight_grad: float32 [1024, 1024], P('dp', 'tensor')
- key_weight_grad: float32 [1024, 512], P('dp', 'tensor')
- value_weight_grad: float32 [1024, 512], P('dp', 'tensor')
- output_weight_grad: float32 [1024, 1024], P('tensor', 'dp')
- router_weight_grad: float32 [1024, 32], P('dp')
- gate_weight_grad: float32 [32, 1024, 512], P(None, 'dp', 'tensor')
- up_weight_grad: float32 [32, 1024, 512], P(None, 'dp', 'tensor')
- down_weight_grad: float32 [32, 512, 1024], P(None, 'tensor', 'dp')
Inputs may be any that keep to these rules, and one draw needn't show every extreme that they name: Row s lists the lengths of the 4 sequences of slot s, packed in this order from the slot's first token; each row sums to 224 and its largest entry is 128; the other 32 tokens of a slot are padding. Slot s is processed by dp device placement[s]; rows d * 256 to (d + 1) * 256 - 1 of inputs, cotangent and routes are the tokens of the slot that device d processes. `routes`: each row names 8 different experts; rows of padding are ignored.
All inputs are finite; a program needn't handle non-finite values.
Results may differ from a plain program's by a relative error of at most 0.023.
Values may be sent and summed in bfloat16 or wider, within the bound.
No kernel may reach another device: no remote copies, remote signals or barrier semaphores. Data moves between devices by JAX's collectives and lax.ppermute only.
A program may use at most 256 MiB of HBM per device.

v0:
```python
import jax
import jax.numpy as jnp
from jax import lax
from jax.sharding import PartitionSpec as P

HEAD_DIM = 64


EPSILON = 1e-06
ROPE_BASE = 10000.0
PRECISE = lax.Precision.HIGHEST
NEGATIVE = -1e30


def rope_tables(positions, half_dim):
    freq_index = jnp.arange(half_dim, dtype=jnp.int32).astype(jnp.float32)
    frequency = jnp.exp(-(2.0 * freq_index / (2.0 * half_dim)) * jnp.log(ROPE_BASE))
    angles = positions.astype(jnp.float32)[:, None] * frequency[None, :]
    return (jnp.cos(angles)[:, None, :], jnp.sin(angles)[:, None, :])


def rotate(values, cos_table, sin_table):
    half_dim = values.shape[-1] // 2
    first_half = values[..., :half_dim]
    second = values[..., half_dim:]
    return jnp.concatenate(
        [first_half * cos_table - second * sin_table, second * cos_table + first_half * sin_table],
        axis=-1,
    )


def rotate_back(values, cos_table, sin_table):
    half_dim = values.shape[-1] // 2
    first_half = values[..., :half_dim]
    second = values[..., half_dim:]
    return jnp.concatenate(
        [first_half * cos_table + second * sin_table, second * cos_table - first_half * sin_table],
        axis=-1,
    )


def split_parts(values):
    upper = values.astype(jnp.bfloat16)
    lower = (values - upper.astype(jnp.float32)).astype(jnp.bfloat16)
    return (upper, lower)


def split_dot(one_hot, values):
    upper, lower = split_parts(values)
    return jnp.dot(one_hot, upper, preferred_element_type=jnp.float32) + jnp.dot(
        one_hot, lower, preferred_element_type=jnp.float32
    )


def reroute(first_rows, second_rows):
    return (
        lax.all_to_all(
            first_rows.astype(jnp.bfloat16), "dp", split_axis=0, concat_axis=0, tiled=True
        ).astype(first_rows.dtype),
        lax.all_to_all(
            second_rows.astype(jnp.bfloat16), "dp", split_axis=0, concat_axis=0, tiled=True
        ).astype(second_rows.dtype),
    )


def slot_layout(slot_lengths, slot_routes, capacity, window):
    row_count = slot_routes.shape[0]
    top_count = slot_routes.shape[1]
    seq_count = slot_lengths.shape[0]
    seg_ends = jnp.cumsum(slot_lengths)
    seg_starts = seg_ends - slot_lengths
    row_index = jnp.arange(row_count, dtype=jnp.int32)
    segment = jnp.sum((row_index[:, None] >= seg_ends[None, :]).astype(jnp.int32), axis=1)
    seg_begins = jnp.concatenate([seg_starts, seg_ends[-1:]])
    seg_ids = jnp.arange(seq_count + 1, dtype=jnp.int32)
    begin_row = jnp.sum(
        jnp.where(segment[:, None] == seg_ids[None, :], seg_begins[None, :], 0), axis=1
    )
    positions = row_index - begin_row
    token_live = segment < seq_count
    flat_routes = slot_routes.reshape(row_count * top_count)
    live_pairs = (
        flat_routes[:, None] == jnp.arange(window, dtype=jnp.int32)[None, :]
    ) & jnp.repeat(token_live, top_count)[:, None]
    live_int = live_pairs.astype(jnp.int32)
    earlier = jnp.cumsum(live_int, axis=0) - live_int
    slot_place = jnp.sum(earlier * live_int, axis=1)
    kept_pairs = (jnp.sum(live_int, axis=1) > 0) & (slot_place < capacity)
    slot_index = jnp.where(kept_pairs, flat_routes * capacity + slot_place, -1).reshape(
        row_count, top_count
    )
    return (segment, positions, token_live, slot_index)


def local(
    inputs,
    cotangent,
    attn_gain,
    expert_gain,
    query_weight,
    key_weight,
    value_weight,
    output_weight,
    router_weight,
    gate_weight,
    up_weight,
    down_weight,
    routes,
    lengths,
    placement,
):
    row_count = routes.shape[0]
    top_count = routes.shape[1]
    expert_count = router_weight.shape[1]
    window = gate_weight.shape[0]
    capacity = row_count * top_count // expert_count
    slot_count = window * capacity
    kv_local = key_weight.shape[1] // HEAD_DIM
    heads_local = query_weight.shape[1] // HEAD_DIM
    group = heads_local // kv_local
    scale = 1.0 / HEAD_DIM
    width_half = inputs.shape[1]
    offset = lax.axis_index("tensor") * width_half
    devices = lax.axis_size("dp")
    dp_index = lax.axis_index("dp")
    rank_list = jnp.arange(devices, dtype=jnp.int32)
    holder = jnp.sum(jnp.where(placement == dp_index, rank_list, 0))
    slot_lengths = lax.dynamic_index_in_dim(lengths, holder, 0, keepdims=False)
    segment, positions, token_live, slot_index = slot_layout(slot_lengths, routes, capacity, window)
    row_index = jnp.arange(row_count, dtype=jnp.int32)
    allowed = (segment[:, None] == segment[None, :]) & (row_index[None, :] <= row_index[:, None])
    cos_table, sin_table = rope_tables(positions, HEAD_DIM // 2)
    live_column = token_live.astype(jnp.float32)[:, None]
    full_inputs, full_cot = (
        lax.all_gather(inputs, "tensor", axis=1, tiled=True),
        lax.all_gather(cotangent, "tensor", axis=1, tiled=True),
    )
    wide_inputs = full_inputs.astype(jnp.float32)
    attn_scale = lax.rsqrt(jnp.mean(wide_inputs * wide_inputs, axis=-1, keepdims=True) + EPSILON)
    normed = (wide_inputs * attn_scale * attn_gain).astype(jnp.bfloat16)
    query_pre = jnp.dot(normed, query_weight, preferred_element_type=jnp.float32)
    key_pre = jnp.dot(normed, key_weight, preferred_element_type=jnp.float32)
    value_pre = jnp.dot(normed, value_weight, preferred_element_type=jnp.float32)
    query_rot = (
        rotate(query_pre.reshape(row_count, heads_local, HEAD_DIM), cos_table, sin_table)
        .astype(jnp.bfloat16)
        .reshape(row_count, kv_local, group, HEAD_DIM)
    )
    key_rot = rotate(key_pre.reshape(row_count, kv_local, HEAD_DIM), cos_table, sin_table).astype(
        jnp.bfloat16
    )
    value_rows = value_pre.astype(jnp.bfloat16).reshape(row_count, kv_local, HEAD_DIM)

    def masked_scores():
        raw_scores = (
            jnp.einsum("qhgd,khd->hgqk", query_rot, key_rot, preferred_element_type=jnp.float32)
            * scale
        )
        return jnp.where(allowed, raw_scores, NEGATIVE)

    masked = masked_scores()
    row_max = jnp.max(masked, axis=-1, keepdims=True)
    exp_terms = jnp.exp(masked - row_max)
    row_total = jnp.sum(exp_terms, axis=-1, keepdims=True)
    attn_probs = exp_terms / row_total
    log_total = row_max + jnp.log(row_total)
    context = jnp.einsum(
        "hgqk,khd->qhgd",
        attn_probs.astype(jnp.bfloat16),
        value_rows,
        preferred_element_type=jnp.float32,
    ).reshape(row_count, heads_local * HEAD_DIM)
    context = (context * live_column).astype(jnp.bfloat16)
    attn_part = jnp.dot(context, output_weight, preferred_element_type=jnp.float32)
    attn_whole = lax.psum(attn_part.astype(jnp.bfloat16), "tensor").astype(jnp.float32)
    residual = wide_inputs + attn_whole
    expert_scale = lax.rsqrt(jnp.mean(residual * residual, axis=-1, keepdims=True) + EPSILON)
    mixed_rows = (residual * expert_scale * expert_gain).astype(jnp.bfloat16)
    logits = jnp.dot(mixed_rows, router_weight, preferred_element_type=jnp.float32)
    pick_all = (
        routes[:, :, None] == jnp.arange(expert_count, dtype=jnp.int32)[None, None, :]
    ).astype(jnp.float32)
    pick_window = (routes[:, :, None] == jnp.arange(window, dtype=jnp.int32)[None, None, :]).astype(
        jnp.float32
    )
    gate_probs = jax.nn.softmax(
        jnp.einsum("tkn,tn->tk", pick_all, logits, precision=PRECISE), axis=-1
    )
    token_gates = jnp.einsum("tk,tke->te", gate_probs, pick_window, precision=PRECISE)
    columns = jnp.arange(slot_count, dtype=jnp.int32)
    dispatch = jnp.zeros((row_count, slot_count), jnp.bfloat16)
    for pick in range(top_count):
        dispatch = dispatch + (slot_index[:, pick : pick + 1] == columns[None, :]).astype(
            jnp.bfloat16
        )
    dispatch_three = dispatch.astype(jnp.float32).reshape(row_count, window, capacity)
    gate_slot = jnp.einsum("te,tec->ec", token_gates, dispatch_three, precision=PRECISE).reshape(
        slot_count
    )
    slot_in = (
        lax.dot_general(
            dispatch, mixed_rows, (((0,), (0,)), ((), ())), preferred_element_type=jnp.float32
        )
        .astype(jnp.bfloat16)
        .reshape(window, capacity, -1)
    )
    gate_full, up_full, down_full = (
        lax.all_gather(gate_weight, "dp", axis=1, tiled=True),
        lax.all_gather(up_weight, "dp", axis=1, tiled=True),
        lax.all_gather(down_weight, "dp", axis=2, tiled=True),
    )
    gate_pre = jnp.einsum("ecd,edf->ecf", slot_in, gate_full, preferred_element_type=jnp.float32)
    up_pre = jnp.einsum("ecd,edf->ecf", slot_in, up_full, preferred_element_type=jnp.float32)
    sigma = jax.nn.sigmoid(gate_pre)
    hidden = (gate_pre * sigma * up_pre).astype(jnp.bfloat16)
    expert_out = jnp.einsum(
        "ecf,efd->ecd", hidden, down_full, preferred_element_type=jnp.float32
    ).reshape(slot_count, -1)
    moe_part = split_dot(dispatch, gate_slot[:, None] * expert_out)
    moe_half = lax.psum_scatter(
        moe_part.astype(jnp.bfloat16), "tensor", scatter_dimension=1, tiled=True
    ).astype(jnp.float32)
    residual_half = lax.dynamic_slice_in_dim(residual, offset, width_half, 1)
    outputs_half = (residual_half + moe_half).astype(jnp.bfloat16)
    cot_wide = full_cot.astype(jnp.float32)
    slot_cot = lax.dot_general(
        dispatch, full_cot, (((0,), (0,)), ((), ())), preferred_element_type=jnp.float32
    )
    gate_slot_grad = jnp.sum(slot_cot * expert_out, axis=1)
    slot_grad = (gate_slot[:, None] * slot_cot).astype(jnp.bfloat16).reshape(window, capacity, -1)
    down_w_grad = jnp.einsum("ecf,ecd->efd", hidden, slot_grad, preferred_element_type=jnp.float32)
    hidden_grad = jnp.einsum(
        "ecd,efd->ecf", slot_grad, down_full, preferred_element_type=jnp.float32
    )
    gate_pre_grad = (hidden_grad * up_pre * sigma * (1.0 + gate_pre * (1.0 - sigma))).astype(
        jnp.bfloat16
    )
    up_pre_grad = (hidden_grad * gate_pre * sigma).astype(jnp.bfloat16)
    gate_w_grad = jnp.einsum(
        "ecd,ecf->edf", slot_in, gate_pre_grad, preferred_element_type=jnp.float32
    )
    up_w_grad = jnp.einsum("ecd,ecf->edf", slot_in, up_pre_grad, preferred_element_type=jnp.float32)
    slot_in_grad = (
        jnp.einsum("ecf,edf->ecd", gate_pre_grad, gate_full, preferred_element_type=jnp.float32)
        + jnp.einsum("ecf,edf->ecd", up_pre_grad, up_full, preferred_element_type=jnp.float32)
    ).reshape(slot_count, -1)
    token_gate_grad = jnp.einsum(
        "tec,ec->te", dispatch_three, gate_slot_grad.reshape(window, capacity), precision=PRECISE
    )
    gates_grad = jnp.einsum("tke,te->tk", pick_window, token_gate_grad, precision=PRECISE)
    picked_grad = gate_probs * (
        gates_grad - jnp.sum(gate_probs * gates_grad, axis=-1, keepdims=True)
    )
    logits_grad = jnp.einsum("tkn,tk->tn", pick_all, picked_grad, precision=PRECISE)
    logits_upper, logits_lower = split_parts(logits_grad)
    router_part = lax.dot_general(
        mixed_rows, logits_upper, (((0,), (0,)), ((), ())), preferred_element_type=jnp.float32
    ) + lax.dot_general(
        mixed_rows, logits_lower, (((0,), (0,)), ((), ())), preferred_element_type=jnp.float32
    )
    mixed_part = split_dot(dispatch, slot_in_grad)
    mixed_part = (
        mixed_part
        + jnp.einsum("tn,dn->td", logits_upper, router_weight, preferred_element_type=jnp.float32)
        + jnp.einsum("tn,dn->td", logits_lower, router_weight, preferred_element_type=jnp.float32)
    )
    mixed_grad, router_grad = (
        lax.psum(mixed_part.astype(jnp.bfloat16), "tensor").astype(jnp.float32),
        lax.psum(router_part.astype(jnp.bfloat16), "tensor").astype(jnp.float32),
    )
    scaled_two = mixed_grad * expert_gain
    expert_gain_grad = jnp.sum(mixed_grad * residual * expert_scale, axis=0)
    cube_two = expert_scale * expert_scale * expert_scale
    residual_grad = (
        cot_wide
        + expert_scale * scaled_two
        - residual * cube_two * jnp.mean(scaled_two * residual, axis=-1, keepdims=True)
    )
    residual_low = residual_grad.astype(jnp.bfloat16)
    output_w_grad = lax.dot_general(
        context, residual_low, (((0,), (0,)), ((), ())), preferred_element_type=jnp.float32
    )
    context_grad = jnp.einsum(
        "td,hd->th", residual_low, output_weight, preferred_element_type=jnp.float32
    ).astype(jnp.bfloat16)
    context_grad = jnp.where(
        token_live[:, None], context_grad, jnp.zeros_like(context_grad)
    ).reshape(row_count, kv_local, group, HEAD_DIM)
    again = masked_scores()
    probs_again = jnp.exp(again - log_total)
    prob_grad = jnp.einsum(
        "qhgd,khd->hgqk", context_grad, value_rows, preferred_element_type=jnp.float32
    )
    row_inner = jnp.sum(probs_again * prob_grad, axis=-1, keepdims=True)
    score_grad = (probs_again * (prob_grad - row_inner)).astype(jnp.bfloat16)
    query_grad = (
        jnp.einsum("hgqk,khd->qhgd", score_grad, key_rot, preferred_element_type=jnp.float32)
        * scale
    )
    key_grad = (
        jnp.einsum("hgqk,qhgd->khd", score_grad, query_rot, preferred_element_type=jnp.float32)
        * scale
    )
    value_grad = jnp.einsum(
        "hgqk,qhgd->khd",
        probs_again.astype(jnp.bfloat16),
        context_grad,
        preferred_element_type=jnp.float32,
    )
    query_pre_grad = (
        rotate_back(query_grad.reshape(row_count, heads_local, HEAD_DIM), cos_table, sin_table)
        .astype(jnp.bfloat16)
        .reshape(row_count, -1)
    )
    key_pre_grad = (
        rotate_back(key_grad, cos_table, sin_table).astype(jnp.bfloat16).reshape(row_count, -1)
    )
    value_pre_grad = value_grad.astype(jnp.bfloat16).reshape(row_count, -1)
    query_w_grad = lax.dot_general(
        normed, query_pre_grad, (((0,), (0,)), ((), ())), preferred_element_type=jnp.float32
    )
    key_w_grad = lax.dot_general(
        normed, key_pre_grad, (((0,), (0,)), ((), ())), preferred_element_type=jnp.float32
    )
    value_w_grad = lax.dot_general(
        normed, value_pre_grad, (((0,), (0,)), ((), ())), preferred_element_type=jnp.float32
    )
    normed_part = jnp.einsum(
        "th,dh->td", query_pre_grad, query_weight, preferred_element_type=jnp.float32
    )
    normed_part = normed_part + jnp.einsum(
        "th,dh->td", key_pre_grad, key_weight, preferred_element_type=jnp.float32
    )
    normed_part = normed_part + jnp.einsum(
        "th,dh->td", value_pre_grad, value_weight, preferred_element_type=jnp.float32
    )
    normed_grad = lax.psum(normed_part.astype(jnp.bfloat16), "tensor").astype(jnp.float32)
    scaled_one = normed_grad * attn_gain
    attn_gain_grad = jnp.sum(normed_grad * wide_inputs * attn_scale, axis=0)
    cube_one = attn_scale * attn_scale * attn_scale
    input_grad = (
        residual_grad
        + attn_scale * scaled_one
        - wide_inputs * cube_one * jnp.mean(scaled_one * wide_inputs, axis=-1, keepdims=True)
    )
    input_half = lax.dynamic_slice_in_dim(input_grad, offset, width_half, 1)
    (
        query_part,
        key_part,
        value_part,
        output_part,
        router_share,
        attn_gain_part,
        expert_gain_part,
        gate_w_part,
        up_w_part,
        down_w_part,
    ) = (
        lax.psum_scatter(query_w_grad, "dp", scatter_dimension=0, tiled=True),
        lax.psum_scatter(key_w_grad, "dp", scatter_dimension=0, tiled=True),
        lax.psum_scatter(value_w_grad, "dp", scatter_dimension=0, tiled=True),
        lax.psum_scatter(output_w_grad, "dp", scatter_dimension=1, tiled=True),
        lax.psum_scatter(router_grad, "dp", scatter_dimension=0, tiled=True),
        lax.psum_scatter(attn_gain_grad, "dp", scatter_dimension=0, tiled=True),
        lax.psum_scatter(expert_gain_grad, "dp", scatter_dimension=0, tiled=True),
        lax.psum_scatter(gate_w_grad, "dp", scatter_dimension=1, tiled=True),
        lax.psum_scatter(up_w_grad, "dp", scatter_dimension=1, tiled=True),
        lax.psum_scatter(down_w_grad, "dp", scatter_dimension=2, tiled=True),
    )
    piece_rows = row_count // devices
    out_pieces = outputs_half.astype(jnp.float32).reshape(devices, piece_rows, width_half)
    grad_pieces = input_half.reshape(devices, piece_rows, width_half)
    spread_out, spread_grad = reroute(out_pieces, grad_pieces)
    moved_out = jnp.take(spread_out, placement, axis=0)
    moved_grad = jnp.take(spread_grad, placement, axis=0)
    final_out, final_grad = reroute(moved_out, moved_grad)
    outputs = final_out.reshape(row_count, width_half).astype(jnp.bfloat16)
    input_result = final_grad.reshape(row_count, width_half)
    return (
        outputs,
        input_result,
        attn_gain_part,
        expert_gain_part,
        query_part,
        key_part,
        value_part,
        output_part,
        router_share,
        gate_w_part,
        up_w_part,
        down_w_part,
    )


def solution(mesh):
    in_specs = (
        P("dp", "tensor"),
        P("dp", "tensor"),
        P(),
        P(),
        P(None, "tensor"),
        P(None, "tensor"),
        P(None, "tensor"),
        P("tensor", None),
        P(),
        P(None, "dp", "tensor"),
        P(None, "dp", "tensor"),
        P(None, "tensor", "dp"),
        P("dp", None),
        P(),
        P(),
    )
    out_specs = (
        P("dp", "tensor"),
        P("dp", "tensor"),
        P("dp"),
        P("dp"),
        P("dp", "tensor"),
        P("dp", "tensor"),
        P("dp", "tensor"),
        P("tensor", "dp"),
        P("dp", None),
        P(None, "dp", "tensor"),
        P(None, "dp", "tensor"),
        P(None, "tensor", "dp"),
    )
    return jax.shard_map(local, mesh=mesh, in_specs=in_specs, out_specs=out_specs, check_vma=False)
```

profile of v0, /device:TPU:0, one launch (start us, length us, event | category | flops | bytes accessed | tf_op | source)
XLA Modules:
  0.0 1958.9 jit_solution(14708146120479554742)
XLA Ops:
  8.1 1.9 compare_select_fusion
  13.8 10.2 all_gather.15
  24.8 1.5 convolution_convert_fusion.3
  35.2 9.1 reduce-window.11
  46.8 8.5 all_gather.19
  55.3 7.4 all-reduce.8.cloned.1.call-done
  62.7 1.3 multiply_reduce_fusion
  66.8 5.0 convolution_convert_fusion
  71.8 91.5 %all-gather.4.cloned.1.call-done = bf16[32,1024,256]{2,1,0:T(8,128)(2,1)} async-done(((bf16[32,64,256]{2,1,0:T(8,128)(2,1)}), bf16[32,1024,256]{2,1,0:T(8,128)(2,1)}) %all-gather.4.cloned.1.call-update) | async-done | bytes 16777232 | tf_op jit(solution)/shard_map/all_gather | solution.py:208
  163.3 11.0 fusion.109
  174.3 116.0 %all-gather.6.cloned.1.call-done = bf16[32,1024,256]{2,1,0:T(8,128)(2,1)} async-done(((bf16[32,64,256]{2,1,0:T(8,128)(2,1)}), bf16[32,1024,256]{2,1,0:T(8,128)(2,1)}) %all-gather.6.cloned.1.call-update) | async-done | bytes 16777232 | tf_op jit(solution)/shard_map/all_gather | solution.py:209
  290.3 11.7 multiply_convert_fusion.3
  302.1 115.3 %all-gather.8.cloned.1.call-done = bf16[32,256,1024]{1,2,0:T(8,128)(2,1)} async-done(((bf16[32,256,64]{1,2,0:T(8,128)(2,1)}), bf16[32,256,1024]{1,2,0:T(8,128)(2,1)}) %all-gather.8.cloned.1.call-update) | async-done | bytes 16777232 | tf_op jit(solution)/shard_map/all_gather | solution.py:210
  417.3 14.2 fusion.110
  431.5 10.3 fusion.1
  442.5 3.4 fusion.63
  445.9 1.5 copy.132
  447.4 2.9 select_reduce_fusion
  450.3 1.6 copy.118
  452.8 1.6 reduce_max.19
  455.9 1.3 multiply_bitcast_fusion
  457.2 1.5 copy.108
  458.7 2.6 fusion.54
  461.3 1.6 copy.110
  462.9 3.7 fusion.65
  467.4 10.2 subtract_convert_fusion
  477.7 11.8 multiply_convert_fusion.1
  489.5 14.5 fusion.111
  504.0 13.3 convolution_add_fusion
  517.4 7.2 fusion
  524.7 4.1 fusion.98
  529.7 2.1 fusion.53
  532.1 5.2 convolution_add_fusion.5
  538.9 1.8 fusion.25
  540.8 6.4 fusion.103
  547.2 18.4 all-reduce.10.cloned.1.call-done
  565.6 1.4 fusion.34
  567.1 2.6 fusion.27
  571.3 2.3 fusion.3
  579.4 6.0 fusion.16
  585.4 24.2 %all-reduce.12.cloned.1.call-done = (bf16[256,1024]{1,0:T(8,128)(2,1)}, bf16[1024,32]{0,1:T(8,128)(2,1)}) async-done(((bf16[256,1024]{1,0:T(8,128)(2,1)}, bf16[1024,32]{0,1:T(8,128)(2,1)}), (bf16[256,1024]{1,0:T(8,128)(2,1)}, bf16[1024,32]{0,1:T(8,128)(2,1)})) %all-reduce.12.cloned.1.call-update) | async-done | bytes 589840 | tf_op jit(solution)/shard_map/psum | solution.py:337
  609.6 1.8 copy.127
  611.4 1.4 fusion.88
  612.9 1.4 fusion.86
  614.4 1.9 fusion.90
  616.7 1.8 fusion.69
  618.6 18.2 fusion.113
  636.8 18.3 fusion.114
  655.5 18.0 fusion.115
  675.0 1.7 add_convert_fusion
  676.8 5.7 all-to-all-start
  683.8 8.6 all-to-all-done
  692.5 3.5 all-to-all-start.2
  696.6 9.4 all-to-all-done.2
  707.5 12.8 all_to_all.20
  720.3 3.5 all-to-all-start.3
  725.1 34.5 %all-reduce.2 = (f32[1024]{0:T(1024)S(1)}, f32[1024]{0:T(1024)S(1)}) all-reduce(f32[1024]{0:T(1024)S(1)} %get-tuple-element.15, f32[1024]{0:T(1024)S(1)} %get-tuple-element.13), channel_id=3, replica_groups=mesh['dp'=16,'tensor'=2] {'dp'}, use_global_device_ids=true, to_apply=%region_24.26.clone | all-reduce | flops 2048 | bytes 16384
  760.8 1.4 copy.128
  763.1 45.5 %reduce-scatter.18.cloned.1.call-done = f32[64,256]{1,0:T(8,128)} async-done(((f32[1024,256]{1,0:T(8,128)}), f32[64,256]{1,0:T(8,128)}) %reduce-scatter.18.cloned.1.call-update) | async-done | bytes 65552 | tf_op jit(solution)/shard_map/reduce_scatter | solution.py:361
  808.7 65.4 %reduce-scatter.14.cloned.1.call-done = f32[64,512]{1,0:T(8,128)} async-done(((f32[1024,512]{1,0:T(8,128)}), f32[64,512]{1,0:T(8,128)}) %reduce-scatter.14.cloned.1.call-update) | async-done | bytes 131088 | tf_op jit(solution)/shard_map/reduce_scatter | solution.py:359
  874.0 64.9 %reduce-scatter.20.cloned.1.call-done = f32[512,64]{0,1:T(8,128)} async-done(((f32[512,1024]{0,1:T(8,128)}), f32[512,64]{0,1:T(8,128)}) %reduce-scatter.20.cloned.1.call-update) | async-done | bytes 131088 | tf_op jit(solution)/shard_map/reduce_scatter | solution.py:362
  938.9 336.8 %reduce-scatter.22.cloned.1.call-done = f32[32,64,256]{2,1,0:T(8,128)} async-done(((f32[32,1024,256]{2,1,0:T(8,128)}), f32[32,64,256]{2,1,0:T(8,128)}) %reduce-scatter.22.cloned.1.call-update) | async-done | bytes 2097168 | tf_op jit(solution)/shard_map/reduce_scatter | solution.py:366
  1275.8 337.2 %reduce-scatter.24.cloned.1.call-done = f32[32,64,256]{2,1,0:T(8,128)} async-done(((f32[32,1024,256]{2,1,0:T(8,128)}), f32[32,64,256]{2,1,0:T(8,128)}) %reduce-scatter.24.cloned.1.call-update) | async-done | bytes 2097168 | tf_op jit(solution)/shard_map/reduce_scatter | solution.py:367
  1613.0 337.1 %reduce-scatter.26.cloned.1.call-done = f32[32,256,64]{1,2,0:T(8,128)} async-done(((f32[32,256,1024]{1,2,0:T(8,128)}), f32[32,256,64]{1,2,0:T(8,128)}) %reduce-scatter.26.cloned.1.call-update) | async-done | bytes 2097168 | tf_op jit(solution)/shard_map/reduce_scatter | solution.py:368
  (297 shorter events, 39.4 us)
Async XLA Ops:
  8.0 23.1 %copy-start = (bf16[512,1024]{1,0:T(8,128)(2,1)S(1)}, bf16[512,1024]{1,0:T(8,128)(2,1)}, u32[]{:S(2)}) copy-start(bf16[512,1024]{1,0:T(8,128)(2,1)} %param.24) | copy-start | bytes 3145732
  8.0 18.3 copy-start.36
  8.0 18.3 copy-start.13
  8.1 54.6 %all-reduce.8.cloned.1.call-start = ((), (), s32[]{:S(2)}) async-start(), calls=%async_computation.13 | async-start | bytes 1048576 | tf_op jit(solution)/shard_map/psum | solution.py:175
  13.8 20.9 %copy-start.46 = (pred[256]{0:T(512)(128)(4,1)}, pred[256]{0:T(512)(128)(4,1)S(1)}, u32[]{:S(2)}) copy-start(pred[256]{0:T(512)(128)(4,1)S(1)} %get-tuple-element.36) | copy-start | bytes 772
  24.0 3.7 copy-start.27
  32.4 131.0 %all-gather.4.cloned.1.call-start = ((), (), s32[]{:S(2)}) async-start(), calls=%async_computation.14 | async-start | bytes 17825792 | tf_op jit(solution)/shard_map/all_gather | solution.py:208
  32.9 257.4 %all-gather.6.cloned.1.call-start = ((), (), s32[]{:S(2)}) async-start(), calls=%async_computation.15 | async-start | bytes 17825792 | tf_op jit(solution)/shard_map/all_gather | solution.py:209
  33.5 383.8 %all-gather.8.cloned.1.call-start = ((), (), s32[]{:S(2)}) async-start(), calls=%async_computation.16 | async-start | bytes 17825792 | tf_op jit(solution)/shard_map/all_gather | solution.py:210
  34.1 531.5 %all-reduce.10.cloned.1.call-start = ((), (), s32[]{:S(2)}) async-start(), calls=%async_computation.18 | async-start | bytes 1048576 | tf_op jit(solution)/shard_map/psum | solution.py:268
  35.1 11.6 copy-start.29
  44.9 19.7 %copy-start.40 = (f32[1024]{0:T(1024)S(1)}, f32[1024]{0:T(1024)}, u32[]{:S(2)}) copy-start(f32[1024]{0:T(1024)} %param.20) | copy-start | bytes 12292
  46.0 19.8 %copy-start.19 = (bf16[1024,32]{0,1:T(8,128)(2,1)S(1)}, bf16[1024,32]{0,1:T(8,128)(2,1)}, u32[]{:S(2)}) copy-start(bf16[1024,32]{0,1:T(8,128)(2,1)} %param.25) | copy-start | bytes 196612
  46.7 25.1 %copy-start.50 = (s32[256]{0:T(256)}, s32[256]{0:T(256)S(1)}, u32[]{:S(2)}) copy-start(s32[256]{0:T(256)S(1)} %get-tuple-element.19) | copy-start | bytes 3076
  46.7 25.1 %copy-start.54 = (s32[256]{0:T(256)}, s32[256]{0:T(256)S(1)}, u32[]{:S(2)}) copy-start(s32[256]{0:T(256)S(1)} %get-tuple-element.20) | copy-start | bytes 3076
  46.7 25.1 %copy-start.59 = (s32[256]{0:T(256)}, s32[256]{0:T(256)S(1)}, u32[]{:S(2)}) copy-start(s32[256]{0:T(256)S(1)} %get-tuple-element.21) | copy-start | bytes 3076
  46.7 25.1 %copy-start.63 = (s32[256]{0:T(256)}, s32[256]{0:T(256)S(1)}, u32[]{:S(2)}) copy-start(s32[256]{0:T(256)S(1)} %get-tuple-element.22) | copy-start | bytes 3076
  46.7 25.1 %copy-start.67 = (s32[256]{0:T(256)}, s32[256]{0:T(256)S(1)}, u32[]{:S(2)}) copy-start(s32[256]{0:T(256)S(1)} %get-tuple-element.23) | copy-start | bytes 3076
  46.7 25.1 %copy-start.71 = (s32[256]{0:T(256)}, s32[256]{0:T(256)S(1)}, u32[]{:S(2)}) copy-start(s32[256]{0:T(256)S(1)} %get-tuple-element.24) | copy-start | bytes 3076
  46.7 25.1 %copy-start.75 = (s32[256]{0:T(256)}, s32[256]{0:T(256)S(1)}, u32[]{:S(2)}) copy-start(s32[256]{0:T(256)S(1)} %get-tuple-element.25) | copy-start | bytes 3076
  46.8 25.1 %copy-start.79 = (s32[256]{0:T(256)}, s32[256]{0:T(256)S(1)}, u32[]{:S(2)}) copy-start(s32[256]{0:T(256)S(1)} %get-tuple-element.26) | copy-start | bytes 3076
  64.6 7.2 copy-start.44
  457.2 5.7 copy-start.51
  457.2 5.7 copy-start.55
  467.4 10.2 copy-start.4
  467.4 10.2 copy-start.9
  477.7 11.8 copy-start.5
  517.3 7.3 copy-start.52
  517.3 7.3 copy-start.56
  517.3 7.3 copy-start.60
  517.3 7.3 copy-start.64
  517.3 7.3 copy-start.68
  517.3 7.3 copy-start.72
  517.3 7.3 copy-start.76
  517.4 7.3 copy-start.80
  524.7 4.1 copy-start.43
  531.7 5.8 copy-start.12
  532.1 5.2 copy-start.20
  538.7 70.9 %all-reduce.12.cloned.1.call-start = ((), (), s32[]{:S(2)}) async-start(), calls=%async_computation.27 | async-start | bytes 1179648 | tf_op jit(solution)/shard_map/psum | solution.py:337
  540.8 24.8 %copy-start.8 = (bf16[256,1024]{1,0:T(8,128)(2,1)S(1)}, bf16[256,1024]{1,0:T(8,128)(2,1)}, u32[]{:S(2)}) copy-start(bf16[256,1024]{1,0:T(8,128)(2,1)} %all-reduce.8.cloned.1.call-done) | copy-start | bytes 1572868
  540.8 24.8 %copy-start.41 = (f32[1024]{0:T(1024)S(1)}, f32[1024]{0:T(1024)}, u32[]{:S(2)}) copy-start(f32[1024]{0:T(1024)} %param.20) | copy-start | bytes 12292
  540.8 24.8 %copy-start.45 = (f32[256]{0:T(256)S(1)}, f32[256]{0:T(256)}, u32[]{:S(2)}) copy-start(f32[256]{0:T(256)} %copy-done.44) | copy-start | bytes 3076
  540.8 26.3 %copy-start.49 = (f32[256]{0:T(256)S(1)}, f32[256]{0:T(256)}, u32[]{:S(2)}) copy-start(f32[256]{0:T(256)} %get-tuple-element.59) | copy-start | bytes 3076
  579.2 95.4 %reduce-scatter.12.cloned.1.call-start = ((), (), s32[]{:S(2)}) async-start(), calls=%async_computation.17 | async-start | bytes 786432 | tf_op jit(solution)/shard_map/reduce_scatter | solution.py:220
  579.3 32.1 %copy-start.37 = (f32[1024]{0:T(1024)S(1)}, f32[1024]{0:T(1024)}, u32[]{:S(2)}) copy-start(f32[1024]{0:T(1024)} %param.19) | copy-start | bytes 12292
  579.4 32.1 %copy-start.39 = (f32[256]{0:T(256)S(1)}, f32[256]{0:T(256)}, u32[]{:S(2)}) copy-start(f32[256]{0:T(256)} %copy-done.38) | copy-start | bytes 3076
  585.4 175.4 %reduce-scatter.28.cloned.1.call-start = ((), (), s32[]{:S(2)}) async-start(), calls=%async_computation.26 | async-start | bytes 557056
  611.4 151.8 %reduce-scatter.16.cloned.1.call-start = ((), (), s32[]{:S(2)}) async-start(), calls=%async_computation.20 | async-start | bytes 1114112 | tf_op jit(solution)/shard_map/reduce_scatter | solution.py:360
  612.9 195.8 %reduce-scatter.18.cloned.1.call-start = ((), (), s32[]{:S(2)}) async-start(), calls=%async_computation.21 | async-start | bytes 1114112 | tf_op jit(solution)/shard_map/reduce_scatter | solution.py:361
  614.4 259.6 %reduce-scatter.14.cloned.1.call-start = ((), (), s32[]{:S(2)}) async-start(), calls=%async_computation.19 | async-start | bytes 2228224 | tf_op jit(solution)/shard_map/reduce_scatter | solution.py:359
  616.3 322.6 %reduce-scatter.20.cloned.1.call-start = ((), (), s32[]{:S(2)}) async-start(), calls=%async_computation.22 | async-start | bytes 2228224 | tf_op jit(solution)/shard_map/reduce_scatter | solution.py:362
  618.5 657.2 %reduce-scatter.22.cloned.1.call-start = ((), (), s32[]{:S(2)}) async-start(), calls=%async_computation.23 | async-start | bytes 35651584 | tf_op jit(solution)/shard_map/reduce_scatter | solution.py:366
  636.8 976.2 %reduce-scatter.24.cloned.1.call-start = ((), (), s32[]{:S(2)}) async-start(), calls=%async_computation.24 | async-start | bytes 35651584 | tf_op jit(solution)/shard_map/reduce_scatter | solution.py:367
  655.1 1295.0 %reduce-scatter.26.cloned.1.call-start = ((), (), s32[]{:S(2)}) async-start(), calls=%async_computation.25 | async-start | bytes 35651584 | tf_op jit(solution)/shard_map/reduce_scatter | solution.py:368
  673.5 9.0 copy-start.22
  674.6 8.4 copy-start.48
  676.8 6.2 copy-start.11
  676.8 15.7 all-to-all-start
  682.4 13.6 copy-start.83
  682.4 13.6 copy-start.84
  683.8 40.0 %copy-start.85 = (u32[32]{0:T(128)S(1)}, u32[32]{0:T(128)}, u32[]{:S(2)}) copy-start(u32[32]{0:T(128)} %constant.87) | copy-start | bytes 388
  692.5 13.5 all-to-all-start.2
  696.1 1254.7 %copy-start.1 = (bf16[512,1024]{1,0:T(8,128)(2,1)S(1)}, bf16[512,1024]{1,0:T(8,128)(2,1)}, u32[]{:S(2)}) copy-start(bf16[512,1024]{1,0:T(8,128)(2,1)} %param.24) | copy-start | bytes 3145732
  720.3 42.0 %all-to-all-start.3 = ((bf16[16,16,512]{2,1,0:T(8,128)(2,1)}), bf16[16,16,512]{2,1,0:T(8,128)(2,1)S(1)}, u32[]{:S(2)}, u32[]{:S(2)}) async-start(bf16[16,16,512]{2,1,0:T(8,128)(2,1)} %get-tuple-element.61), calls=%async_computation.4 | async-start | bytes 524288 | tf_op jit(solution)/shard_map/all_to_all | solution.py:60
  (42 other events, 73.6 us)
Sparse Core Ops, SparseCore 0:
  32.5 30.1 all-reduce.7
  538.8 26.7 all-reduce.9
  579.3 30.1 all-reduce.11
  611.8 14.5 reduce-scatter.11
  630.3 55.7 reduce-scatter.27
  690.6 57.3 reduce-scatter.15
  752.2 56.3 reduce-scatter.17
  813.4 60.5 reduce-scatter.13
  878.3 60.5 reduce-scatter.19
  944.2 331.5 reduce-scatter.21
  1281.2 331.7 reduce-scatter.23
  1618.2 331.7 reduce-scatter.25
Sparse Core Ops, SparseCore 1:
  35.3 128.0 all-gather.3
  165.6 124.6 all-gather.5
  292.6 124.6 all-gather.7
where the time goes:
time: 1970 us; the launch traced here: 1960 us
  waiting for transfers between devices  1580 us (80%)
  matrix products  201 us (10%)
  blocking collectives  66 us (3%)
  other arithmetic  53.2 us (3%)
  local copies, waits for them, and re-layouts  24.3 us (1%)
  between operations  20.3 us (1%)
    reduce_scatter x1, waiting for transfers between devices, local(): lax.psum_scatter(up_w_grad, 'dp', scatter_dimension=1, tiled=True)  337 us
    reduce_scatter x1, waiting for transfers between devices, local(): lax.psum_scatter(down_w_grad, 'dp', scatter_dimension=2, tiled=True)  337 us
    reduce_scatter x1, waiting for transfers between devices, local(): lax.psum_scatter(gate_w_grad, 'dp', scatter_dimension=1, tiled=True)  337 us
    all_gather x1, waiting for transfers between devices, local(): lax.all_gather(up_weight, 'dp', axis=1, tiled=True)  116 us
    all_gather x1, waiting for transfers between devices, local(): lax.all_gather(down_weight, 'dp', axis=2, tiled=True)  115 us
    all_gather x1, waiting for transfers between devices, local(): lax.all_gather(gate_weight, 'dp', axis=1, tiled=True)  91.5 us
    reduce_scatter x1, waiting for transfers between devices, local(): lax.psum_scatter(query_w_grad, 'dp', scatter_dimension=0, tiled=True)  65.4 us
    reduce_scatter x1, waiting for transfers between devices, local(): lax.psum_scatter(output_w_grad, 'dp', scatter_dimension=1, tiled=True)  64.9 us
  transfers between devices with their start and end apart: 18, of which 14 were waited for; matrix products, arithmetic and copies ran while one was open for 7% of the time, Pallas kernels for 0%

commit v1 on v0

v1 whole, which is shorter than its diff:
```python
import jax
import jax.numpy as jnp
from jax import lax
from jax.sharding import PartitionSpec as P

HEAD_DIM = 64


EPSILON = 1e-06
ROPE_BASE = 10000.0
PRECISE = lax.Precision.HIGHEST
NEGATIVE = -1e30


def rope_tables(positions, half_dim):
    freq_index = jnp.arange(half_dim, dtype=jnp.int32).astype(jnp.float32)
    frequency = jnp.exp(-(2.0 * freq_index / (2.0 * half_dim)) * jnp.log(ROPE_BASE))
    angles = positions.astype(jnp.float32)[:, None] * frequency[None, :]
    return (jnp.cos(angles)[:, None, :], jnp.sin(angles)[:, None, :])


def rotate(values, cos_table, sin_table):
    half_dim = values.shape[-1] // 2
    first_half = values[..., :half_dim]
    second = values[..., half_dim:]
    return jnp.concatenate(
        [first_half * cos_table - second * sin_table, second * cos_table + first_half * sin_table],
        axis=-1,
    )


def rotate_back(values, cos_table, sin_table):
    half_dim = values.shape[-1] // 2
    first_half = values[..., :half_dim]
    second = values[..., half_dim:]
    return jnp.concatenate(
        [first_half * cos_table + second * sin_table, second * cos_table - first_half * sin_table],
        axis=-1,
    )


def split_parts(values):
    upper = values.astype(jnp.bfloat16)
    lower = (values - upper.astype(jnp.float32)).astype(jnp.bfloat16)
    return (upper, lower)


def swap_tensor(values):
    return lax.ppermute(values, "tensor", [(0, 1), (1, 0)])


def mm(left, right, contract):
    return lax.dot_general(
        left, right, ((contract[:1], contract[1:]), ((), ())), preferred_element_type=jnp.float32
    )


def local(
    inputs,
    cotangent,
    attn_gain,
    expert_gain,
    query_weight,
    key_weight,
    value_weight,
    output_weight,
    router_weight,
    gate_weight,
    up_weight,
    down_weight,
    routes,
    lengths,
    placement,
):
    row_count, top_count = routes.shape
    expert_count = router_weight.shape[1]
    capacity = row_count * top_count // expert_count
    kv_local = key_weight.shape[1] // HEAD_DIM
    heads_local = query_weight.shape[1] // HEAD_DIM
    group = heads_local // kv_local
    scale = 1.0 / HEAD_DIM
    width_half = inputs.shape[1]
    width = 2 * width_half
    plane = lax.axis_index("tensor")
    devices = lax.axis_size("dp")
    dp_index = lax.axis_index("dp")
    plane_experts = expert_count // 2
    members = plane_experts
    clusters = devices // members
    member = dp_index % members
    if clusters == 1:
        inside = across = None
    else:
        inside = [[c * members + m for m in range(members)] for c in range(clusters)]
        across = [[c * members + m for c in range(clusters)] for m in range(members)]

    def exchange(values):
        return lax.all_to_all(
            values, "dp", split_axis=0, concat_axis=0, tiled=True, axis_index_groups=inside
        )

    def gather_small(values):
        return lax.all_gather(values, "dp", axis=0, tiled=False, axis_index_groups=inside)

    def halves(values, axis):
        size = values.shape[axis] // 2
        return (
            lax.dynamic_slice_in_dim(values, plane * size, size, axis),
            lax.dynamic_slice_in_dim(values, (1 - plane) * size, size, axis),
        )

    def join(own, other, axis):
        first = jnp.where(plane == 0, own, other)
        second = jnp.where(plane == 0, other, own)
        return jnp.concatenate([first, second], axis=axis)

    def add_planes(part):
        low = part.astype(jnp.bfloat16)
        return low.astype(jnp.float32) + swap_tensor(low).astype(jnp.float32)

    down_t = jnp.swapaxes(down_weight, 1, 2)
    stacked = jnp.stack([gate_weight, up_weight, down_t], axis=1)
    own_w, other_w = halves(stacked, 0)
    other_w = swap_tensor(other_w)

    def place_weights(values):
        values = exchange(values)
        if clusters > 1:
            values = lax.all_gather(values, "dp", axis=0, tiled=True, axis_index_groups=across)
        return [values[:, i].reshape(width, -1) for i in range(3)]

    own_w = place_weights(own_w)
    other_w = place_weights(other_w)
    gate_full, up_full, down_full = [
        jnp.concatenate([a, b], axis=1) for a, b in zip(own_w, other_w)
    ]

    rank_list = jnp.arange(devices, dtype=jnp.int32)
    holder = jnp.sum(jnp.where(placement == dp_index, rank_list, 0))
    slot_lengths = lax.dynamic_index_in_dim(lengths, holder, 0, keepdims=False)
    seq_count = slot_lengths.shape[0]
    seq_ids = jnp.arange(seq_count, dtype=jnp.int32)
    seg_ends = jnp.sum(
        jnp.where(seq_ids[None, :] <= seq_ids[:, None], slot_lengths[None, :], 0), axis=1
    )
    row_index = jnp.arange(row_count, dtype=jnp.int32)
    past = row_index[:, None] >= seg_ends[None, :]
    segment = jnp.sum(past.astype(jnp.int32), axis=1)
    positions = row_index - jnp.max(jnp.where(past, seg_ends[None, :], 0), axis=1)
    token_live = segment < seq_count
    allowed = (segment[:, None] == segment[None, :]) & (row_index[None, :] <= row_index[:, None])
    cos_table, sin_table = rope_tables(positions, HEAD_DIM // 2)
    live_column = token_live.astype(jnp.float32)[:, None]
    experts = jnp.arange(expert_count, dtype=jnp.int32)
    picked = jnp.any(routes.T[:, None, :] == experts[None, :, None], axis=0)
    counted = picked & token_live[None, :]
    before = (row_index[:, None] < row_index[None, :]).astype(jnp.bfloat16)
    place = mm(counted.astype(jnp.bfloat16), before, (1, 0)).astype(jnp.int32)
    slot_of = jnp.where(counted & (place < capacity), place, -1)
    slot_own = lax.dynamic_slice_in_dim(slot_of, plane * plane_experts, plane_experts, 0)
    hot = slot_own[:, None, :] == jnp.arange(capacity, dtype=jnp.int32)[None, :, None]
    dispatch_t = hot.astype(jnp.bfloat16).reshape(plane_experts * capacity, row_count)

    full_cot = join(cotangent, swap_tensor(cotangent), 1)
    slot_cot = mm(dispatch_t, full_cot, (1, 0)).astype(jnp.bfloat16)
    slot_cot = exchange(slot_cot)

    full_inputs = join(inputs, swap_tensor(inputs), 1)
    wide_inputs = full_inputs.astype(jnp.float32)
    attn_scale = lax.rsqrt(jnp.mean(wide_inputs * wide_inputs, axis=-1, keepdims=True) + EPSILON)
    normed = (wide_inputs * attn_scale * attn_gain).astype(jnp.bfloat16)
    query_pre = jnp.dot(normed, query_weight, preferred_element_type=jnp.float32)
    key_pre = jnp.dot(normed, key_weight, preferred_element_type=jnp.float32)
    value_pre = jnp.dot(normed, value_weight, preferred_element_type=jnp.float32)
    query_rot = (
        rotate(query_pre.reshape(row_count, heads_local, HEAD_DIM), cos_table, sin_table)
        .astype(jnp.bfloat16)
        .reshape(row_count, kv_local, group, HEAD_DIM)
    )
    key_rot = rotate(key_pre.reshape(row_count, kv_local, HEAD_DIM), cos_table, sin_table).astype(
        jnp.bfloat16
    )
    value_rows = value_pre.astype(jnp.bfloat16).reshape(row_count, kv_local, HEAD_DIM)

    def masked_scores():
        raw_scores = (
            jnp.einsum("qhgd,khd->hgqk", query_rot, key_rot, preferred_element_type=jnp.float32)
            * scale
        )
        return jnp.where(allowed, raw_scores, NEGATIVE)

    masked = masked_scores()
    row_max = jnp.max(masked, axis=-1, keepdims=True)
    exp_terms = jnp.exp(masked - row_max)
    row_total = jnp.sum(exp_terms, axis=-1, keepdims=True)
    attn_probs = exp_terms / row_total
    log_total = row_max + jnp.log(row_total)
    context = jnp.einsum(
        "hgqk,khd->qhgd",
        attn_probs.astype(jnp.bfloat16),
        value_rows,
        preferred_element_type=jnp.float32,
    ).reshape(row_count, heads_local * HEAD_DIM)
    context = (context * live_column).astype(jnp.bfloat16)
    attn_part = jnp.dot(context, output_weight, preferred_element_type=jnp.float32)
    residual = wide_inputs + add_planes(attn_part)
    expert_scale = lax.rsqrt(jnp.mean(residual * residual, axis=-1, keepdims=True) + EPSILON)
    mixed_rows = (residual * expert_scale * expert_gain).astype(jnp.bfloat16)

    slot_in = exchange(mm(dispatch_t, mixed_rows, (1, 0)).astype(jnp.bfloat16))

    logits = mm(router_weight, mixed_rows, (0, 1))
    logits = jnp.where(picked, logits, NEGATIVE)
    weights = jnp.exp(logits - jnp.max(logits, axis=0, keepdims=True))
    gates = weights / jnp.sum(weights, axis=0, keepdims=True)
    gates_own = lax.dynamic_slice_in_dim(gates, plane * plane_experts, plane_experts, 0)
    weighted = jnp.where(hot, gates_own[:, None, :], 0.0)
    gate_slot = jnp.sum(weighted, axis=2)
    weighted = weighted.astype(jnp.bfloat16).reshape(plane_experts * capacity, row_count)
    gate_rows = lax.dynamic_index_in_dim(gather_small(gate_slot), member, 1, keepdims=False)
    gate_rows = gate_rows.reshape(members * capacity, 1)

    gate_pre = mm(slot_in, gate_full, (1, 0))
    up_pre = mm(slot_in, up_full, (1, 0))
    sigma = jax.nn.sigmoid(gate_pre)
    hidden = (gate_pre * sigma * up_pre).astype(jnp.bfloat16)
    expert_out = mm(hidden, down_full, (1, 1))
    slot_gate_grad = jnp.sum(expert_out * slot_cot.astype(jnp.float32), axis=1)
    slot_gate_grad = slot_gate_grad.reshape(members, capacity)
    slot_gate_grad = lax.dynamic_index_in_dim(
        gather_small(slot_gate_grad), member, 1, keepdims=False
    )
    hidden_grad = mm(slot_cot, down_full, (1, 0))
    gate_pre_grad = hidden_grad * up_pre * sigma * (1.0 + gate_pre * (1.0 - sigma))
    up_pre_grad = hidden_grad * gate_pre * sigma
    slot_in_grad = mm(gate_pre_grad.astype(jnp.bfloat16), gate_full, (1, 1)) + mm(
        up_pre_grad.astype(jnp.bfloat16), up_full, (1, 1)
    )
    slot_in_grad = exchange(slot_in_grad.astype(jnp.bfloat16))
    expert_out = exchange(expert_out.astype(jnp.bfloat16))
    scaled_cot = (gate_rows * slot_cot.astype(jnp.float32)).astype(jnp.bfloat16)
    w_grads = [
        mm(slot_in, (gate_rows * gate_pre_grad).astype(jnp.bfloat16), (0, 0)),
        mm(slot_in, (gate_rows * up_pre_grad).astype(jnp.bfloat16), (0, 0)),
        mm(scaled_cot, hidden, (0, 0)),
    ]
    w_grads = jnp.stack([w.reshape(devices, width // devices, -1) for w in w_grads], axis=1)
    w_grads = w_grads.astype(jnp.bfloat16)

    moe_part = mm(weighted, expert_out, (0, 0)).astype(jnp.bfloat16)
    moe_own, moe_other = halves(moe_part, 1)
    moe_half = moe_own.astype(jnp.float32) + swap_tensor(moe_other).astype(jnp.float32)
    residual_half, _ = halves(residual, 1)
    outputs_half = (residual_half + moe_half).astype(jnp.bfloat16)

    token_gate_grad = jnp.sum(
        jnp.where(hot, slot_gate_grad[:, :, None], 0.0), axis=1
    )
    mean_grad = jnp.sum(gates_own * token_gate_grad, axis=0, keepdims=True)
    spread = jnp.zeros_like(gates)
    spread = lax.dynamic_update_slice_in_dim(spread, token_gate_grad, plane * plane_experts, 0)
    logits_grad = gates * (spread - mean_grad)
    logits_upper, logits_lower = split_parts(logits_grad)
    router_part = mm(logits_upper, mixed_rows, (1, 0)) + mm(logits_lower, mixed_rows, (1, 0))
    router_grad = add_planes(router_part)
    mixed_part = (
        mm(weighted, slot_in_grad, (0, 0))
        + mm(logits_upper, router_weight, (0, 1))
        + mm(logits_lower, router_weight, (0, 1))
    )
    mixed_grad = add_planes(mixed_part)
    scaled_two = mixed_grad * expert_gain
    expert_gain_grad = jnp.sum(mixed_grad * residual * expert_scale, axis=0)
    cube_two = expert_scale * expert_scale * expert_scale
    residual_grad = (
        full_cot.astype(jnp.float32)
        + expert_scale * scaled_two
        - residual * cube_two * jnp.mean(scaled_two * residual, axis=-1, keepdims=True)
    )
    residual_low = residual_grad.astype(jnp.bfloat16)
    output_w_grad = mm(residual_low, context, (0, 0))
    context_grad = jnp.einsum(
        "td,hd->th", residual_low, output_weight, preferred_element_type=jnp.float32
    ).astype(jnp.bfloat16)
    context_grad = jnp.where(
        token_live[:, None], context_grad, jnp.zeros_like(context_grad)
    ).reshape(row_count, kv_local, group, HEAD_DIM)
    again = masked_scores()
    probs_again = jnp.exp(again - log_total)
    prob_grad = jnp.einsum(
        "qhgd,khd->hgqk", context_grad, value_rows, preferred_element_type=jnp.float32
    )
    row_inner = jnp.sum(probs_again * prob_grad, axis=-1, keepdims=True)
    score_grad = (probs_again * (prob_grad - row_inner)).astype(jnp.bfloat16)
    query_grad = (
        jnp.einsum("hgqk,khd->qhgd", score_grad, key_rot, preferred_element_type=jnp.float32)
        * scale
    )
    key_grad = (
        jnp.einsum("hgqk,qhgd->khd", score_grad, query_rot, preferred_element_type=jnp.float32)
        * scale
    )
    value_grad = jnp.einsum(
        "hgqk,qhgd->khd",
        probs_again.astype(jnp.bfloat16),
        context_grad,
        preferred_element_type=jnp.float32,
    )
    query_pre_grad = (
        rotate_back(query_grad.reshape(row_count, heads_local, HEAD_DIM), cos_table, sin_table)
        .astype(jnp.bfloat16)
        .reshape(row_count, -1)
    )
    key_pre_grad = (
        rotate_back(key_grad, cos_table, sin_table).astype(jnp.bfloat16).reshape(row_count, -1)
    )
    value_pre_grad = value_grad.astype(jnp.bfloat16).reshape(row_count, -1)
    query_w_grad = mm(normed, query_pre_grad, (0, 0))
    key_w_grad = mm(normed, key_pre_grad, (0, 0))
    value_w_grad = mm(normed, value_pre_grad, (0, 0))
    normed_part = (
        mm(query_pre_grad, query_weight, (1, 1))
        + mm(key_pre_grad, key_weight, (1, 1))
        + mm(value_pre_grad, value_weight, (1, 1))
    )
    normed_grad = add_planes(normed_part)
    scaled_one = normed_grad * attn_gain
    attn_gain_grad = jnp.sum(normed_grad * wide_inputs * attn_scale, axis=0)
    cube_one = attn_scale * attn_scale * attn_scale
    input_grad = (
        residual_grad
        + attn_scale * scaled_one
        - wide_inputs * cube_one * jnp.mean(scaled_one * wide_inputs, axis=-1, keepdims=True)
    )
    input_half, _ = halves(input_grad, 1)

    vectors = jnp.concatenate(
        [router_grad, attn_gain_grad[None], expert_gain_grad[None]], axis=0
    ).T
    vectors = jnp.pad(vectors, ((0, 0), (0, 128 - vectors.shape[1])))
    parts = jnp.concatenate(
        [output_w_grad, query_w_grad, key_w_grad, value_w_grad, vectors], axis=1
    ).astype(jnp.bfloat16)
    share = lax.psum_scatter(parts, "dp", scatter_dimension=0, tiled=True).astype(jnp.float32)
    cuts = [output_w_grad.shape[1]]
    for w in (query_w_grad, key_w_grad, value_w_grad):
        cuts.append(cuts[-1] + w.shape[1])
    output_part = share[:, : cuts[0]].T
    query_part = share[:, cuts[0] : cuts[1]]
    key_part = share[:, cuts[1] : cuts[2]]
    value_part = share[:, cuts[2] : cuts[3]]
    router_share = share[:, cuts[3] : cuts[3] + expert_count]
    attn_gain_part = share[:, cuts[3] + expert_count]
    expert_gain_part = share[:, cuts[3] + expert_count + 1]

    own_g, other_g = jnp.split(w_grads, 2, axis=3)

    def return_grads(values):
        if clusters > 1:
            values = lax.psum_scatter(
                values, "dp", scatter_dimension=0, tiled=True, axis_index_groups=across
            )
        return exchange(values)

    other_g = swap_tensor(return_grads(other_g))
    own_g = return_grads(own_g)
    both = join(own_g, other_g, 0).astype(jnp.float32)
    gate_w_part = both[:, 0]
    up_w_part = both[:, 1]
    down_w_part = jnp.swapaxes(both[:, 2], 1, 2)

    piece_rows = row_count // devices

    def reroute(values):
        spread = lax.all_to_all(
            values.reshape(devices, piece_rows, -1), "dp", split_axis=0, concat_axis=0, tiled=True
        )
        moved = jnp.take(spread, placement, axis=0)
        return lax.all_to_all(moved, "dp", split_axis=0, concat_axis=0, tiled=True).reshape(
            row_count, -1
        )

    outputs = reroute(outputs_half)
    input_result = reroute(input_half.astype(jnp.bfloat16)).astype(jnp.float32)
    return (
        outputs,
        input_result,
        attn_gain_part,
        expert_gain_part,
        query_part,
        key_part,
        value_part,
        output_part,
        router_share,
        gate_w_part,
        up_w_part,
        down_w_part,
    )


def solution(mesh):
    in_specs = (
        P("dp", "tensor"),
        P("dp", "tensor"),
        P(),
        P(),
        P(None, "tensor"),
        P(None, "tensor"),
        P(None, "tensor"),
        P("tensor", None),
        P(),
        P(None, "dp", "tensor"),
        P(None, "dp", "tensor"),
        P(None, "tensor", "dp"),
        P("dp", None),
        P(),
        P(),
    )
    out_specs = (
        P("dp", "tensor"),
        P("dp", "tensor"),
        P("dp"),
        P("dp"),
        P("dp", "tensor"),
        P("dp", "tensor"),
        P("dp", "tensor"),
        P("tensor", "dp"),
        P("dp", None),
        P(None, "dp", "tensor"),
        P(None, "dp", "tensor"),
        P(None, "tensor", "dp"),
    )
    return jax.shard_map(local, mesh=mesh, in_specs=in_specs, out_specs=out_specs, check_vma=False)
```

time: 1970 us -> 553 us (0.28)
  waiting for transfers between devices: 1580 us -> 189 us
  matrix products: 201 us -> 57.1 us
  starting transfers between devices: 14.1 us -> 108 us
  local copies, waits for them, and re-layouts: 24.3 us -> 56.5 us
    reduce_scatter x8 -> x0, waiting for transfers between devices: 1190 us -> none  [the longest x1 337 us: local(): lax.psum_scatter(up_w_grad, 'dp', scatter_dimension=1, tiled=True)]
    all_gather x3 -> x0, waiting for transfers between devices: 323 us -> none  [the longest x1 116 us: local(): lax.all_gather(up_weight, 'dp', axis=1, tiled=True)]
    dot_general x30 -> x26, matrix products: 192 us -> 50.2 us  [mm(): lax.dot_general(left, right, ((contract[:1], contract[1:]), ((), ())), pr...]
    all_to_all x3 -> x12, waiting for transfers between devices: 18 us -> 129 us  [the longest x8 107 us: exchange(): lax.all_to_all(values, 'dp', split_axis=0, concat_axis=0, tiled=True, axi...]
    all_to_all x3 -> x12, starting transfers between devices: 12.7 us -> 98 us  [the longest x8 70.4 us: exchange(): lax.all_to_all(values, 'dp', split_axis=0, concat_axis=0, tiled=True, axi...]
    all_gather x2, blocking collectives: 18.7 us -> 84 us  [gather_small(): lax.all_gather(values, 'dp', axis=0, tiled=False, axis_index_groups=inside)]
    ppermute x0 -> x9, waiting for transfers between devices: none -> 60.4 us  [swap_tensor(): return lax.ppermute(values, 'tensor', [(0, 1), (1, 0)])]
    psum x3 -> x0, waiting for transfers between devices: 50 us -> none  [the longest x1 24.2 us: local(): lax.psum(normed_part.astype(jnp.bfloat16), 'tensor').astype(jnp.float32)]
  transfers between devices with their start and end apart: 18 -> 22, of which waited for: 14 -> 12; matrix products, arithmetic and copies ran while one was open for 7% -> 23% of each run, Pallas kernels for 0% -> 0%
where the time goes in v1:
time: 553 us; the launch traced here: 550 us
  waiting for transfers between devices  189 us (34%)
  starting transfers between devices  108 us (20%)
  blocking collectives  84 us (15%)
  matrix products  57.1 us (10%)
  local copies, waits for them, and re-layouts  56.5 us (10%)
  other arithmetic  37.6 us (7%)
  between operations  17.3 us (3%)
    all_to_all x8, waiting for transfers between devices, exchange(): lax.all_to_all(values, 'dp', split_axis=0, concat_axis=0, tiled=True, axi...  107 us
    all_gather x2, blocking collectives, gather_small(): lax.all_gather(values, 'dp', axis=0, tiled=False, axis_index_groups=inside)  84 us
    all_to_all x8, starting transfers between devices, exchange(): lax.all_to_all(values, 'dp', split_axis=0, concat_axis=0, tiled=True, axi...  70.4 us
    ppermute x9, waiting for transfers between devices, swap_tensor(): return lax.ppermute(values, 'tensor', [(0, 1), (1, 0)])  60.4 us
    dot_general x26, matrix products, mm(): lax.dot_general(left, right, ((contract[:1], contract[1:]), ((), ())), pr...  50.2 us
    unnamed x177, local copies, waits for them, and re-layouts  21.9 us
    all_to_all x2, starting transfers between devices, reroute(): lax.all_to_all(values.reshape(devices, piece_rows, -1), 'dp', split_axis=...  14.4 us
    all_to_all x2, waiting for transfers between devices, reroute(): lax.all_to_all(moved, 'dp', split_axis=0, concat_axis=0, tiled=True)  13.9 us
  transfers between devices with their start and end apart: 22, of which 12 were waited for; matrix products, arithmetic and copies ran while one was open for 23% of the time, Pallas kernels for 0%

profile of v1, /device:TPU:0, one launch (start us, length us, event | category | flops | bytes accessed | tf_op | source)
XLA Modules:
  0.0 550.1 jit_solution(17113575687312573210)
XLA Ops:
  7.2 3.0 collective-permute-start
  10.2 2.2 pad_maximum_fusion
  12.4 2.1 constant_dynamic-slice_fusion.3
  14.5 6.1 %all-to-all-start.1 = ((bf16[16,3,64,256]{3,2,1,0:T(8,128)(2,1)}), bf16[16,3,64,256]{3,2,1,0:T(8,128)(2,1)}, u32[]{:S(2)}, u32[]{:S(2)}) async-start(bf16[16,3,64,256]{3,2,1,0:T(8,128)(2,1)} %get-tuple-element.85), calls=%async_computation.1 | async-start | bytes 3145728 | tf_op jit(solution)/shard_map/all_to_all | solution.py:98
  29.5 28.1 %collective-permute-done.2 = bf16[16,3,64,256]{3,2,1,0:T(8,128)(2,1)} collective-permute-done((bf16[16,3,64,256]{3,2,1,0:T(8,128)(2,1)}, bf16[16,3,64,256]{3,2,1,0:T(8,128)(2,1)}, u32[]{:S(2)}, u32[]{:S(2)}) %collective-permute-start.2) | collective-permute-done | bytes 1572896 | tf_op jit(solution)/shard_map/ppermute | solution.py:49
  57.6 5.8 %all-to-all-start.2 = ((bf16[16,3,64,256]{3,2,1,0:T(8,128)(2,1)}), bf16[16,3,64,256]{3,2,1,0:T(8,128)(2,1)}, u32[]{:S(2)}, u32[]{:S(2)}) async-start(bf16[16,3,64,256]{3,2,1,0:T(8,128)(2,1)} %collective-permute-done.2), calls=%async_computation.2 | async-start | bytes 3145728 | tf_op jit(solution)/shard_map/all_to_all | solution.py:98
  67.3 13.2 %collective-permute-done.1 = bf16[256,1024]{1,0:T(8,128)(2,1)S(1)} collective-permute-done((bf16[256,1024]{1,0:T(8,128)(2,1)S(1)}, bf16[256,1024]{1,0:T(8,128)(2,1)S(1)}, u32[]{:S(2)}, u32[]{:S(2)}) %collective-permute-start.1) | collective-permute-done | bytes 524320 | tf_op jit(solution)/shard_map/ppermute | solution.py:49
  82.7 2.0 convolution_convert_fusion.1
  84.8 10.7 %all-to-all-done.2 = bf16[16,3,64,256]{3,2,1,0:T(8,128)(2,1)} async-done(((bf16[16,3,64,256]{3,2,1,0:T(8,128)(2,1)}), bf16[16,3,64,256]{3,2,1,0:T(8,128)(2,1)}, u32[]{:S(2)}, u32[]{:S(2)}) %all-to-all-start.2) | async-done | bytes 1572896 | tf_op jit(solution)/shard_map/all_to_all | solution.py:98
  95.5 9.2 %all-to-all-start = ((bf16[16,64,1024]{2,1,0:T(8,128)(2,1)}), bf16[16,64,1024]{2,1,0:T(8,128)(2,1)}, u32[]{:S(2)}, u32[]{:S(2)}) async-start(bf16[16,64,1024]{2,1,0:T(8,128)(2,1)} %bitcast.184), calls=%async_computation | async-start | bytes 4194304 | tf_op jit(solution)/shard_map/all_to_all | solution.py:98
  105.2 8.2 %collective-permute-done.4 = bf16[256,512]{1,0:T(8,128)(2,1)S(1)} collective-permute-done((bf16[256,512]{1,0:T(8,128)(2,1)}, bf16[256,512]{1,0:T(8,128)(2,1)S(1)}, u32[]{:S(2)}, u32[]{:S(2)}) %collective-permute-start.4) | collective-permute-done | bytes 262176 | tf_op jit(solution)/shard_map/ppermute | solution.py:49
  115.2 3.0 convolution_convert_fusion
  118.2 27.6 %all-to-all-done = bf16[16,64,1024]{2,1,0:T(8,128)(2,1)} async-done(((bf16[16,64,1024]{2,1,0:T(8,128)(2,1)}), bf16[16,64,1024]{2,1,0:T(8,128)(2,1)}, u32[]{:S(2)}, u32[]{:S(2)}) %all-to-all-start) | async-done | bytes 2097184 | tf_op jit(solution)/shard_map/all_to_all | solution.py:98
  145.8 11.3 %all-to-all-start.6 = ((bf16[16,64,1024]{2,1,0:T(8,128)(2,1)}), bf16[16,64,1024]{2,1,0:T(8,128)(2,1)}, u32[]{:S(2)}, u32[]{:S(2)}) async-start(bf16[16,64,1024]{2,1,0:T(8,128)(2,1)} %bitcast.183), calls=%async_computation.6 | async-start | bytes 4194304 | tf_op jit(solution)/shard_map/all_to_all | solution.py:98
  157.1 2.3 fusion.95
  159.4 2.7 fusion.96
  162.1 3.2 fusion.48
  166.6 4.7 multiply_convert_fusion.2
  171.3 26.9 %all-to-all-done.6 = bf16[16,64,1024]{2,1,0:T(8,128)(2,1)} async-done(((bf16[16,64,1024]{2,1,0:T(8,128)(2,1)}), bf16[16,64,1024]{2,1,0:T(8,128)(2,1)}, u32[]{:S(2)}, u32[]{:S(2)}) %all-to-all-start.6) | async-done | bytes 2097184 | tf_op jit(solution)/shard_map/all_to_all | solution.py:98
  198.2 5.4 fusion
  203.7 11.4 %all-to-all-start.3 = ((bf16[16,64,1024]{2,1,0:T(8,128)(2,1)}), bf16[16,64,1024]{2,1,0:T(8,128)(2,1)}, u32[]{:S(2)}, u32[]{:S(2)}) async-start(bf16[16,64,1024]{2,1,0:T(8,128)(2,1)} %bitcast.187), calls=%async_computation.3 | async-start | bytes 4194304 | tf_op jit(solution)/shard_map/all_to_all | solution.py:98
  215.1 2.1 fusion.82
  221.7 4.2 fusion.45
  227.3 40.1 %all_gather.9 = f32[16,16,64]{2,1,0:T(8,128)} all-gather(f32[1,16,64]{2,1,0:T(8,128)} %all_gather_reshape.3), channel_id=1, replica_groups=mesh['dp'=16,'tensor'=2] {'dp'}, dimensions={0}, use_global_device_ids=true | all-gather | bytes 69632 | tf_op jit(solution)/shard_map/all_gather | solution.py:103
  267.4 5.0 fusion.40
  272.4 2.7 add_convert_fusion
  275.2 11.4 %all-to-all-start.7 = ((bf16[16,64,1024]{2,1,0:T(8,128)(2,1)}), bf16[16,64,1024]{2,1,0:T(8,128)(2,1)}, u32[]{:S(2)}, u32[]{:S(2)}) async-start(bf16[16,64,1024]{2,1,0:T(8,128)(2,1)} %bitcast.188), calls=%async_computation.7 | async-start | bytes 4194304 | tf_op jit(solution)/shard_map/all_to_all | solution.py:98
  288.0 3.9 copy.77
  291.9 1.8 select_reduce_fusion
  293.7 43.9 %all-gather = f32[256,64]{1,0:T(8,128)S(1)} all-gather(f32[16,64]{1,0:T(8,128)S(1)} %get-tuple-element.65), channel_id=2, replica_groups=mesh['dp'=16,'tensor'=2] {'dp'}, dimensions={0}, use_global_device_ids=true | all-gather | bytes 69632 | tf_op jit(solution)/shard_map/all_gather | solution.py:103
  339.6 3.3 fusion.2
  342.9 3.9 copy.78
  349.6 1.9 fusion.22
  352.1 3.2 fusion.12
  355.9 1.5 fusion.11
  357.4 1.5 fusion.10
  359.0 2.0 pad_maximum_fusion.1
  361.1 2.3 fusion.14
  364.9 1.5 collective-permute-start.3
  366.4 2.4 convolution_bitcast_fusion
  373.6 11.5 %all-to-all-start.11 = ((bf16[16,3,64,256]{3,2,1,0:T(8,128)(2,1)}), bf16[16,3,64,256]{3,2,1,0:T(8,128)(2,1)}, u32[]{:S(2)}, u32[]{:S(2)}) async-start(bf16[16,3,64,256]{3,2,1,0:T(8,128)(2,1)} %copy.80), calls=%async_computation.11 | async-start | bytes 3145728 | tf_op jit(solution)/shard_map/all_to_all | solution.py:98
  386.2 2.0 add_convert_fusion.1
  388.2 1.6 multiply_reduce_fusion
  389.9 1.6 multiply_subtract_fusion
  393.7 1.8 copy.73
  395.5 1.6 fusion.3
  401.6 1.5 collective-permute-start.6
  405.0 10.9 %collective-permute-done.6 = bf16[256,1024]{1,0:T(8,128)(2,1)S(1)} collective-permute-done((bf16[256,1024]{1,0:T(8,128)(2,1)S(1)}, bf16[256,1024]{1,0:T(8,128)(2,1)S(1)}, u32[]{:S(2)}, u32[]{:S(2)}) %collective-permute-start.6) | collective-permute-done | bytes 524320 | tf_op jit(solution)/shard_map/ppermute | solution.py:49
  417.2 8.9 %all-to-all-start.4 = ((bf16[16,16,512]{2,1,0:T(8,128)(2,1)}), bf16[16,16,512]{2,1,0:T(8,128)(2,1)S(1)}, u32[]{:S(2)}, u32[]{:S(2)}) async-start(bf16[16,16,512]{2,1,0:T(8,128)(2,1)} %bitcast.29), calls=%async_computation.4 | async-start | bytes 524288 | tf_op jit(solution)/shard_map/all_to_all | solution.py:375
  426.9 5.6 %copy.94 = bf16[1024,1664]{1,0:T(8,128)(2,1)} copy(bf16[1024,1664]{0,1:T(8,128)(2,1)} %pad_dynamic-update-slice_fusion) | data formatting | bytes 6815744
  433.8 1.9 fusion.50
  436.2 5.5 %all-to-all-start.8 = ((bf16[16,16,512]{2,1,0:T(8,128)(2,1)}), bf16[16,16,512]{2,1,0:T(8,128)(2,1)S(1)}, u32[]{:S(2)}, u32[]{:S(2)}) async-start(bf16[16,16,512]{2,1,0:T(8,128)(2,1)} %bitcast.196), calls=%async_computation.8 | async-start | bytes 524288 | tf_op jit(solution)/shard_map/all_to_all | solution.py:375
  441.7 2.8 copy.79
  444.5 7.2 %all-to-all-done.8 = bf16[16,16,512]{2,1,0:T(8,128)(2,1)S(1)} async-done(((bf16[16,16,512]{2,1,0:T(8,128)(2,1)}), bf16[16,16,512]{2,1,0:T(8,128)(2,1)S(1)}, u32[]{:S(2)}, u32[]{:S(2)}) %all-to-all-start.8) | async-done | bytes 262176 | tf_op jit(solution)/shard_map/all_to_all | solution.py:375
  451.7 3.7 all-to-all-start.10
  455.5 1.5 collective-permute-start.8
  459.0 42.0 %all-to-all-done.10 = bf16[16,3,64,256]{3,2,1,0:T(8,128)(2,1)S(1)} async-done(((bf16[16,3,64,256]{3,2,1,0:T(8,128)(2,1)}), bf16[16,3,64,256]{3,2,1,0:T(8,128)(2,1)S(1)}, u32[]{:S(2)}, u32[]{:S(2)}) %all-to-all-start.10) | async-done | bytes 1572896 | tf_op jit(solution)/shard_map/all_to_all | solution.py:98
  501.0 9.1 %all-to-all-start.5 = ((bf16[16,16,512]{2,1,0:T(8,128)(2,1)}), bf16[16,16,512]{2,1,0:T(8,128)(2,1)S(1)}, u32[]{:S(2)}, u32[]{:S(2)}) async-start(bf16[16,16,512]{2,1,0:T(8,128)(2,1)} %get-tuple-element.118), calls=%async_computation.5 | async-start | bytes 524288 | tf_op jit(solution)/shard_map/all_to_all | solution.py:379
  510.1 3.3 broadcast_select_fusion.1
  513.4 8.6 %all-to-all-done.5 = bf16[16,16,512]{2,1,0:T(8,128)(2,1)S(1)} async-done(((bf16[16,16,512]{2,1,0:T(8,128)(2,1)}), bf16[16,16,512]{2,1,0:T(8,128)(2,1)S(1)}, u32[]{:S(2)}, u32[]{:S(2)}) %all-to-all-start.5) | async-done | bytes 262176 | tf_op jit(solution)/shard_map/all_to_all | solution.py:379
  522.0 4.2 all-to-all-start.9
  526.1 1.8 maximum_convert_fusion
  528.0 2.9 slice_bitcast_fusion
  530.9 5.3 all-to-all-done.9
  (281 shorter events, 58.3 us)
Async XLA Ops:
  7.2 58.5 %copy-start = (bf16[512,1024]{1,0:T(8,128)(2,1)S(1)}, bf16[512,1024]{1,0:T(8,128)(2,1)}, u32[]{:S(2)}) copy-start(bf16[512,1024]{1,0:T(8,128)(2,1)} %param.24) | copy-start | bytes 3145732
  7.2 18.0 %collective-permute-start = (bf16[256,512]{1,0:T(8,128)(2,1)}, bf16[256,512]{1,0:T(8,128)(2,1)}, u32[]{:S(2)}, u32[]{:S(2)}) collective-permute-start(bf16[256,512]{1,0:T(8,128)(2,1)} %param.17), channel_id=1, source_target_pairs={{0,1},{1,0},{2,3},{3,2},{4,5},{5,4},{6,7},{7,6},{8,9},{9,8},{10,11... | collective-permute-start | bytes 786440 | tf_op jit(solution)/shard_map/ppermute | solution.py:49
  14.5 6.8 %copy-start.77 = (s32[16]{0:T(128)S(1)}, s32[16]{0:T(128)}, u32[]{:S(2)}) copy-start(s32[16]{0:T(128)} %param.31) | copy-start | bytes 196
  14.5 9.9 %copy-start.75 = (s32[16,4]{0,1:T(4,128)S(1)}, s32[16,4]{0,1:T(4,128)}, u32[]{:S(2)}) copy-start(s32[16,4]{0,1:T(4,128)} %param.30) | copy-start | bytes 772
  14.5 10.5 %copy-start.68 = (s32[256,8]{0,1:T(8,128)S(1)}, s32[256,8]{0,1:T(8,128)}, u32[]{:S(2)}) copy-start(s32[256,8]{0,1:T(8,128)} %param.29) | copy-start | bytes 24580
  14.5 10.8 %copy-start.43 = (bf16[256,512]{1,0:T(8,128)(2,1)S(1)}, bf16[256,512]{1,0:T(8,128)(2,1)}, u32[]{:S(2)}) copy-start(bf16[256,512]{1,0:T(8,128)(2,1)} %param.17) | copy-start | bytes 786436
  14.5 12.6 %copy-start.33 = (bf16[1024,256]{1,0:T(8,128)(2,1)S(1)}, bf16[1024,256]{1,0:T(8,128)(2,1)}, u32[]{:S(2)}) copy-start(bf16[1024,256]{1,0:T(8,128)(2,1)} %param.22) | copy-start | bytes 1572868
  14.5 12.6 %copy-start.71 = (f32[1024]{0:T(1024)S(1)}, f32[1024]{0:T(1024)}, u32[]{:S(2)}) copy-start(f32[1024]{0:T(1024)} %param.19) | copy-start | bytes 12292
  14.5 43.1 %all-to-all-start.1 = ((bf16[16,3,64,256]{3,2,1,0:T(8,128)(2,1)}), bf16[16,3,64,256]{3,2,1,0:T(8,128)(2,1)}, u32[]{:S(2)}, u32[]{:S(2)}) async-start(bf16[16,3,64,256]{3,2,1,0:T(8,128)(2,1)} %get-tuple-element.85), calls=%async_computation.1 | async-start | bytes 3145728 | tf_op jit(solution)/shard_map/all_to_all | solution.py:98
  20.6 37.0 %collective-permute-start.2 = (bf16[16,3,64,256]{3,2,1,0:T(8,128)(2,1)}, bf16[16,3,64,256]{3,2,1,0:T(8,128)(2,1)}, u32[]{:S(2)}, u32[]{:S(2)}) collective-permute-start(bf16[16,3,64,256]{3,2,1,0:T(8,128)(2,1)} %get-tuple-element.86), channel_id=1, source_target_pairs={{0,1},{1,0},{2,3},{3,2},{4,5},{5,4},{6,7},{7,6},{8,9},{9,8},{10,11... | collective-permute-start | bytes 4718600 | tf_op jit(solution)/shard_map/ppermute | solution.py:49
  21.2 6.3 %copy-start.22 = (bf16[1024,512]{1,0:T(8,128)(2,1)S(1)}, bf16[1024,512]{1,0:T(8,128)(2,1)}, u32[]{:S(2)}) copy-start(bf16[1024,512]{1,0:T(8,128)(2,1)} %param.21) | copy-start | bytes 3145732
  24.8 42.1 %copy-start.69 = (pred[256]{0:T(512)(128)(4,1)}, pred[256]{0:T(512)(128)(4,1)S(1)}, u32[]{:S(2)}) copy-start(pred[256]{0:T(512)(128)(4,1)S(1)} %get-tuple-element.75) | copy-start | bytes 772
  25.0 41.8 %copy-start.56 = (pred[32,256]{1,0:T(8,128)(4,1)}, pred[32,256]{1,0:T(8,128)(4,1)S(1)}, u32[]{:S(2)}) copy-start(pred[32,256]{1,0:T(8,128)(4,1)S(1)} %fusion.62) | copy-start | bytes 24580
  27.0 36.7 %copy-start.65 = (f32[256]{0:T(256)}, f32[256]{0:T(256)S(1)}, u32[]{:S(2)}) copy-start(f32[256]{0:T(256)S(1)} %get-tuple-element.114) | copy-start | bytes 3076
  29.5 35.6 %copy-start.59 = (f32[4,2,256]{2,1,0:T(2,128)}, f32[4,2,256]{2,1,0:T(2,128)S(1)}, u32[]{:S(2)}) copy-start(f32[4,2,256]{2,1,0:T(2,128)S(1)} %get-tuple-element.121) | copy-start | bytes 24580
  57.6 37.8 %all-to-all-start.2 = ((bf16[16,3,64,256]{3,2,1,0:T(8,128)(2,1)}), bf16[16,3,64,256]{3,2,1,0:T(8,128)(2,1)}, u32[]{:S(2)}, u32[]{:S(2)}) async-start(bf16[16,3,64,256]{3,2,1,0:T(8,128)(2,1)} %collective-permute-done.2), calls=%async_computation.2 | async-start | bytes 3145728 | tf_op jit(solution)/shard_map/all_to_all | solution.py:98
  65.7 16.0 %copy-start.57 = (f32[1024]{0:T(1024)S(1)}, f32[1024]{0:T(1024)}, u32[]{:S(2)}) copy-start(f32[1024]{0:T(1024)} %param.20) | copy-start | bytes 12292
  66.2 14.3 %collective-permute-start.1 = (bf16[256,1024]{1,0:T(8,128)(2,1)S(1)}, bf16[256,1024]{1,0:T(8,128)(2,1)S(1)}, u32[]{:S(2)}, u32[]{:S(2)}) collective-permute-start(bf16[256,1024]{1,0:T(8,128)(2,1)S(1)} %convolution_convert_fusion.9), channel_id=1, source_target_pairs={{0,1},{1,0},{2,3},{3,2},{4,5},{5,4},{6,7},{7,6},{8,9},{9,8},{10,11... | collective-permute-start | bytes 1572872 | tf_op jit(solution)/shard_map/ppermute | solution.py:49
  67.2 14.7 %copy-start.20 = (pred[1024,256]{1,0:T(32,128)(4,1)}, pred[1024,256]{1,0:T(32,128)(4,1)S(1)}, u32[]{:S(2)}) copy-start(pred[1024,256]{1,0:T(32,128)(4,1)S(1)} %bitcast_compare_fusion) | copy-start | bytes 786436
  81.4 3.4 copy-start.63
  95.5 50.3 %all-to-all-start = ((bf16[16,64,1024]{2,1,0:T(8,128)(2,1)}), bf16[16,64,1024]{2,1,0:T(8,128)(2,1)}, u32[]{:S(2)}, u32[]{:S(2)}) async-start(bf16[16,64,1024]{2,1,0:T(8,128)(2,1)} %bitcast.184), calls=%async_computation | async-start | bytes 4194304 | tf_op jit(solution)/shard_map/all_to_all | solution.py:98
  104.6 8.8 %collective-permute-start.4 = (bf16[256,512]{1,0:T(8,128)(2,1)}, bf16[256,512]{1,0:T(8,128)(2,1)S(1)}, u32[]{:S(2)}, u32[]{:S(2)}) collective-permute-start(bf16[256,512]{1,0:T(8,128)(2,1)} %param.18), channel_id=1, source_target_pairs={{0,1},{1,0},{2,3},{3,2},{4,5},{5,4},{6,7},{7,6},{8,9},{9,8},{10,11... | collective-permute-start | bytes 786440 | tf_op jit(solution)/shard_map/ppermute | solution.py:49
  145.8 52.4 %all-to-all-start.6 = ((bf16[16,64,1024]{2,1,0:T(8,128)(2,1)}), bf16[16,64,1024]{2,1,0:T(8,128)(2,1)}, u32[]{:S(2)}, u32[]{:S(2)}) async-start(bf16[16,64,1024]{2,1,0:T(8,128)(2,1)} %bitcast.183), calls=%async_computation.6 | async-start | bytes 4194304 | tf_op jit(solution)/shard_map/all_to_all | solution.py:98
  159.4 5.9 %copy-start.37 = (bf16[16,1,64,256]{3,2,1,0:T(8,128)(2,1)}, bf16[16,1,64,256]{3,2,1,0:T(8,128)(2,1)S(1)}, u32[]{:S(2)}) copy-start(bf16[16,1,64,256]{3,2,1,0:T(8,128)(2,1)S(1)} %get-tuple-element.89) | copy-start | bytes 1572868
  159.4 5.9 %copy-start.35 = (bf16[16,1,64,256]{3,2,1,0:T(8,128)(2,1)}, bf16[16,1,64,256]{3,2,1,0:T(8,128)(2,1)S(1)}, u32[]{:S(2)}) copy-start(bf16[16,1,64,256]{3,2,1,0:T(8,128)(2,1)S(1)} %get-tuple-element.88) | copy-start | bytes 1572868
  162.1 3.2 copy-start.40
  162.1 3.3 copy-start.38
  203.7 14.9 %copy-start.24 = (bf16[1024,32]{0,1:T(8,128)(2,1)S(1)}, bf16[1024,32]{0,1:T(8,128)(2,1)}, u32[]{:S(2)}) copy-start(bf16[1024,32]{0,1:T(8,128)(2,1)} %param.25) | copy-start | bytes 196612
  203.7 71.5 %all-to-all-start.3 = ((bf16[16,64,1024]{2,1,0:T(8,128)(2,1)}), bf16[16,64,1024]{2,1,0:T(8,128)(2,1)}, u32[]{:S(2)}, u32[]{:S(2)}) async-start(bf16[16,64,1024]{2,1,0:T(8,128)(2,1)} %bitcast.187), calls=%async_computation.3 | async-start | bytes 4194304 | tf_op jit(solution)/shard_map/all_to_all | solution.py:98
  215.1 6.6 %copy-start.41 = (bf16[16,1,64,256]{3,2,1,0:T(8,128)(2,1)S(1)}, bf16[16,1,64,256]{3,2,1,0:T(8,128)(2,1)}, u32[]{:S(2)}) copy-start(bf16[16,1,64,256]{3,2,1,0:T(8,128)(2,1)} %get-tuple-element.87) | copy-start | bytes 1572868
  215.1 6.6 %copy-start.42 = (bf16[16,1,64,256]{3,2,1,0:T(8,128)(2,1)S(1)}, bf16[16,1,64,256]{3,2,1,0:T(8,128)(2,1)}, u32[]{:S(2)}) copy-start(bf16[16,1,64,256]{3,2,1,0:T(8,128)(2,1)} %get-tuple-element.90) | copy-start | bytes 1572868
  267.4 5.0 copy-start.36
  267.4 5.0 copy-start.39
  267.4 5.0 copy-start.80
  267.4 5.1 copy-start.82
  275.2 91.2 %all-to-all-start.7 = ((bf16[16,64,1024]{2,1,0:T(8,128)(2,1)}), bf16[16,64,1024]{2,1,0:T(8,128)(2,1)}, u32[]{:S(2)}, u32[]{:S(2)}) async-start(bf16[16,64,1024]{2,1,0:T(8,128)(2,1)} %bitcast.188), calls=%async_computation.7 | async-start | bytes 4194304 | tf_op jit(solution)/shard_map/all_to_all | solution.py:98
  348.4 3.7 copy-start.48
  348.4 3.7 copy-start.51
  351.5 33.7 %collective-permute-start.7 = (bf16[32,1024]{1,0:T(8,128)(2,1)}, bf16[32,1024]{1,0:T(8,128)(2,1)}, u32[]{:S(2)}, u32[]{:S(2)}) collective-permute-start(bf16[32,1024]{1,0:T(8,128)(2,1)} %fusion.22), channel_id=1, source_target_pairs={{0,1},{1,0},{2,3},{3,2},{4,5},{5,4},{6,7},{7,6},{8,9},{9,8},{10,11... | collective-permute-start | bytes 196616 | tf_op jit(solution)/shard_map/ppermute | solution.py:49
  352.0 3.3 copy-start.21
  352.0 3.3 copy-start.62
  352.0 3.3 copy-start.81
  352.1 3.8 copy-start.83
  364.9 21.3 %collective-permute-start.3 = (bf16[256,512]{1,0:T(8,128)(2,1)}, bf16[256,512]{1,0:T(8,128)(2,1)}, u32[]{:S(2)}, u32[]{:S(2)}) collective-permute-start(bf16[256,512]{1,0:T(8,128)(2,1)} %constant_dynamic-slice_fusion.1), channel_id=1, source_target_pairs={{0,1},{1,0},{2,3},{3,2},{4,5},{5,4},{6,7},{7,6},{8,9},{9,8},{10,11... | collective-permute-start | bytes 786440 | tf_op jit(solution)/shard_map/ppermute | solution.py:49
  370.2 18.0 %collective-permute-start.5 = (bf16[256,1024]{1,0:T(8,128)(2,1)}, bf16[256,1024]{1,0:T(8,128)(2,1)}, u32[]{:S(2)}, u32[]{:S(2)}) collective-permute-start(bf16[256,1024]{1,0:T(8,128)(2,1)} %fusion.13), channel_id=1, source_target_pairs={{0,1},{1,0},{2,3},{3,2},{4,5},{5,4},{6,7},{7,6},{8,9},{9,8},{10,11... | collective-permute-start | bytes 1572872 | tf_op jit(solution)/shard_map/ppermute | solution.py:49
  373.6 14.6 %copy-start.58 = (f32[1024]{0:T(1024)S(1)}, f32[1024]{0:T(1024)}, u32[]{:S(2)}) copy-start(f32[1024]{0:T(1024)} %param.20) | copy-start | bytes 12292
  373.6 14.6 %copy-start.64 = (f32[256]{0:T(256)S(1)}, f32[256]{0:T(256)}, u32[]{:S(2)}) copy-start(f32[256]{0:T(256)} %copy-done.63) | copy-start | bytes 3076
  373.6 43.6 %all-to-all-start.11 = ((bf16[16,3,64,256]{3,2,1,0:T(8,128)(2,1)}), bf16[16,3,64,256]{3,2,1,0:T(8,128)(2,1)}, u32[]{:S(2)}, u32[]{:S(2)}) async-start(bf16[16,3,64,256]{3,2,1,0:T(8,128)(2,1)} %copy.80), calls=%async_computation.11 | async-start | bytes 3145728 | tf_op jit(solution)/shard_map/all_to_all | solution.py:98
  385.1 3.1 copy-start.2
  385.1 4.7 copy-start.17
  385.2 4.7 copy-start.19
  385.2 4.7 copy-start.74
  401.6 14.2 %collective-permute-start.6 = (bf16[256,1024]{1,0:T(8,128)(2,1)S(1)}, bf16[256,1024]{1,0:T(8,128)(2,1)S(1)}, u32[]{:S(2)}, u32[]{:S(2)}) collective-permute-start(bf16[256,1024]{1,0:T(8,128)(2,1)S(1)} %fusion.17), channel_id=1, source_target_pairs={{0,1},{1,0},{2,3},{3,2},{4,5},{5,4},{6,7},{7,6},{8,9},{9,8},{10,11... | collective-permute-start | bytes 1572872 | tf_op jit(solution)/shard_map/ppermute | solution.py:49
  405.0 12.2 %copy-start.11 = (bf16[1024,1664]{0,1:T(8,128)(2,1)}, bf16[1024,1664]{0,1:T(8,128)(2,1)S(1)}, u32[]{:S(2)}) copy-start(bf16[1024,1664]{0,1:T(8,128)(2,1)S(1)} %fusion.16) | copy-start | bytes 10223620
  417.2 19.0 %all-to-all-start.4 = ((bf16[16,16,512]{2,1,0:T(8,128)(2,1)}), bf16[16,16,512]{2,1,0:T(8,128)(2,1)S(1)}, u32[]{:S(2)}, u32[]{:S(2)}) async-start(bf16[16,16,512]{2,1,0:T(8,128)(2,1)} %bitcast.29), calls=%async_computation.4 | async-start | bytes 524288 | tf_op jit(solution)/shard_map/all_to_all | solution.py:375
  426.1 110.9 %reduce-scatter.4.cloned.1.call-start = ((), (), s32[]{:S(2)}) async-start(), calls=%async_computation.13 | async-start | bytes 3620864
  436.2 15.6 %all-to-all-start.8 = ((bf16[16,16,512]{2,1,0:T(8,128)(2,1)}), bf16[16,16,512]{2,1,0:T(8,128)(2,1)S(1)}, u32[]{:S(2)}, u32[]{:S(2)}) async-start(bf16[16,16,512]{2,1,0:T(8,128)(2,1)} %bitcast.196), calls=%async_computation.8 | async-start | bytes 524288 | tf_op jit(solution)/shard_map/all_to_all | solution.py:375
  444.5 12.4 %copy-start.76 = (s32[16]{0:T(128)S(1)}, s32[16]{0:T(128)}, u32[]{:S(2)}) copy-start(s32[16]{0:T(128)} %get-tuple-element.119) | copy-start | bytes 196
  444.5 12.5 %copy-start.78 = (s32[16]{0:T(128)S(1)}, s32[16]{0:T(128)}, u32[]{:S(2)}) copy-start(s32[16]{0:T(128)} %param.31) | copy-start | bytes 196
  451.7 49.3 %all-to-all-start.10 = ((bf16[16,3,64,256]{3,2,1,0:T(8,128)(2,1)}), bf16[16,3,64,256]{3,2,1,0:T(8,128)(2,1)S(1)}, u32[]{:S(2)}, u32[]{:S(2)}) async-start(bf16[16,3,64,256]{3,2,1,0:T(8,128)(2,1)} %copy.79), calls=%async_computation.10 | async-start | bytes 3145728 | tf_op jit(solution)/shard_map/all_to_all | solution.py:98
  455.5 54.7 %collective-permute-start.8 = (bf16[16,3,64,256]{3,2,1,0:T(8,128)(2,1)}, bf16[16,3,64,256]{3,2,1,0:T(8,128)(2,1)}, u32[]{:S(2)}, u32[]{:S(2)}) collective-permute-start(bf16[16,3,64,256]{3,2,1,0:T(8,128)(2,1)} %all-to-all-done.11), channel_id=1, source_target_pairs={{0,1},{1,0},{2,3},{3,2},{4,5},{5,4},{6,7},{7,6},{8,9},{9,8},{10,11... | collective-permute-start | bytes 4718600 | tf_op jit(solution)/shard_map/ppermute | solution.py:49
  501.0 9.1 %copy-start.10 = (bf16[16,3,64,256]{3,2,1,0:T(8,128)(2,1)}, bf16[16,3,64,256]{3,2,1,0:T(8,128)(2,1)S(1)}, u32[]{:S(2)}) copy-start(bf16[16,3,64,256]{3,2,1,0:T(8,128)(2,1)S(1)} %all-to-all-done.10) | copy-start | bytes 4718596
  501.0 20.9 %all-to-all-start.5 = ((bf16[16,16,512]{2,1,0:T(8,128)(2,1)}), bf16[16,16,512]{2,1,0:T(8,128)(2,1)S(1)}, u32[]{:S(2)}, u32[]{:S(2)}) async-start(bf16[16,16,512]{2,1,0:T(8,128)(2,1)} %get-tuple-element.118), calls=%async_computation.5 | async-start | bytes 524288 | tf_op jit(solution)/shard_map/all_to_all | solution.py:379
  522.0 14.2 %all-to-all-start.9 = ((bf16[16,16,512]{2,1,0:T(8,128)(2,1)}), bf16[16,16,512]{2,1,0:T(8,128)(2,1)S(1)}, u32[]{:S(2)}, u32[]{:S(2)}) async-start(bf16[16,16,512]{2,1,0:T(8,128)(2,1)} %get-tuple-element.117), calls=%async_computation.9 | async-start | bytes 524288 | tf_op jit(solution)/shard_map/all_to_all | solution.py:379
  (43 other events, 63.2 us)
Sparse Core Ops, SparseCore 0:
  432.7 89.6 reduce-scatter.3

commit v2 on v1

--- a/solution.py
+++ b/solution.py
@@ -1,6 +1,8 @@
 import jax
 import jax.numpy as jnp
 from jax import lax
+from jax.experimental import pallas as pl
+from jax.experimental.pallas import tpu as pltpu
 from jax.sharding import PartitionSpec as P
 
 HEAD_DIM = 64
@@ -53,6 +55,187 @@
     return lax.dot_general(
         left, right, ((contract[:1], contract[1:]), ((), ())), preferred_element_type=jnp.float32
     )
+
+
+def after(values, *others):
+    return lax.optimization_barrier((values,) + others)[0]
+
+
+def dot(left, right, left_axis=1, right_axis=0):
+    return lax.dot_general(
+        left,
+        right,
+        (((left_axis,), (right_axis,)), ((), ())),
+        preferred_element_type=jnp.float32,
+    )
+
+
+def expert_kernel(
+    expert_ref,
+    rows_ref,
+    cot_ref,
+    gate_ref,
+    pair_ref,
+    router_ref,
+    back_ref,
+    moe_ref,
+    hidden_ref,
+    gate_grad_ref,
+    up_grad_ref,
+    slot_grad_ref,
+    logits_ref,
+):
+    width = rows_ref.shape[1]
+    expert_count = router_ref.shape[0]
+    rows = rows_ref[...]
+    cot = cot_ref[:, :width].astype(jnp.float32)
+    router = router_ref[...]
+    logits = jnp.where(
+        cot_ref[:, width : width + expert_count].astype(jnp.float32) > 0.5,
+        dot(rows, router, 1, 1),
+        NEGATIVE,
+    )
+    terms = jnp.exp(logits - jnp.max(logits, axis=1, keepdims=True))
+    gates = terms / jnp.sum(terms, axis=1, keepdims=True)
+    own = (lax.broadcasted_iota(jnp.int32, gates.shape, 1) == expert_ref[0]).astype(jnp.float32)
+    gate = jnp.sum(gates * own, axis=1, keepdims=True)
+
+    def weight(ref, *place):
+        value = ref[(slice(None),) + place]
+        return value.reshape(width, value.shape[-1])
+
+    halves = range(gate_ref.shape[1])
+    columns = gate_ref.shape[-1]
+    kept = []
+    out = 0.0
+    for f in halves:
+        gate_pre = dot(rows, weight(gate_ref, f))
+        up_pre = dot(rows, weight(pair_ref, f, 0))
+        sigma = 1.0 / (1.0 + jnp.exp(-gate_pre))
+        hidden = (gate_pre * sigma * up_pre).astype(jnp.bfloat16)
+        hidden_ref[:, f * columns : (f + 1) * columns] = hidden
+        out = out + dot(hidden, weight(pair_ref, f, 1), 1, 1)
+        kept.append((gate_pre, up_pre, sigma))
+    gate_grad = jnp.sum(out * cot, axis=1, keepdims=True)
+    moe_ref[...] = (gate * out).astype(jnp.bfloat16)
+    slot_grad = (gate * cot).astype(jnp.bfloat16)
+    slot_grad_ref[...] = slot_grad
+    logits_grad = gate_grad * gate * (own - gates)
+    upper = logits_grad.astype(jnp.bfloat16)
+    lower = (logits_grad - upper.astype(jnp.float32)).astype(jnp.bfloat16)
+    logits_ref[0] = upper
+    logits_ref[1] = lower
+    back = dot(upper, router) + dot(lower, router)
+    for f in halves:
+        gate_pre, up_pre, sigma = kept[f]
+        hidden_grad = dot(slot_grad, weight(pair_ref, f, 1))
+        gate_pre_grad = hidden_grad * up_pre * sigma * (1.0 + gate_pre * (1.0 - sigma))
+        gate_pre_grad = gate_pre_grad.astype(jnp.bfloat16)
+        up_pre_grad = (hidden_grad * gate_pre * sigma).astype(jnp.bfloat16)
+        gate_grad_ref[:, f * columns : (f + 1) * columns] = gate_pre_grad
+        up_grad_ref[:, f * columns : (f + 1) * columns] = up_pre_grad
+        back = back + dot(gate_pre_grad, weight(gate_ref, f), 1, 1)
+        back = back + dot(up_pre_grad, weight(pair_ref, f, 0), 1, 1)
+    back_ref[...] = back.astype(jnp.bfloat16)
+
+
+def run_expert(expert, rows, cot, gate_w, pair_w, router_t):
+    count, width = rows.shape
+    hidden = 2 * gate_w.shape[-1]
+    step = count // 4
+    bf16 = jnp.bfloat16
+    row_block = lambda columns: pl.BlockSpec((step, columns), lambda i: (i, 0))
+    whole = lambda value: pl.BlockSpec(value.shape, lambda i: (0,) * value.ndim)
+    experts = router_t.shape[0]
+    return pl.pallas_call(
+        expert_kernel,
+        grid=(4,),
+        in_specs=[
+            pl.BlockSpec(memory_space=pltpu.SMEM),
+            row_block(width),
+            row_block(cot.shape[1]),
+            whole(gate_w),
+            whole(pair_w),
+            whole(router_t),
+        ],
+        out_specs=[
+            row_block(width),
+            row_block(width),
+            row_block(hidden),
+            row_block(hidden),
+            row_block(hidden),
+            row_block(width),
+            pl.BlockSpec((2, step, experts), lambda i: (0, i, 0)),
+        ],
+        out_shape=[
+            jax.ShapeDtypeStruct((count, width), bf16),
+            jax.ShapeDtypeStruct((count, width), bf16),
+            jax.ShapeDtypeStruct((count, hidden), bf16),
+            jax.ShapeDtypeStruct((count, hidden), bf16),
+            jax.ShapeDtypeStruct((count, hidden), bf16),
+            jax.ShapeDtypeStruct((count, width), bf16),
+            jax.ShapeDtypeStruct((2, count, experts), bf16),
+        ],
+        compiler_params=pltpu.CompilerParams(vmem_limit_bytes=48 << 20),
+        cost_estimate=pl.CostEstimate(
+            flops=12 * count * width * hidden, bytes_accessed=16 << 20, transcendentals=count * hidden
+        ),
+        name="expert_rows",
+    )(expert.reshape(1), rows, cot, gate_w, pair_w, router_t)
+
+
+def expert_grad_kernel(
+    rows_ref, slot_grad_ref, hidden_ref, gate_grad_ref, up_grad_ref, logits_ref, out_ref, router_ref
+):
+    rows = rows_ref[...]
+    blocks, planes, _, block_rows, columns = out_ref.shape
+    pieces = (
+        dot(rows, gate_grad_ref[...], 0, 0),
+        dot(rows, up_grad_ref[...], 0, 0),
+        dot(slot_grad_ref[...], hidden_ref[...], 0, 0),
+    )
+    for i, piece in enumerate(pieces):
+        piece = piece.astype(jnp.bfloat16)
+        for f in range(planes):
+            out_ref[:, f, i] = piece[:, f * columns : (f + 1) * columns].reshape(
+                blocks, block_rows, columns
+            )
+    router_ref[...] = dot(logits_ref[0], rows, 0, 0) + dot(logits_ref[1], rows, 0, 0)
+
+
+def run_expert_grads(rows, slot_grad, hidden, gate_grad, up_grad, logits, shape):
+    count, width = rows.shape
+    steps = 4
+    step = width // steps
+    blocks = shape[0] // steps
+    column_block = pl.BlockSpec((count, step), lambda i: (0, i))
+    whole = lambda value: pl.BlockSpec(value.shape, lambda i: (0,) * value.ndim)
+    experts = logits.shape[2]
+    return pl.pallas_call(
+        expert_grad_kernel,
+        grid=(steps,),
+        in_specs=[
+            column_block,
+            column_block,
+            whole(hidden),
+            whole(gate_grad),
+            whole(up_grad),
+            whole(logits),
+        ],
+        out_specs=[
+            pl.BlockSpec((blocks,) + shape[1:], lambda i: (i, 0, 0, 0, 0)),
+            pl.BlockSpec((experts, step), lambda i: (0, i)),
+        ],
+        out_shape=[
+            jax.ShapeDtypeStruct(shape, jnp.bfloat16),
+            jax.ShapeDtypeStruct((experts, width), jnp.float32),
+        ],
+        compiler_params=pltpu.CompilerParams(vmem_limit_bytes=48 << 20),
+        cost_estimate=pl.CostEstimate(
+            flops=6 * count * width * hidden.shape[1], bytes_accessed=12 << 20, transcendentals=0
+        ),
+        name="expert_grads",
+    )(rows, slot_grad, hidden, gate_grad, up_grad, logits)
 
 
 def local(
@@ -84,23 +267,22 @@
     plane = lax.axis_index("tensor")
     devices = lax.axis_size("dp")
     dp_index = lax.axis_index("dp")
-    plane_experts = expert_count // 2
-    members = plane_experts
+    members = expert_count // 2
+    near = members // 2
     clusters = devices // members
     member = dp_index % members
-    if clusters == 1:
-        inside = across = None
-    else:
-        inside = [[c * members + m for m in range(members)] for c in range(clusters)]
-        across = [[c * members + m for c in range(clusters)] for m in range(members)]
-
-    def exchange(values):
-        return lax.all_to_all(
-            values, "dp", split_axis=0, concat_axis=0, tiled=True, axis_index_groups=inside
-        )
-
-    def gather_small(values):
-        return lax.all_gather(values, "dp", axis=0, tiled=False, axis_index_groups=inside)
+    expert = 2 * member + plane
+    inside = [[c * members + m for m in range(members)] for c in range(clusters)]
+    across = [[c * members + m for c in range(clusters)] for m in range(members)]
+
+    def cross(values):
+        return lax.ppermute(values, "dp", [(i, i ^ near) for i in range(devices)])
+
+    def spread(blocks):
+        return [blocks[0]] + [
+            lax.ppermute(blocks[s], "dp", [(i, i ^ s) for i in range(devices)])
+            for s in range(1, near)
+        ]
 
     def halves(values, axis):
         size = values.shape[axis] // 2
@@ -118,22 +300,61 @@
         low = part.astype(jnp.bfloat16)
         return low.astype(jnp.float32) + swap_tensor(low).astype(jnp.float32)
 
-    down_t = jnp.swapaxes(down_weight, 1, 2)
-    stacked = jnp.stack([gate_weight, up_weight, down_t], axis=1)
-    own_w, other_w = halves(stacked, 0)
-    other_w = swap_tensor(other_w)
-
-    def place_weights(values):
-        values = exchange(values)
-        if clusters > 1:
-            values = lax.all_gather(values, "dp", axis=0, tiled=True, axis_index_groups=across)
-        return [values[:, i].reshape(width, -1) for i in range(3)]
-
-    own_w = place_weights(own_w)
-    other_w = place_weights(other_w)
-    gate_full, up_full, down_full = [
-        jnp.concatenate([a, b], axis=1) for a, b in zip(own_w, other_w)
-    ]
+    routes_t = routes.T
+    routes_pair = jnp.stack([routes_t, cross(routes_t)])
+    full_inputs = join(inputs, swap_tensor(inputs), 1)
+    cot_cross = cross(cotangent)
+
+    def to_owner(values):
+        if clusters == 1:
+            owned = lax.all_to_all(
+                values, ("dp", "tensor"), split_axis=0, concat_axis=0, tiled=True
+            )
+            return owned.reshape((devices, 2) + owned.shape[1:])
+        by_plane = values.reshape((members, 2) + values.shape[1:])
+        own_w = lax.dynamic_index_in_dim(by_plane, plane, 1, keepdims=False)
+        other_w = swap_tensor(lax.dynamic_index_in_dim(by_plane, 1 - plane, 1, keepdims=False))
+        owned = jnp.stack(
+            [jnp.where(plane == 0, own_w, other_w), jnp.where(plane == 0, other_w, own_w)], axis=1
+        )
+        owned = lax.all_to_all(
+            owned, "dp", split_axis=0, concat_axis=0, tiled=True, axis_index_groups=inside
+        )
+        owned = lax.all_gather(owned, "dp", axis=0, tiled=True, axis_index_groups=across)
+        owned = owned.reshape((members, clusters) + owned.shape[1:])
+        owned = jnp.moveaxis(owned, 1, -3)
+        return owned.reshape(owned.shape[:-3] + (-1, owned.shape[-1]))
+
+    def from_owner(values):
+        if clusters == 1:
+            return lax.all_to_all(
+                values.reshape((2 * devices,) + values.shape[2:]),
+                ("dp", "tensor"),
+                split_axis=0,
+                concat_axis=0,
+                tiled=True,
+            )
+        values = values.reshape(values.shape[:-2] + (clusters, -1, values.shape[-1]))
+        values = jnp.moveaxis(values, -3, 1)
+        values = values.reshape((devices,) + values.shape[2:])
+        values = lax.psum_scatter(
+            values, "dp", scatter_dimension=0, tiled=True, axis_index_groups=across
+        )
+        values = lax.all_to_all(
+            values, "dp", split_axis=0, concat_axis=0, tiled=True, axis_index_groups=inside
+        )
+        own_g = lax.dynamic_index_in_dim(values, plane, 1, keepdims=False)
+        other_g = swap_tensor(lax.dynamic_index_in_dim(values, 1 - plane, 1, keepdims=False))
+        values = jnp.stack(
+            [jnp.where(plane == 0, own_g, other_g), jnp.where(plane == 0, other_g, own_g)], axis=1
+        )
+        return values.reshape((expert_count,) + values.shape[2:])
+
+    owned_gate = to_owner(after(gate_weight, cot_cross))
+
+    cot_pair = jnp.concatenate([cotangent, cot_cross], axis=0)
+    cot_pair = join(cot_pair, swap_tensor(cot_pair), 1)
+    full_cot = cot_pair[:row_count]
 
     rank_list = jnp.arange(devices, dtype=jnp.int32)
     holder = jnp.sum(jnp.where(placement == dp_index, rank_list, 0))
@@ -147,25 +368,46 @@
     past = row_index[:, None] >= seg_ends[None, :]
     segment = jnp.sum(past.astype(jnp.int32), axis=1)
     positions = row_index - jnp.max(jnp.where(past, seg_ends[None, :], 0), axis=1)
-    token_live = segment < seq_count
+    token_live = row_index < jnp.sum(slot_lengths)
     allowed = (segment[:, None] == segment[None, :]) & (row_index[None, :] <= row_index[:, None])
     cos_table, sin_table = rope_tables(positions, HEAD_DIM // 2)
     live_column = token_live.astype(jnp.float32)[:, None]
+
+    before = (row_index[:, None] < row_index[None, :]).astype(jnp.bfloat16)
     experts = jnp.arange(expert_count, dtype=jnp.int32)
-    picked = jnp.any(routes.T[:, None, :] == experts[None, :, None], axis=0)
-    counted = picked & token_live[None, :]
-    before = (row_index[:, None] < row_index[None, :]).astype(jnp.bfloat16)
+    near_ids = jnp.arange(near, dtype=jnp.int32)
+    near_experts = 2 * (member ^ near_ids) + plane
+    counted = jnp.any(routes_pair[None] == near_experts[:, None, None, None], axis=2)
+    counted = (counted & token_live[None, None, :]).reshape(2 * near, row_count)
     place = mm(counted.astype(jnp.bfloat16), before, (1, 0)).astype(jnp.int32)
-    slot_of = jnp.where(counted & (place < capacity), place, -1)
-    slot_own = lax.dynamic_slice_in_dim(slot_of, plane * plane_experts, plane_experts, 0)
-    hot = slot_own[:, None, :] == jnp.arange(capacity, dtype=jnp.int32)[None, :, None]
-    dispatch_t = hot.astype(jnp.bfloat16).reshape(plane_experts * capacity, row_count)
-
-    full_cot = join(cotangent, swap_tensor(cotangent), 1)
-    slot_cot = mm(dispatch_t, full_cot, (1, 0)).astype(jnp.bfloat16)
-    slot_cot = exchange(slot_cot)
-
-    full_inputs = join(inputs, swap_tensor(inputs), 1)
+    place = jnp.where(counted & (place < capacity), place, -1).reshape(near, 2, 1, 1, row_count)
+    pair_ids = jnp.arange(2, dtype=jnp.int32)
+    same = pair_ids[:, None] == pair_ids[None, :]
+    slots = jnp.arange(capacity, dtype=jnp.int32)
+    hot = (place == slots[None, None, :, None, None]) & same[None, :, None, :, None]
+    hot = hot.astype(jnp.bfloat16).reshape(2 * near * capacity, 2 * row_count)
+    picked = jnp.any(routes_pair[:, :, :, None] == experts[None, None, None, :], axis=1)
+    picked = jnp.pad(
+        picked.astype(jnp.bfloat16).reshape(2 * row_count, expert_count),
+        ((0, 0), (0, 128 - expert_count)),
+    )
+
+    def dispatch(tokens):
+        rows = mm(hot, tokens, (1, 0)).astype(jnp.bfloat16)
+        return jnp.concatenate(spread(jnp.split(rows, near, axis=0)), axis=0)
+
+    def combine(rows):
+        rows = jnp.concatenate(spread(jnp.split(rows, near, axis=0)), axis=0)
+        parts = mm(hot, rows, (0, 0))
+        mine, others = parts[:row_count], parts[row_count:]
+        others_own, others_away = halves(others, 1)
+        mine_own, mine_away = halves(mine, 1)
+        others = others_own + swap_tensor(others_away.astype(jnp.bfloat16)).astype(jnp.float32)
+        mine = mine_own + swap_tensor(mine_away.astype(jnp.bfloat16)).astype(jnp.float32)
+        return mine + cross(others.astype(jnp.bfloat16)).astype(jnp.float32)
+
+    slot_cot = dispatch(jnp.concatenate([cot_pair, picked], axis=1))
+
     wide_inputs = full_inputs.astype(jnp.float32)
     attn_scale = lax.rsqrt(jnp.mean(wide_inputs * wide_inputs, axis=-1, keepdims=True) + EPSILON)
     normed = (wide_inputs * attn_scale * attn_gain).astype(jnp.bfloat16)
@@ -203,72 +445,35 @@
     ).reshape(row_count, heads_local * HEAD_DIM)
     context = (context * live_column).astype(jnp.bfloat16)
     attn_part = jnp.dot(context, output_weight, preferred_element_type=jnp.float32)
-    residual = wide_inputs + add_planes(attn_part)
+    attn_whole = add_planes(attn_part)
+    residual = wide_inputs + attn_whole
     expert_scale = lax.rsqrt(jnp.mean(residual * residual, axis=-1, keepdims=True) + EPSILON)
     mixed_rows = (residual * expert_scale * expert_gain).astype(jnp.bfloat16)
-
-    slot_in = exchange(mm(dispatch_t, mixed_rows, (1, 0)).astype(jnp.bfloat16))
-
-    logits = mm(router_weight, mixed_rows, (0, 1))
-    logits = jnp.where(picked, logits, NEGATIVE)
-    weights = jnp.exp(logits - jnp.max(logits, axis=0, keepdims=True))
-    gates = weights / jnp.sum(weights, axis=0, keepdims=True)
-    gates_own = lax.dynamic_slice_in_dim(gates, plane * plane_experts, plane_experts, 0)
-    weighted = jnp.where(hot, gates_own[:, None, :], 0.0)
-    gate_slot = jnp.sum(weighted, axis=2)
-    weighted = weighted.astype(jnp.bfloat16).reshape(plane_experts * capacity, row_count)
-    gate_rows = lax.dynamic_index_in_dim(gather_small(gate_slot), member, 1, keepdims=False)
-    gate_rows = gate_rows.reshape(members * capacity, 1)
-
-    gate_pre = mm(slot_in, gate_full, (1, 0))
-    up_pre = mm(slot_in, up_full, (1, 0))
-    sigma = jax.nn.sigmoid(gate_pre)
-    hidden = (gate_pre * sigma * up_pre).astype(jnp.bfloat16)
-    expert_out = mm(hidden, down_full, (1, 1))
-    slot_gate_grad = jnp.sum(expert_out * slot_cot.astype(jnp.float32), axis=1)
-    slot_gate_grad = slot_gate_grad.reshape(members, capacity)
-    slot_gate_grad = lax.dynamic_index_in_dim(
-        gather_small(slot_gate_grad), member, 1, keepdims=False
-    )
-    hidden_grad = mm(slot_cot, down_full, (1, 0))
-    gate_pre_grad = hidden_grad * up_pre * sigma * (1.0 + gate_pre * (1.0 - sigma))
-    up_pre_grad = hidden_grad * gate_pre * sigma
-    slot_in_grad = mm(gate_pre_grad.astype(jnp.bfloat16), gate_full, (1, 1)) + mm(
-        up_pre_grad.astype(jnp.bfloat16), up_full, (1, 1)
-    )
-    slot_in_grad = exchange(slot_in_grad.astype(jnp.bfloat16))
-    expert_out = exchange(expert_out.astype(jnp.bfloat16))
-    scaled_cot = (gate_rows * slot_cot.astype(jnp.float32)).astype(jnp.bfloat16)
-    w_grads = [
-        mm(slot_in, (gate_rows * gate_pre_grad).astype(jnp.bfloat16), (0, 0)),
-        mm(slot_in, (gate_rows * up_pre_grad).astype(jnp.bfloat16), (0, 0)),
-        mm(scaled_cot, hidden, (0, 0)),
-    ]
-    w_grads = jnp.stack([w.reshape(devices, width // devices, -1) for w in w_grads], axis=1)
-    w_grads = w_grads.astype(jnp.bfloat16)
-
-    moe_part = mm(weighted, expert_out, (0, 0)).astype(jnp.bfloat16)
-    moe_own, moe_other = halves(moe_part, 1)
-    moe_half = moe_own.astype(jnp.float32) + swap_tensor(moe_other).astype(jnp.float32)
-    residual_half, _ = halves(residual, 1)
-    outputs_half = (residual_half + moe_half).astype(jnp.bfloat16)
-
-    token_gate_grad = jnp.sum(
-        jnp.where(hot, slot_gate_grad[:, :, None], 0.0), axis=1
-    )
-    mean_grad = jnp.sum(gates_own * token_gate_grad, axis=0, keepdims=True)
-    spread = jnp.zeros_like(gates)
-    spread = lax.dynamic_update_slice_in_dim(spread, token_gate_grad, plane * plane_experts, 0)
-    logits_grad = gates * (spread - mean_grad)
-    logits_upper, logits_lower = split_parts(logits_grad)
-    router_part = mm(logits_upper, mixed_rows, (1, 0)) + mm(logits_lower, mixed_rows, (1, 0))
+    mixed_cross = cross(halves(mixed_rows, 1)[0])
+    owned_pair = to_owner(
+        after(jnp.stack([up_weight, jnp.swapaxes(down_weight, 1, 2)], axis=1), mixed_cross)
+    )
+    mixed_cross = join(mixed_cross, swap_tensor(mixed_cross), 1)
+    slot_in = dispatch(jnp.concatenate([mixed_rows, mixed_cross], axis=0))
+
+    slot_back, slot_moe, hidden, gate_pre_grad, up_pre_grad, slot_grad, logits_grad = run_expert(
+        expert, slot_in, slot_cot, owned_gate, owned_pair, router_weight.T
+    )
+    mixed_half = combine(slot_back).astype(jnp.bfloat16)
+    w_grads, router_part = run_expert_grads(
+        slot_in,
+        slot_grad,
+        hidden,
+        gate_pre_grad,
+        up_pre_grad,
+        logits_grad,
+        (members, 2, 3, width // members, gate_weight.shape[2]),
+    )
+    mixed_grad = join(mixed_half, after(swap_tensor(mixed_half), w_grads), 1).astype(jnp.float32)
+    moe_half = combine(slot_moe)
+    outputs_half = (halves(residual, 1)[0] + moe_half).astype(jnp.bfloat16)
     router_grad = add_planes(router_part)
-    mixed_part = (
-        mm(weighted, slot_in_grad, (0, 0))
-        + mm(logits_upper, router_weight, (0, 1))
-        + mm(logits_lower, router_weight, (0, 1))
-    )
-    mixed_grad = add_planes(mixed_part)
+
     scaled_two = mixed_grad * expert_gain
     expert_gain_grad = jnp.sum(mixed_grad * residual * expert_scale, axis=0)
     cube_two = expert_scale * expert_scale * expert_scale
@@ -353,35 +558,22 @@
     attn_gain_part = share[:, cuts[3] + expert_count]
     expert_gain_part = share[:, cuts[3] + expert_count + 1]
 
-    own_g, other_g = jnp.split(w_grads, 2, axis=3)
-
-    def return_grads(values):
-        if clusters > 1:
-            values = lax.psum_scatter(
-                values, "dp", scatter_dimension=0, tiled=True, axis_index_groups=across
-            )
-        return exchange(values)
-
-    other_g = swap_tensor(return_grads(other_g))
-    own_g = return_grads(own_g)
-    both = join(own_g, other_g, 0).astype(jnp.float32)
-    gate_w_part = both[:, 0]
-    up_w_part = both[:, 1]
-    down_w_part = jnp.swapaxes(both[:, 2], 1, 2)
+    both = from_owner(after(w_grads, mixed_half))
+    gate_w_part = both[:, 0].astype(jnp.float32)
+    up_w_part = both[:, 1].astype(jnp.float32)
+    down_w_part = jnp.swapaxes(both[:, 2], 1, 2).astype(jnp.float32)
 
     piece_rows = row_count // devices
-
-    def reroute(values):
-        spread = lax.all_to_all(
-            values.reshape(devices, piece_rows, -1), "dp", split_axis=0, concat_axis=0, tiled=True
-        )
-        moved = jnp.take(spread, placement, axis=0)
-        return lax.all_to_all(moved, "dp", split_axis=0, concat_axis=0, tiled=True).reshape(
-            row_count, -1
-        )
-
-    outputs = reroute(outputs_half)
-    input_result = reroute(input_half.astype(jnp.bfloat16)).astype(jnp.float32)
+    moved = jnp.concatenate([outputs_half, input_half.astype(jnp.bfloat16)], axis=1)
+    moved = after(moved, both)
+    moved = lax.all_to_all(
+        moved.reshape(devices, piece_rows, width), "dp", split_axis=0, concat_axis=0, tiled=True
+    )
+    moved = jnp.take(moved, placement, axis=0)
+    moved = lax.all_to_all(moved, "dp", split_axis=0, concat_axis=0, tiled=True)
+    moved = moved.reshape(row_count, width)
+    outputs = moved[:, :width_half]
+    input_result = moved[:, width_half:].astype(jnp.float32)
     return (
         outputs,
         input_result,

time: 553 us -> 430 us (0.78)
  blocking collectives: 84 us -> 0 us
  starting transfers between devices: 108 us -> 72.6 us
  matrix products: 57.1 us -> 22 us
  Pallas kernels: 0 us -> 24.2 us
  waiting for transfers between devices: 189 us -> 210 us
  other arithmetic: 37.6 us -> 29.6 us
    ppermute x0 -> x33, waiting for transfers between devices: none -> 140 us  [the longest x28 115 us: spread(): lax.ppermute(blocks[s], 'dp', [(i, i ^ s) for i in range(devices)])]
    all_to_all x12 -> x5, waiting for transfers between devices: 129 us -> 18.6 us  [the longest x1 13.1 us: local(): lax.all_to_all(moved.reshape(devices, piece_rows, width), 'dp', split_axi...]
    all_gather x2 -> x0, blocking collectives: 84 us -> none  [gather_small(): lax.all_gather(values, 'dp', axis=0, tiled=False, axis_index_groups=inside)]
    all_to_all x12 -> x5, starting transfers between devices: 98 us -> 21.4 us  [the longest x2 10 us: to_owner(): lax.all_to_all(values, ('dp', 'tensor'), split_axis=0, concat_axis=0, til...]
    ppermute x0 -> x33, starting transfers between devices: none -> 35.7 us  [the longest x28 20 us: spread(): lax.ppermute(blocks[s], 'dp', [(i, i ^ s) for i in range(devices)])]
    dot_general x26 -> x12, matrix products: 50.2 us -> 15.1 us  [mm(): lax.dot_general(left, right, ((contract[:1], contract[1:]), ((), ())), pr...]
    pallas_call x0 -> x2, Pallas kernels: none -> 24.2 us  [the longest x1 17.1 us: run_expert(): pl.pallas_call(expert_kernel, grid=(4,), in_specs=[pl.BlockSpec(memory_sp...]
    unnamed x177 -> x164, local copies, waits for them, and re-layouts: 21.9 us -> 34.3 us
  transfers between devices with their start and end apart: 22 -> 50, of which waited for: 12 -> 32; matrix products, arithmetic and copies ran while one was open for 23% -> 21% of each run, Pallas kernels for 0% -> 2%
where the time goes in v2:
time: 430 us; the launch traced here: 429 us
  waiting for transfers between devices  210 us (49%)
  starting transfers between devices  72.6 us (17%)
  local copies, waits for them, and re-layouts  52.5 us (12%)
  other arithmetic  29.6 us (7%)
  Pallas kernels  24.2 us (6%)
  matrix products  22 us (5%)
  between operations  17.3 us (4%)
    ppermute x28, waiting for transfers between devices, spread(): lax.ppermute(blocks[s], 'dp', [(i, i ^ s) for i in range(devices)])  115 us
    ppermute x11, waiting for transfers between devices, swap_tensor(): return lax.ppermute(values, 'tensor', [(0, 1), (1, 0)])  51.6 us
    unnamed x164, local copies, waits for them, and re-layouts  34.3 us
    ppermute x5, waiting for transfers between devices, cross(): return lax.ppermute(values, 'dp', [(i, i ^ near) for i in range(devices)])  25.1 us
    ppermute x28, starting transfers between devices, spread(): lax.ppermute(blocks[s], 'dp', [(i, i ^ s) for i in range(devices)])  20 us
    pallas_call x1, Pallas kernels, run_expert(): pl.pallas_call(expert_kernel, grid=(4,), in_specs=[pl.BlockSpec(memory_sp...  17.1 us
    ppermute x5, starting transfers between devices, cross(): return lax.ppermute(values, 'dp', [(i, i ^ near) for i in range(devices)])  15.7 us
    ppermute x11, starting transfers between devices, swap_tensor(): return lax.ppermute(values, 'tensor', [(0, 1), (1, 0)])  15.2 us
  transfers between devices with their start and end apart: 50, of which 32 were waited for; matrix products, arithmetic and copies ran while one was open for 21% of the time, Pallas kernels for 2%

profile of v2, /device:TPU:0, one launch (start us, length us, event | category | flops | bytes accessed | tf_op | source)
XLA Modules:
  0.0 428.7 jit_solution(3759776035568999374)
XLA Ops:
  7.2 4.1 collective-permute-start.2
  11.4 1.7 collective-permute-start
  13.1 1.8 compare_select_fusion
  23.5 3.1 pad_maximum_fusion
  33.9 6.1 %all-to-all-start = ((bf16[32,64,256]{2,1,0:T(8,128)(2,1)}), bf16[32,64,256]{2,1,0:T(8,128)(2,1)S(1)}, u32[]{:S(2)}, u32[]{:S(2)}) async-start(bf16[32,64,256]{2,1,0:T(8,128)(2,1)} %param.24), calls=%async_computation | async-start | bytes 2097152 | tf_op jit(solution)/shard_map/all_to_all | solution.py:310
  44.5 1.8 collective-permute-start.13
  46.2 8.0 %collective-permute-done.1 = bf16[256,1024]{1,0:T(8,128)(2,1)} collective-permute-done((bf16[256,1024]{1,0:T(8,128)(2,1)S(1)}, bf16[256,1024]{1,0:T(8,128)(2,1)}, u32[]{:S(2)}, u32[]{:S(2)}) %collective-permute-start.1) | collective-permute-done | bytes 524320 | tf_op jit(solution)/shard_map/ppermute | solution.py:51
  56.4 2.3 collective-permute-start.3
  58.7 9.2 %collective-permute-done.13 = bf16[512,512]{1,0:T(8,128)(2,1)S(1)} collective-permute-done((bf16[512,512]{1,0:T(8,128)(2,1)}, bf16[512,512]{1,0:T(8,128)(2,1)S(1)}, u32[]{:S(2)}, u32[]{:S(2)}) %collective-permute-start.13) | collective-permute-done | bytes 524320 | tf_op jit(solution)/shard_map/ppermute | solution.py:51
  68.0 2.9 convolution_convert_fusion
  70.9 6.7 %collective-permute-done.3 = bf16[256,512]{1,0:T(8,128)(2,1)} collective-permute-done((bf16[256,512]{1,0:T(8,128)(2,1)S(1)}, bf16[256,512]{1,0:T(8,128)(2,1)}, u32[]{:S(2)}, u32[]{:S(2)}) %collective-permute-start.3) | collective-permute-done | bytes 262176 | tf_op jit(solution)/shard_map/ppermute | solution.py:279
  77.6 3.9 all-to-all-start.1
  81.5 3.0 fusion.72
  84.5 1.7 collective-permute-start.15
  88.1 2.5 collective-permute-start.19
  90.6 1.7 constant_dynamic-update-slice_fusion.15
  92.3 16.3 %collective-permute-done.15 = bf16[128,1152]{1,0:T(8,128)(2,1)} collective-permute-done((bf16[128,1152]{1,0:T(8,128)(2,1)}, bf16[128,1152]{1,0:T(8,128)(2,1)}, u32[]{:S(2)}, u32[]{:S(2)}) %collective-permute-start.15) | collective-permute-done | bytes 294944 | tf_op jit(solution)/shard_map/ppermute | solution.py:283
  108.6 1.7 constant_dynamic-update-slice_fusion.14
  110.3 5.7 %collective-permute-done.16 = bf16[128,1152]{1,0:T(8,128)(2,1)S(1)} collective-permute-done((bf16[128,1152]{1,0:T(8,128)(2,1)}, bf16[128,1152]{1,0:T(8,128)(2,1)S(1)}, u32[]{:S(2)}, u32[]{:S(2)}) %collective-permute-start.16) | collective-permute-done | bytes 294944 | tf_op jit(solution)/shard_map/ppermute | solution.py:283
  117.8 4.8 %collective-permute-done.17 = bf16[128,1152]{1,0:T(8,128)(2,1)S(1)} collective-permute-done((bf16[128,1152]{1,0:T(8,128)(2,1)}, bf16[128,1152]{1,0:T(8,128)(2,1)S(1)}, u32[]{:S(2)}, u32[]{:S(2)}) %collective-permute-start.17) | collective-permute-done | bytes 294944 | tf_op jit(solution)/shard_map/ppermute | solution.py:283
  123.4 5.6 %collective-permute-done.18 = bf16[128,1152]{1,0:T(8,128)(2,1)S(1)} collective-permute-done((bf16[128,1152]{1,0:T(8,128)(2,1)}, bf16[128,1152]{1,0:T(8,128)(2,1)S(1)}, u32[]{:S(2)}, u32[]{:S(2)}) %collective-permute-start.18) | collective-permute-done | bytes 294944 | tf_op jit(solution)/shard_map/ppermute | solution.py:283
  132.9 1.7 collective-permute-start.5
  134.6 3.5 collective-permute-done.19
  139.4 4.2 collective-permute-done.20
  147.2 2.5 collective-permute-done.6
  150.4 4.7 %collective-permute-done.7 = bf16[128,1024]{1,0:T(8,128)(2,1)S(1)} collective-permute-done((bf16[128,1024]{1,0:T(8,128)(2,1)S(1)}, bf16[128,1024]{1,0:T(8,128)(2,1)S(1)}, u32[]{:S(2)}, u32[]{:S(2)}) %collective-permute-start.7) | collective-permute-done | bytes 262176 | tf_op jit(solution)/shard_map/ppermute | solution.py:283
  158.5 6.1 %collective-permute-done.10 = bf16[128,1024]{1,0:T(8,128)(2,1)S(1)} collective-permute-done((bf16[128,1024]{1,0:T(8,128)(2,1)S(1)}, bf16[128,1024]{1,0:T(8,128)(2,1)S(1)}, u32[]{:S(2)}, u32[]{:S(2)}) %collective-permute-start.10) | collective-permute-done | bytes 262176 | tf_op jit(solution)/shard_map/ppermute | solution.py:283
  165.4 3.7 collective-permute-done.11
  169.8 17.1 %expert_rows.1 = (bf16[1024,1024]{1,0:T(8,128)(2,1)}, bf16[1024,1024]{1,0:T(8,128)(2,1)}, bf16[1024,512]{1,0:T(8,128)(2,1)S(1)}, bf16[1024,512]{1,0:T(8,128)(2,1...) custom-call(s32[1]{0:T(128)} %bitcast.15.expert_ref, ...), custom_call_target="tpu_custom_call" | custom-call | flops 6442450944 | bytes 16777216 | tf_op jit(solution)/shard_map/expert_rows/pallas_call | solution.py:150
  186.9 3.6 fusion.76
  194.6 1.7 collective-permute-start.36
  197.9 2.6 collective-permute-done.32
  202.2 2.2 collective-permute-done.33
  207.7 6.4 %collective-permute-done.36 = bf16[128,1024]{1,0:T(8,128)(2,1)S(1)} collective-permute-done((bf16[128,1024]{1,0:T(8,128)(2,1)S(1)}, bf16[128,1024]{1,0:T(8,128)(2,1)S(1)}, u32[]{:S(2)}, u32[]{:S(2)}) %collective-permute-start.36) | collective-permute-done | bytes 262176 | tf_op jit(solution)/shard_map/ppermute | solution.py:283
  214.8 4.4 %collective-permute-done.37 = bf16[128,1024]{1,0:T(8,128)(2,1)S(1)} collective-permute-done((bf16[128,1024]{1,0:T(8,128)(2,1)S(1)}, bf16[128,1024]{1,0:T(8,128)(2,1)S(1)}, u32[]{:S(2)}, u32[]{:S(2)}) %collective-permute-start.37) | collective-permute-done | bytes 262176 | tf_op jit(solution)/shard_map/ppermute | solution.py:283
  219.9 2.9 fusion.81
  225.2 7.0 %collective-permute-done.39 = bf16[256,512]{1,0:T(8,128)(2,1)S(1)} collective-permute-done((bf16[256,512]{1,0:T(8,128)(2,1)S(1)}, bf16[256,512]{1,0:T(8,128)(2,1)S(1)}, u32[]{:S(2)}, u32[]{:S(2)}) %collective-permute-start.39) | collective-permute-done | bytes 262176 | tf_op jit(solution)/shard_map/ppermute | solution.py:51
  232.3 2.6 collective-permute-start.40
  234.9 7.1 %expert_grads.1 = (bf16[16,2,3,64,256]{4,3,2,1,0:T(8,128)(2,1)}, f32[32,1024]{1,0:T(8,128)S(1)}) custom-call(bf16[1024,1024]{1,0:T(8,128)(2,1)} %constant_dynamic-update-slice_fusion.rows_ref, bf16[1024,1024]{1,0:T(8,128)(2,1)} %get-tuple-element.30.slot_grad_ref, bf16[1024,512]{1,0:T(8,128)(2,1)S(1)} %get-tuple-element.31.hidden_ref, ...), custom_call_target="tpu_custom_call" | custom-call | flops 3221225472 | bytes 12582912 | tf_op jit(solution)/shard_map/expert_grads/pallas_call | solution.py:214
  242.1 1.7 collective-permute-start.43
  243.8 1.8 collective-permute-done.40
  248.6 3.7 all-to-all-start.2
  252.6 4.3 %collective-permute-done.41 = bf16[256,512]{1,0:T(8,128)(2,1)} collective-permute-done((bf16[256,512]{1,0:T(8,128)(2,1)}, bf16[256,512]{1,0:T(8,128)(2,1)}, u32[]{:S(2)}, u32[]{:S(2)}) %collective-permute-start.41) | collective-permute-done | bytes 262176 | tf_op jit(solution)/shard_map/ppermute | solution.py:51
  260.9 1.8 copy.70
  269.2 2.7 collective-permute-start.42
  277.3 17.9 %collective-permute-done.42 = bf16[256,1024]{1,0:T(8,128)(2,1)S(1)} collective-permute-done((bf16[256,1024]{1,0:T(8,128)(2,1)S(1)}, bf16[256,1024]{1,0:T(8,128)(2,1)S(1)}, u32[]{:S(2)}, u32[]{:S(2)}) %collective-permute-start.42) | collective-permute-done | bytes 524320 | tf_op jit(solution)/shard_map/ppermute | solution.py:51
  296.5 5.6 %copy.87 = bf16[1024,1664]{1,0:T(8,128)(2,1)} copy(bf16[1024,1664]{0,1:T(8,128)(2,1)} %pad_dynamic-update-slice_fusion) | data formatting | bytes 6815744
  302.1 1.7 fusion.74
  304.0 1.8 collective-permute-start.23
  305.8 1.7 collective-permute-start.25
  307.6 6.9 %collective-permute-done.22 = bf16[128,1024]{1,0:T(8,128)(2,1)S(1)} collective-permute-done((bf16[128,1024]{1,0:T(8,128)(2,1)S(1)}, bf16[128,1024]{1,0:T(8,128)(2,1)S(1)}, u32[]{:S(2)}, u32[]{:S(2)}) %collective-permute-start.22) | collective-permute-done | bytes 262176 | tf_op jit(solution)/shard_map/ppermute | solution.py:283
  314.5 6.1 %collective-permute-done.23 = bf16[128,1024]{1,0:T(8,128)(2,1)S(1)} collective-permute-done((bf16[128,1024]{1,0:T(8,128)(2,1)S(1)}, bf16[128,1024]{1,0:T(8,128)(2,1)S(1)}, u32[]{:S(2)}, u32[]{:S(2)}) %collective-permute-start.23) | collective-permute-done | bytes 262176 | tf_op jit(solution)/shard_map/ppermute | solution.py:283
  320.7 7.6 %collective-permute-done.25 = bf16[128,1024]{1,0:T(8,128)(2,1)S(1)} collective-permute-done((bf16[128,1024]{1,0:T(8,128)(2,1)S(1)}, bf16[128,1024]{1,0:T(8,128)(2,1)S(1)}, u32[]{:S(2)}, u32[]{:S(2)}) %collective-permute-start.25) | collective-permute-done | bytes 262176 | tf_op jit(solution)/shard_map/ppermute | solution.py:283
  328.3 8.2 %collective-permute-done.26 = bf16[128,1024]{1,0:T(8,128)(2,1)S(1)} collective-permute-done((bf16[128,1024]{1,0:T(8,128)(2,1)S(1)}, bf16[128,1024]{1,0:T(8,128)(2,1)S(1)}, u32[]{:S(2)}, u32[]{:S(2)}) %collective-permute-start.26) | collective-permute-done | bytes 262176 | tf_op jit(solution)/shard_map/ppermute | solution.py:283
  336.5 12.4 %collective-permute-done.27 = bf16[128,1024]{1,0:T(8,128)(2,1)S(1)} collective-permute-done((bf16[128,1024]{1,0:T(8,128)(2,1)S(1)}, bf16[128,1024]{1,0:T(8,128)(2,1)S(1)}, u32[]{:S(2)}, u32[]{:S(2)}) %collective-permute-start.27) | collective-permute-done | bytes 262176 | tf_op jit(solution)/shard_map/ppermute | solution.py:283
  350.8 2.1 collective-permute-start.28
  352.8 5.1 %collective-permute-done.29 = bf16[256,512]{1,0:T(8,128)(2,1)S(1)} collective-permute-done((bf16[256,512]{1,0:T(8,128)(2,1)S(1)}, bf16[256,512]{1,0:T(8,128)(2,1)S(1)}, u32[]{:S(2)}, u32[]{:S(2)}) %collective-permute-start.29) | collective-permute-done | bytes 262176 | tf_op jit(solution)/shard_map/ppermute | solution.py:51
  358.0 6.6 %collective-permute-start.30 = (bf16[256,512]{1,0:T(8,128)(2,1)S(1)}, bf16[256,512]{1,0:T(8,128)(2,1)S(1)}, u32[]{:S(2)}, u32[]{:S(2)}) collective-permute-start(bf16[256,512]{1,0:T(8,128)(2,1)S(1)} %add_convert_fusion.3), channel_id=1, source_target_pairs={{0,16},{2,18},{4,20},{6,22},{8,24},{10,26},{12,28},{14,30},{16,0},... | collective-permute-start | bytes 786440 | tf_op jit(solution)/shard_map/ppermute | solution.py:279
  364.8 16.7 %collective-permute-done.30 = bf16[256,512]{1,0:T(8,128)(2,1)S(1)} collective-permute-done((bf16[256,512]{1,0:T(8,128)(2,1)S(1)}, bf16[256,512]{1,0:T(8,128)(2,1)S(1)}, u32[]{:S(2)}, u32[]{:S(2)}) %collective-permute-start.30) | collective-permute-done | bytes 262176 | tf_op jit(solution)/shard_map/ppermute | solution.py:279
  382.8 3.6 all-to-all-start.3
  387.8 13.1 %all-to-all-done.3 = bf16[16,16,1024]{2,1,0:T(8,128)(2,1)S(1)} async-done(((bf16[16,16,1024]{2,1,0:T(8,128)(2,1)}), bf16[16,16,1024]{2,1,0:T(8,128)(2,1)S(1)}, u32[]{:S(2)}, u32[]{:S(2)}) %all-to-all-start.3) | async-done | bytes 524320 | tf_op jit(solution)/shard_map/all_to_all | solution.py:569
  402.4 4.1 all-to-all-start.4
  410.7 4.8 %convert_bitcast_fusion = (f32[32,256,64]{1,2,0:T(8,128)}, f32[32,64,256]{2,1,0:T(8,128)}, f32[32,64,256]{2,1,0:T(8,128)}) fusion(bf16[32,3,64,256]{3,2,1,0:T(8,128)(2,1)} %all-to-all-done.2), kind=kLoop, calls=%fused_computation.3 | loop fusion | flops 1572864 | bytes 9437184 | tf_op jit(solution)/shard_map/convert_element_type | solution.py:564
  415.5 5.5 %all-to-all-done.4 = bf16[16,16,1024]{2,1,0:T(8,128)(2,1)S(1)} async-done(((bf16[16,16,1024]{2,1,0:T(8,128)(2,1)}), bf16[16,16,1024]{2,1,0:T(8,128)(2,1)S(1)}, u32[]{:S(2)}, u32[]{:S(2)}) %all-to-all-start.4) | async-done | bytes 524320 | tf_op jit(solution)/shard_map/all_to_all | solution.py:573
  (314 shorter events, 85.4 us)
Async XLA Ops:
  7.2 25.9 %copy-start = (bf16[512,1024]{1,0:T(8,128)(2,1)S(1)}, bf16[512,1024]{1,0:T(8,128)(2,1)}, u32[]{:S(2)}) copy-start(bf16[512,1024]{1,0:T(8,128)(2,1)} %param.22) | copy-start | bytes 3145732
  7.2 19.5 %collective-permute-start.2 = (s32[8,256]{1,0:T(8,128)}, s32[8,256]{1,0:T(8,128)S(1)}, u32[]{:S(2)}, u32[]{:S(2)}) collective-permute-start(s32[8,256]{1,0:T(8,128)} %bitcast.167), channel_id=1, source_target_pairs={{0,16},{2,18},{4,20},{6,22},{8,24},{10,26},{12,28},{14,30},{16,0},... | collective-permute-start | bytes 24584 | tf_op jit(solution)/shard_map/ppermute | solution.py:279
  11.3 22.6 %collective-permute-start.12 = (bf16[256,512]{1,0:T(8,128)(2,1)}, bf16[256,512]{1,0:T(8,128)(2,1)}, u32[]{:S(2)}, u32[]{:S(2)}) collective-permute-start(bf16[256,512]{1,0:T(8,128)(2,1)} %param.16), channel_id=1, source_target_pairs={{0,16},{2,18},{4,20},{6,22},{8,24},{10,26},{12,28},{14,30},{16,0},... | collective-permute-start | bytes 786440 | tf_op jit(solution)/shard_map/ppermute | solution.py:279
  11.4 15.8 %collective-permute-start = (bf16[256,512]{1,0:T(8,128)(2,1)}, bf16[256,512]{1,0:T(8,128)(2,1)}, u32[]{:S(2)}, u32[]{:S(2)}) collective-permute-start(bf16[256,512]{1,0:T(8,128)(2,1)} %param.15), channel_id=1, source_target_pairs={{0,1},{1,0},{2,3},{3,2},{4,5},{5,4},{6,7},{7,6},{8,9},{9,8},{10,11... | collective-permute-start | bytes 786440 | tf_op jit(solution)/shard_map/ppermute | solution.py:51
  28.3 25.9 %copy-start.16 = (bf16[256,512]{1,0:T(8,128)(2,1)}, bf16[256,512]{1,0:T(8,128)(2,1)S(1)}, u32[]{:S(2)}) copy-start(bf16[256,512]{1,0:T(8,128)(2,1)S(1)} %get-tuple-element.153) | copy-start | bytes 786436
  33.5 20.6 %collective-permute-start.1 = (bf16[256,1024]{1,0:T(8,128)(2,1)S(1)}, bf16[256,1024]{1,0:T(8,128)(2,1)}, u32[]{:S(2)}, u32[]{:S(2)}) collective-permute-start(bf16[256,1024]{1,0:T(8,128)(2,1)S(1)} %convolution_convert_fusion.6), channel_id=1, source_target_pairs={{0,1},{1,0},{2,3},{3,2},{4,5},{5,4},{6,7},{7,6},{8,9},{9,8},{10,11... | collective-permute-start | bytes 1572872 | tf_op jit(solution)/shard_map/ppermute | solution.py:51
  33.9 43.7 %all-to-all-start = ((bf16[32,64,256]{2,1,0:T(8,128)(2,1)}), bf16[32,64,256]{2,1,0:T(8,128)(2,1)S(1)}, u32[]{:S(2)}, u32[]{:S(2)}) async-start(bf16[32,64,256]{2,1,0:T(8,128)(2,1)} %param.24), calls=%async_computation | async-start | bytes 2097152 | tf_op jit(solution)/shard_map/all_to_all | solution.py:310
  42.5 13.7 %copy-start.46 = (f32[1024]{0:T(1024)S(1)}, f32[1024]{0:T(1024)}, u32[]{:S(2)}) copy-start(f32[1024]{0:T(1024)} %param.18) | copy-start | bytes 12292
  44.4 23.4 %copy-start.25 = (bf16[512,512]{1,0:T(8,128)(2,1)S(1)}, bf16[512,512]{1,0:T(8,128)(2,1)}, u32[]{:S(2)}) copy-start(bf16[512,512]{1,0:T(8,128)(2,1)} %constant_dynamic-update-slice_fusion.7) | copy-start | bytes 1572868
  44.5 23.4 %collective-permute-start.13 = (bf16[512,512]{1,0:T(8,128)(2,1)}, bf16[512,512]{1,0:T(8,128)(2,1)S(1)}, u32[]{:S(2)}, u32[]{:S(2)}) collective-permute-start(bf16[512,512]{1,0:T(8,128)(2,1)} %constant_dynamic-update-slice_fusion.7), channel_id=1, source_target_pairs={{0,1},{1,0},{2,3},{3,2},{4,5},{5,4},{6,7},{7,6},{8,9},{9,8},{10,11... | collective-permute-start | bytes 1572872 | tf_op jit(solution)/shard_map/ppermute | solution.py:51
  55.5 12.4 %copy-start.10 = (f32[256,1024]{1,0:T(8,128)}, f32[256,1024]{1,0:T(8,128)S(1)}, u32[]{:S(2)}) copy-start(f32[256,1024]{1,0:T(8,128)S(1)} %get-tuple-element.98) | copy-start | bytes 3145732
  56.4 21.2 %collective-permute-start.3 = (bf16[256,512]{1,0:T(8,128)(2,1)S(1)}, bf16[256,512]{1,0:T(8,128)(2,1)}, u32[]{:S(2)}, u32[]{:S(2)}) collective-permute-start(bf16[256,512]{1,0:T(8,128)(2,1)S(1)} %constant_dynamic-slice_fusion), channel_id=1, source_target_pairs={{0,16},{2,18},{4,20},{6,22},{8,24},{10,26},{12,28},{14,30},{16,0},... | collective-permute-start | bytes 786440 | tf_op jit(solution)/shard_map/ppermute | solution.py:279
  77.6 92.2 %all-to-all-start.1 = ((bf16[32,2,64,256]{3,2,1,0:T(8,128)(2,1)}), bf16[32,2,64,256]{3,2,1,0:T(8,128)(2,1)}, u32[]{:S(2)}, u32[]{:S(2)}) async-start(bf16[32,2,64,256]{3,2,1,0:T(8,128)(2,1)} %pad_maximum_fusion), calls=%async_computation.1 | async-start | bytes 4194304 | tf_op jit(solution)/shard_map/all_to_all | solution.py:310
  84.5 3.6 collective-permute-start.14
  84.5 24.0 %collective-permute-start.15 = (bf16[128,1152]{1,0:T(8,128)(2,1)}, bf16[128,1152]{1,0:T(8,128)(2,1)}, u32[]{:S(2)}, u32[]{:S(2)}) collective-permute-start(bf16[128,1152]{1,0:T(8,128)(2,1)} %get-tuple-element.107), channel_id=1, source_target_pairs={{0,4},{2,6},{4,0},{6,2},{8,12},{10,14},{12,8},{14,10},{16,20},{18,... | collective-permute-start | bytes 884744 | tf_op jit(solution)/shard_map/ppermute | solution.py:283
  86.2 29.8 %collective-permute-start.16 = (bf16[128,1152]{1,0:T(8,128)(2,1)}, bf16[128,1152]{1,0:T(8,128)(2,1)S(1)}, u32[]{:S(2)}, u32[]{:S(2)}) collective-permute-start(bf16[128,1152]{1,0:T(8,128)(2,1)} %get-tuple-element.106), channel_id=1, source_target_pairs={{0,6},{2,4},{4,2},{6,0},{8,14},{10,12},{12,10},{14,8},{16,22},{18,... | collective-permute-start | bytes 884744 | tf_op jit(solution)/shard_map/ppermute | solution.py:283
  86.4 36.3 %collective-permute-start.17 = (bf16[128,1152]{1,0:T(8,128)(2,1)}, bf16[128,1152]{1,0:T(8,128)(2,1)S(1)}, u32[]{:S(2)}, u32[]{:S(2)}) collective-permute-start(bf16[128,1152]{1,0:T(8,128)(2,1)} %get-tuple-element.105), channel_id=1, source_target_pairs={{0,8},{2,10},{4,12},{6,14},{8,0},{10,2},{12,4},{14,6},{16,24},{18,... | collective-permute-start | bytes 884744 | tf_op jit(solution)/shard_map/ppermute | solution.py:283
  87.9 41.1 %collective-permute-start.18 = (bf16[128,1152]{1,0:T(8,128)(2,1)}, bf16[128,1152]{1,0:T(8,128)(2,1)S(1)}, u32[]{:S(2)}, u32[]{:S(2)}) collective-permute-start(bf16[128,1152]{1,0:T(8,128)(2,1)} %get-tuple-element.104), channel_id=1, source_target_pairs={{0,10},{2,8},{4,14},{6,12},{8,2},{10,0},{12,6},{14,4},{16,26},{18,... | collective-permute-start | bytes 884744 | tf_op jit(solution)/shard_map/ppermute | solution.py:283
  88.1 50.0 %collective-permute-start.19 = (bf16[128,1152]{1,0:T(8,128)(2,1)}, bf16[128,1152]{1,0:T(8,128)(2,1)S(1)}, u32[]{:S(2)}, u32[]{:S(2)}) collective-permute-start(bf16[128,1152]{1,0:T(8,128)(2,1)} %get-tuple-element.103), channel_id=1, source_target_pairs={{0,12},{2,14},{4,8},{6,10},{8,4},{10,6},{12,0},{14,2},{16,28},{18,... | collective-permute-start | bytes 884744 | tf_op jit(solution)/shard_map/ppermute | solution.py:283
  108.6 35.0 %collective-permute-start.20 = (bf16[128,1152]{1,0:T(8,128)(2,1)}, bf16[128,1152]{1,0:T(8,128)(2,1)S(1)}, u32[]{:S(2)}, u32[]{:S(2)}) collective-permute-start(bf16[128,1152]{1,0:T(8,128)(2,1)} %get-tuple-element.102), channel_id=1, source_target_pairs={{0,14},{2,12},{4,10},{6,8},{8,6},{10,4},{12,2},{14,0},{16,30},{18,... | collective-permute-start | bytes 884744 | tf_op jit(solution)/shard_map/ppermute | solution.py:283
  116.0 13.8 %collective-permute-start.4 = (bf16[256,512]{1,0:T(8,128)(2,1)}, bf16[256,512]{1,0:T(8,128)(2,1)S(1)}, u32[]{:S(2)}, u32[]{:S(2)}) collective-permute-start(bf16[256,512]{1,0:T(8,128)(2,1)} %collective-permute-done.3), channel_id=1, source_target_pairs={{0,1},{1,0},{2,3},{3,2},{4,5},{5,4},{6,7},{7,6},{8,9},{9,8},{10,11... | collective-permute-start | bytes 786440 | tf_op jit(solution)/shard_map/ppermute | solution.py:51
  132.9 13.1 %collective-permute-start.5 = (bf16[128,1024]{1,0:T(8,128)(2,1)S(1)}, bf16[128,1024]{1,0:T(8,128)(2,1)S(1)}, u32[]{:S(2)}, u32[]{:S(2)}) collective-permute-start(bf16[128,1024]{1,0:T(8,128)(2,1)S(1)} %get-tuple-element.136), channel_id=1, source_target_pairs={{0,2},{2,0},{4,6},{6,4},{8,10},{10,8},{12,14},{14,12},{16,18},{18,... | collective-permute-start | bytes 786440 | tf_op jit(solution)/shard_map/ppermute | solution.py:283
  138.8 10.8 %collective-permute-start.6 = (bf16[128,1024]{1,0:T(8,128)(2,1)S(1)}, bf16[128,1024]{1,0:T(8,128)(2,1)S(1)}, u32[]{:S(2)}, u32[]{:S(2)}) collective-permute-start(bf16[128,1024]{1,0:T(8,128)(2,1)S(1)} %get-tuple-element.135), channel_id=1, source_target_pairs={{0,4},{2,6},{4,0},{6,2},{8,12},{10,14},{12,8},{14,10},{16,20},{18,... | collective-permute-start | bytes 786440 | tf_op jit(solution)/shard_map/ppermute | solution.py:283
  139.4 30.4 %copy-start.1 = (bf16[1024,32]{0,1:T(8,128)(2,1)S(1)}, bf16[1024,32]{0,1:T(8,128)(2,1)}, u32[]{:S(2)}) copy-start(bf16[1024,32]{0,1:T(8,128)(2,1)} %param.23) | copy-start | bytes 196612
  139.4 15.7 %collective-permute-start.7 = (bf16[128,1024]{1,0:T(8,128)(2,1)S(1)}, bf16[128,1024]{1,0:T(8,128)(2,1)S(1)}, u32[]{:S(2)}, u32[]{:S(2)}) collective-permute-start(bf16[128,1024]{1,0:T(8,128)(2,1)S(1)} %get-tuple-element.134), channel_id=1, source_target_pairs={{0,6},{2,4},{4,2},{6,0},{8,14},{10,12},{12,10},{14,8},{16,22},{18,... | collective-permute-start | bytes 786440 | tf_op jit(solution)/shard_map/ppermute | solution.py:283
  144.3 11.5 %collective-permute-start.8 = (bf16[128,1024]{1,0:T(8,128)(2,1)S(1)}, bf16[128,1024]{1,0:T(8,128)(2,1)S(1)}, u32[]{:S(2)}, u32[]{:S(2)}) collective-permute-start(bf16[128,1024]{1,0:T(8,128)(2,1)S(1)} %get-tuple-element.133), channel_id=1, source_target_pairs={{0,8},{2,10},{4,12},{6,14},{8,0},{10,2},{12,4},{14,6},{16,24},{18,... | collective-permute-start | bytes 786440 | tf_op jit(solution)/shard_map/ppermute | solution.py:283
  145.1 12.7 %collective-permute-start.9 = (bf16[128,1024]{1,0:T(8,128)(2,1)S(1)}, bf16[128,1024]{1,0:T(8,128)(2,1)S(1)}, u32[]{:S(2)}, u32[]{:S(2)}) collective-permute-start(bf16[128,1024]{1,0:T(8,128)(2,1)S(1)} %get-tuple-element.132), channel_id=1, source_target_pairs={{0,10},{2,8},{4,14},{6,12},{8,2},{10,0},{12,6},{14,4},{16,26},{18,... | collective-permute-start | bytes 786440 | tf_op jit(solution)/shard_map/ppermute | solution.py:283
  146.0 18.7 %collective-permute-start.10 = (bf16[128,1024]{1,0:T(8,128)(2,1)S(1)}, bf16[128,1024]{1,0:T(8,128)(2,1)S(1)}, u32[]{:S(2)}, u32[]{:S(2)}) collective-permute-start(bf16[128,1024]{1,0:T(8,128)(2,1)S(1)} %get-tuple-element.131), channel_id=1, source_target_pairs={{0,12},{2,14},{4,8},{6,10},{8,4},{10,6},{12,0},{14,2},{16,28},{18,... | collective-permute-start | bytes 786440 | tf_op jit(solution)/shard_map/ppermute | solution.py:283
  149.7 19.4 %collective-permute-start.11 = (bf16[128,1024]{1,0:T(8,128)(2,1)S(1)}, bf16[128,1024]{1,0:T(8,128)(2,1)S(1)}, u32[]{:S(2)}, u32[]{:S(2)}) collective-permute-start(bf16[128,1024]{1,0:T(8,128)(2,1)S(1)} %get-tuple-element.130), channel_id=1, source_target_pairs={{0,14},{2,12},{4,10},{6,8},{8,6},{10,4},{12,2},{14,0},{16,30},{18,... | collective-permute-start | bytes 786440 | tf_op jit(solution)/shard_map/ppermute | solution.py:283
  190.6 29.3 %copy-start.31 = (pred[128,8,2,256]{3,1,2,0:T(8,128)(4,1)S(1)}, pred[128,8,2,256]{3,1,2,0:T(8,128)(4,1)}, u32[]{:S(2)}) copy-start(pred[128,8,2,256]{3,1,2,0:T(8,128)(4,1)} %copy.89) | copy-start | bytes 1572868
  190.6 4.0 collective-permute-start.31
  191.1 9.5 %collective-permute-start.32 = (bf16[128,1024]{1,0:T(8,128)(2,1)}, bf16[128,1024]{1,0:T(8,128)(2,1)}, u32[]{:S(2)}, u32[]{:S(2)}) collective-permute-start(bf16[128,1024]{1,0:T(8,128)(2,1)} %get-tuple-element.127), channel_id=1, source_target_pairs={{0,4},{2,6},{4,0},{6,2},{8,12},{10,14},{12,8},{14,10},{16,20},{18,... | collective-permute-start | bytes 786440 | tf_op jit(solution)/shard_map/ppermute | solution.py:283
  192.6 11.9 %collective-permute-start.33 = (bf16[128,1024]{1,0:T(8,128)(2,1)}, bf16[128,1024]{1,0:T(8,128)(2,1)}, u32[]{:S(2)}, u32[]{:S(2)}) collective-permute-start(bf16[128,1024]{1,0:T(8,128)(2,1)} %get-tuple-element.126), channel_id=1, source_target_pairs={{0,6},{2,4},{4,2},{6,0},{8,14},{10,12},{12,10},{14,8},{16,22},{18,... | collective-permute-start | bytes 786440 | tf_op jit(solution)/shard_map/ppermute | solution.py:283
  192.6 13.5 %collective-permute-start.34 = (bf16[128,1024]{1,0:T(8,128)(2,1)}, bf16[128,1024]{1,0:T(8,128)(2,1)S(1)}, u32[]{:S(2)}, u32[]{:S(2)}) collective-permute-start(bf16[128,1024]{1,0:T(8,128)(2,1)} %get-tuple-element.125), channel_id=1, source_target_pairs={{0,8},{2,10},{4,12},{6,14},{8,0},{10,2},{12,4},{14,6},{16,24},{18,... | collective-permute-start | bytes 786440 | tf_op jit(solution)/shard_map/ppermute | solution.py:283
  193.3 13.6 %collective-permute-start.35 = (bf16[128,1024]{1,0:T(8,128)(2,1)}, bf16[128,1024]{1,0:T(8,128)(2,1)S(1)}, u32[]{:S(2)}, u32[]{:S(2)}) collective-permute-start(bf16[128,1024]{1,0:T(8,128)(2,1)} %get-tuple-element.124), channel_id=1, source_target_pairs={{0,10},{2,8},{4,14},{6,12},{8,2},{10,0},{12,6},{14,4},{16,26},{18,... | collective-permute-start | bytes 786440 | tf_op jit(solution)/shard_map/ppermute | solution.py:283
  194.6 19.5 %collective-permute-start.36 = (bf16[128,1024]{1,0:T(8,128)(2,1)S(1)}, bf16[128,1024]{1,0:T(8,128)(2,1)S(1)}, u32[]{:S(2)}, u32[]{:S(2)}) collective-permute-start(bf16[128,1024]{1,0:T(8,128)(2,1)S(1)} %get-tuple-element.123), channel_id=1, source_target_pairs={{0,12},{2,14},{4,8},{6,10},{8,4},{10,6},{12,0},{14,2},{16,28},{18,... | collective-permute-start | bytes 786440 | tf_op jit(solution)/shard_map/ppermute | solution.py:283
  200.5 18.6 %collective-permute-start.37 = (bf16[128,1024]{1,0:T(8,128)(2,1)S(1)}, bf16[128,1024]{1,0:T(8,128)(2,1)S(1)}, u32[]{:S(2)}, u32[]{:S(2)}) collective-permute-start(bf16[128,1024]{1,0:T(8,128)(2,1)S(1)} %get-tuple-element.122), channel_id=1, source_target_pairs={{0,14},{2,12},{4,10},{6,8},{8,6},{10,4},{12,2},{14,0},{16,30},{18,... | collective-permute-start | bytes 786440 | tf_op jit(solution)/shard_map/ppermute | solution.py:283
  223.0 9.2 %collective-permute-start.39 = (bf16[256,512]{1,0:T(8,128)(2,1)S(1)}, bf16[256,512]{1,0:T(8,128)(2,1)S(1)}, u32[]{:S(2)}, u32[]{:S(2)}) collective-permute-start(bf16[256,512]{1,0:T(8,128)(2,1)S(1)} %dynamic-slice_convert_fusion), channel_id=1, source_target_pairs={{0,1},{1,0},{2,3},{3,2},{4,5},{5,4},{6,7},{7,6},{8,9},{9,8},{10,11... | collective-permute-start | bytes 786440 | tf_op jit(solution)/shard_map/ppermute | solution.py:51
  224.6 19.2 %collective-permute-start.38 = (bf16[256,512]{1,0:T(8,128)(2,1)S(1)}, bf16[256,512]{1,0:T(8,128)(2,1)S(1)}, u32[]{:S(2)}, u32[]{:S(2)}) collective-permute-start(bf16[256,512]{1,0:T(8,128)(2,1)S(1)} %dynamic-slice_convert_fusion.1), channel_id=1, source_target_pairs={{0,1},{1,0},{2,3},{3,2},{4,5},{5,4},{6,7},{7,6},{8,9},{9,8},{10,11... | collective-permute-start | bytes 786440 | tf_op jit(solution)/shard_map/ppermute | solution.py:51
  232.3 13.3 %collective-permute-start.40 = (bf16[256,512]{1,0:T(8,128)(2,1)S(1)}, bf16[256,512]{1,0:T(8,128)(2,1)S(1)}, u32[]{:S(2)}, u32[]{:S(2)}) collective-permute-start(bf16[256,512]{1,0:T(8,128)(2,1)S(1)} %add_convert_fusion.1), channel_id=1, source_target_pairs={{0,16},{2,18},{4,20},{6,22},{8,24},{10,26},{12,28},{14,30},{16,0},... | collective-permute-start | bytes 786440 | tf_op jit(solution)/shard_map/ppermute | solution.py:279
  234.9 13.0 %copy-start.49 = (f32[4,2,256]{2,1,0:T(2,128)S(1)}, f32[4,2,256]{2,1,0:T(2,128)}, u32[]{:S(2)}) copy-start(f32[4,2,256]{2,1,0:T(2,128)} %copy-done.48) | copy-start | bytes 24580
  234.9 13.0 %copy-start.51 = (f32[4,2,256]{2,1,0:T(2,128)S(1)}, f32[4,2,256]{2,1,0:T(2,128)}, u32[]{:S(2)}) copy-start(f32[4,2,256]{2,1,0:T(2,128)} %copy-done.50) | copy-start | bytes 24580
  242.1 5.9 %collective-permute-start.43 = (bf16[32,1024]{1,0:T(8,128)(2,1)S(1)}, bf16[32,1024]{1,0:T(8,128)(2,1)S(1)}, u32[]{:S(2)}, u32[]{:S(2)}) collective-permute-start(bf16[32,1024]{1,0:T(8,128)(2,1)S(1)} %convert_element_type.246), channel_id=1, source_target_pairs={{0,1},{1,0},{2,3},{3,2},{4,5},{5,4},{6,7},{7,6},{8,9},{9,8},{10,11... | collective-permute-start | bytes 196616 | tf_op jit(solution)/shard_map/ppermute | solution.py:51
  246.4 10.5 %collective-permute-start.41 = (bf16[256,512]{1,0:T(8,128)(2,1)}, bf16[256,512]{1,0:T(8,128)(2,1)}, u32[]{:S(2)}, u32[]{:S(2)}) collective-permute-start(bf16[256,512]{1,0:T(8,128)(2,1)} %add_convert_fusion), channel_id=1, source_target_pairs={{0,1},{1,0},{2,3},{3,2},{4,5},{5,4},{6,7},{7,6},{8,9},{9,8},{10,11... | collective-permute-start | bytes 786440 | tf_op jit(solution)/shard_map/ppermute | solution.py:51
  248.6 134.2 %all-to-all-start.2 = ((bf16[32,3,64,256]{3,2,1,0:T(8,128)(2,1)}), bf16[32,3,64,256]{3,2,1,0:T(8,128)(2,1)}, u32[]{:S(2)}, u32[]{:S(2)}) async-start(bf16[32,3,64,256]{3,2,1,0:T(8,128)(2,1)} %bitcast.136), calls=%async_computation.2 | async-start | bytes 6291456 | tf_op jit(solution)/shard_map/all_to_all | solution.py:330
  252.3 134.2 %reduce-scatter.4.cloned.1.call-start = ((), (), s32[]{:S(2)}) async-start(), calls=%async_computation.6 | async-start | bytes 3620864
  269.2 26.1 %collective-permute-start.42 = (bf16[256,1024]{1,0:T(8,128)(2,1)S(1)}, bf16[256,1024]{1,0:T(8,128)(2,1)S(1)}, u32[]{:S(2)}, u32[]{:S(2)}) collective-permute-start(bf16[256,1024]{1,0:T(8,128)(2,1)S(1)} %fusion.9), channel_id=1, source_target_pairs={{0,1},{1,0},{2,3},{3,2},{4,5},{5,4},{6,7},{7,6},{8,9},{9,8},{10,11... | collective-permute-start | bytes 1572872 | tf_op jit(solution)/shard_map/ppermute | solution.py:51
  276.1 19.6 %copy-start.39 = (bf16[32,1024]{1,0:T(8,128)(2,1)S(1)}, bf16[32,1024]{1,0:T(8,128)(2,1)}, u32[]{:S(2)}) copy-start(bf16[32,1024]{1,0:T(8,128)(2,1)} %add_convert_fusion.6) | copy-start | bytes 196612
  303.9 45.1 %copy-start.32 = (pred[128,8,2,256]{3,1,2,0:T(8,128)(4,1)S(1)}, pred[128,8,2,256]{3,1,2,0:T(8,128)(4,1)}, u32[]{:S(2)}) copy-start(pred[128,8,2,256]{3,1,2,0:T(8,128)(4,1)} %copy.89) | copy-start | bytes 1572868
  303.9 3.6 collective-permute-start.21
  304.0 10.5 %collective-permute-start.22 = (bf16[128,1024]{1,0:T(8,128)(2,1)S(1)}, bf16[128,1024]{1,0:T(8,128)(2,1)S(1)}, u32[]{:S(2)}, u32[]{:S(2)}) collective-permute-start(bf16[128,1024]{1,0:T(8,128)(2,1)S(1)} %get-tuple-element.117), channel_id=1, source_target_pairs={{0,4},{2,6},{4,0},{6,2},{8,12},{10,14},{12,8},{14,10},{16,20},{18,... | collective-permute-start | bytes 786440 | tf_op jit(solution)/shard_map/ppermute | solution.py:283
  304.0 16.6 %collective-permute-start.23 = (bf16[128,1024]{1,0:T(8,128)(2,1)S(1)}, bf16[128,1024]{1,0:T(8,128)(2,1)S(1)}, u32[]{:S(2)}, u32[]{:S(2)}) collective-permute-start(bf16[128,1024]{1,0:T(8,128)(2,1)S(1)} %get-tuple-element.116), channel_id=1, source_target_pairs={{0,6},{2,4},{4,2},{6,0},{8,14},{10,12},{12,10},{14,8},{16,22},{18,... | collective-permute-start | bytes 786440 | tf_op jit(solution)/shard_map/ppermute | solution.py:283
  305.8 14.9 %collective-permute-start.24 = (bf16[128,1024]{1,0:T(8,128)(2,1)S(1)}, bf16[128,1024]{1,0:T(8,128)(2,1)S(1)}, u32[]{:S(2)}, u32[]{:S(2)}) collective-permute-start(bf16[128,1024]{1,0:T(8,128)(2,1)S(1)} %get-tuple-element.115), channel_id=1, source_target_pairs={{0,8},{2,10},{4,12},{6,14},{8,0},{10,2},{12,4},{14,6},{16,24},{18,... | collective-permute-start | bytes 786440 | tf_op jit(solution)/shard_map/ppermute | solution.py:283
  305.8 22.5 %collective-permute-start.25 = (bf16[128,1024]{1,0:T(8,128)(2,1)S(1)}, bf16[128,1024]{1,0:T(8,128)(2,1)S(1)}, u32[]{:S(2)}, u32[]{:S(2)}) collective-permute-start(bf16[128,1024]{1,0:T(8,128)(2,1)S(1)} %get-tuple-element.114), channel_id=1, source_target_pairs={{0,10},{2,8},{4,14},{6,12},{8,2},{10,0},{12,6},{14,4},{16,26},{18,... | collective-permute-start | bytes 786440 | tf_op jit(solution)/shard_map/ppermute | solution.py:283
  307.5 29.0 %collective-permute-start.26 = (bf16[128,1024]{1,0:T(8,128)(2,1)S(1)}, bf16[128,1024]{1,0:T(8,128)(2,1)S(1)}, u32[]{:S(2)}, u32[]{:S(2)}) collective-permute-start(bf16[128,1024]{1,0:T(8,128)(2,1)S(1)} %get-tuple-element.113), channel_id=1, source_target_pairs={{0,12},{2,14},{4,8},{6,10},{8,4},{10,6},{12,0},{14,2},{16,28},{18,... | collective-permute-start | bytes 786440 | tf_op jit(solution)/shard_map/ppermute | solution.py:283
  314.5 34.5 %collective-permute-start.27 = (bf16[128,1024]{1,0:T(8,128)(2,1)S(1)}, bf16[128,1024]{1,0:T(8,128)(2,1)S(1)}, u32[]{:S(2)}, u32[]{:S(2)}) collective-permute-start(bf16[128,1024]{1,0:T(8,128)(2,1)S(1)} %get-tuple-element.112), channel_id=1, source_target_pairs={{0,14},{2,12},{4,10},{6,8},{8,6},{10,4},{12,2},{14,0},{16,30},{18,... | collective-permute-start | bytes 786440 | tf_op jit(solution)/shard_map/ppermute | solution.py:283
  350.5 30.9 %copy-start.12 = (f32[256,1024]{1,0:T(8,128)S(1)}, f32[256,1024]{1,0:T(8,128)}, u32[]{:S(2)}) copy-start(f32[256,1024]{1,0:T(8,128)} %copy-done.10) | copy-start | bytes 3145732
  350.6 7.3 %collective-permute-start.29 = (bf16[256,512]{1,0:T(8,128)(2,1)S(1)}, bf16[256,512]{1,0:T(8,128)(2,1)S(1)}, u32[]{:S(2)}, u32[]{:S(2)}) collective-permute-start(bf16[256,512]{1,0:T(8,128)(2,1)S(1)} %dynamic-slice_convert_fusion.2), channel_id=1, source_target_pairs={{0,1},{1,0},{2,3},{3,2},{4,5},{5,4},{6,7},{7,6},{8,9},{9,8},{10,11... | collective-permute-start | bytes 786440 | tf_op jit(solution)/shard_map/ppermute | solution.py:51
  350.7 31.0 %copy-start.15 = (f32[256,1024]{1,0:T(8,128)S(1)}, f32[256,1024]{1,0:T(8,128)}, u32[]{:S(2)}) copy-start(f32[256,1024]{1,0:T(8,128)} %copy-done.13) | copy-start | bytes 3145732
  350.7 31.0 %copy-start.58 = (f32[256]{0:T(256)S(1)}, f32[256]{0:T(256)}, u32[]{:S(2)}) copy-start(f32[256]{0:T(256)} %get-tuple-element.162) | copy-start | bytes 3076
  350.8 14.0 %collective-permute-start.28 = (bf16[256,512]{1,0:T(8,128)(2,1)S(1)}, bf16[256,512]{1,0:T(8,128)(2,1)S(1)}, u32[]{:S(2)}, u32[]{:S(2)}) collective-permute-start(bf16[256,512]{1,0:T(8,128)(2,1)S(1)} %dynamic-slice_convert_fusion.3), channel_id=1, source_target_pairs={{0,1},{1,0},{2,3},{3,2},{4,5},{5,4},{6,7},{7,6},{8,9},{9,8},{10,11... | collective-permute-start | bytes 786440 | tf_op jit(solution)/shard_map/ppermute | solution.py:51
  358.0 23.5 %collective-permute-start.30 = (bf16[256,512]{1,0:T(8,128)(2,1)S(1)}, bf16[256,512]{1,0:T(8,128)(2,1)S(1)}, u32[]{:S(2)}, u32[]{:S(2)}) collective-permute-start(bf16[256,512]{1,0:T(8,128)(2,1)S(1)} %add_convert_fusion.3), channel_id=1, source_target_pairs={{0,16},{2,18},{4,20},{6,22},{8,24},{10,26},{12,28},{14,30},{16,0},... | collective-permute-start | bytes 786440 | tf_op jit(solution)/shard_map/ppermute | solution.py:279
  382.8 18.1 %all-to-all-start.3 = ((bf16[16,16,1024]{2,1,0:T(8,128)(2,1)}), bf16[16,16,1024]{2,1,0:T(8,128)(2,1)S(1)}, u32[]{:S(2)}, u32[]{:S(2)}) async-start(bf16[16,16,1024]{2,1,0:T(8,128)(2,1)} %bitcast.41), calls=%async_computation.3 | async-start | bytes 1048576 | tf_op jit(solution)/shard_map/all_to_all | solution.py:569
  402.4 18.6 %all-to-all-start.4 = ((bf16[16,16,1024]{2,1,0:T(8,128)(2,1)}), bf16[16,16,1024]{2,1,0:T(8,128)(2,1)S(1)}, u32[]{:S(2)}, u32[]{:S(2)}) async-start(bf16[16,16,1024]{2,1,0:T(8,128)(2,1)} %broadcast_select_fusion), calls=%async_computation.4 | async-start | bytes 1048576 | tf_op jit(solution)/shard_map/all_to_all | solution.py:573
  (52 other events, 192.0 us)
Sparse Core Ops, SparseCore 0:
  302.2 77.3 reduce-scatter.3

commit v3 on v2

v3 whole, which is shorter than its diff:
```python
import functools
import math

import jax
import jax.numpy as jnp
from jax import lax
from jax.experimental import pallas as pl
from jax.experimental.pallas import tpu as pltpu
from jax.sharding import PartitionSpec as P

HEAD_DIM = 64


EPSILON = 1e-06
ROPE_BASE = 10000.0
NEGATIVE = -1e30


def swap_tensor(values):
    return lax.ppermute(values, "tensor", [(0, 1), (1, 0)])


def mm(left, right, contract):
    return lax.dot_general(
        left, right, ((contract[:1], contract[1:]), ((), ())), preferred_element_type=jnp.float32
    )


def after(values, *others):
    return lax.optimization_barrier((values,) + others)[0]


def dot(left, right, left_axis=1, right_axis=0):
    return lax.dot_general(
        left,
        right,
        (((left_axis,), (right_axis,)), ((), ())),
        preferred_element_type=jnp.float32,
    )


def params(megabytes):
    return pltpu.CompilerParams(vmem_limit_bytes=megabytes << 20)


def cost(flops, size, transcendentals=0):
    return pl.CostEstimate(
        flops=flops, bytes_accessed=size, transcendentals=transcendentals
    )


SMEM = pl.BlockSpec(memory_space=pltpu.SMEM)
VMEM = pl.BlockSpec(memory_space=pltpu.VMEM)
ANY = pl.BlockSpec(memory_space=pl.ANY)
FULL = 60


def columns_of(plane, width, own):
    half = width // 2
    start = plane * half if own else (1 - plane) * half
    return pl.ds(pl.multiple_of(start, half), half)


def write_blocks(product, columns, out_refs, capacity, which):
    for j, out_ref in enumerate(out_refs):
        out_ref[which * capacity : (which + 1) * capacity, columns] = product[
            j * capacity : (j + 1) * capacity
        ].astype(out_ref.dtype)


def dispatch_cot_kernel(capacity, expert_count, facts_ref, routes_ref, partner_ref, *refs):
    own_ref, cross_ref, away_ref, cross_away_ref, hot_ref = refs[:5]
    out_refs = refs[5:]
    plane, member, live_count = facts_ref[0], facts_ref[1], facts_ref[2]
    tokens = routes_ref.shape[1]
    near = len(out_refs)
    width = 2 * own_ref.shape[1]
    row = lax.broadcasted_iota(jnp.int32, (tokens, tokens), 0)
    column = lax.broadcasted_iota(jnp.int32, (tokens, tokens), 1)
    before = jnp.where(row < column, 1.0, 0.0).astype(jnp.bfloat16)
    live = lax.broadcasted_iota(jnp.int32, (1, tokens), 1) < live_count
    names = lax.broadcasted_iota(jnp.int32, (128, tokens), 0)
    slots = lax.broadcasted_iota(jnp.int32, (near, capacity, tokens), 1)
    ids = lax.broadcasted_iota(jnp.int32, (near, tokens), 0)
    near_experts = 2 * jnp.bitwise_xor(ids, member) + plane
    values = (
        (own_ref[...], away_ref[...]),
        (cross_ref[...], cross_away_ref[...]),
    )
    for which, source in enumerate((routes_ref, partner_ref)):
        picked = names < 0
        counted = ids < 0
        for k in range(source.shape[0]):
            route = source[k : k + 1, :]
            picked = picked | (names == route)
            counted = counted | (near_experts == route)
        counted = counted & live
        place = dot(jnp.where(counted, 1.0, 0.0).astype(jnp.bfloat16), before)
        place = jnp.where(counted, place.astype(jnp.int32), -1)
        hot = jnp.where(place[:, None, :] == slots, 1.0, 0.0).astype(jnp.bfloat16)
        hot = hot.reshape(near * capacity, tokens)
        hot_ref[which] = hot
        own, away = values[which]
        write_blocks(dot(hot, own), columns_of(plane, width, True), out_refs, capacity, which)
        write_blocks(dot(hot, away), columns_of(plane, width, False), out_refs, capacity, which)
        picked = jnp.where(picked, 1.0, 0.0).astype(jnp.bfloat16)
        write_blocks(
            dot(hot, picked, 1, 1), slice(width, width + 128), out_refs, capacity, which
        )


def dispatch_cot(
    facts, routes_t, partner_t, own, crossed, away, cross_away, near, capacity, expert_count
):
    tokens, half = own.shape
    out = jax.ShapeDtypeStruct((2 * capacity, 2 * half + 128), jnp.bfloat16)
    hot = jax.ShapeDtypeStruct((2, near * capacity, tokens), jnp.bfloat16)
    results = pl.pallas_call(
        functools.partial(dispatch_cot_kernel, capacity, expert_count),
        in_specs=[SMEM] + [VMEM] * 6,
        out_specs=[VMEM] * (1 + near),
        out_shape=[hot] + [out] * near,
        compiler_params=params(FULL),
        cost_estimate=cost(8 * near * capacity * tokens * half, 4 << 20),
        name="dispatch_cot",
    )(facts, routes_t, partner_t, own, crossed, away, cross_away)
    return results[0], results[1:]


def dispatch_rows_kernel(capacity, facts_ref, hot_ref, rows_ref, cross_ref, away_ref, *out_refs):
    plane = facts_ref[0]
    width = rows_ref.shape[1]
    write_blocks(dot(hot_ref[0], rows_ref[...]), slice(0, width), out_refs, capacity, 0)
    own, away = columns_of(plane, width, True), columns_of(plane, width, False)
    write_blocks(dot(hot_ref[1], cross_ref[...]), own, out_refs, capacity, 1)
    write_blocks(dot(hot_ref[1], away_ref[...]), away, out_refs, capacity, 1)


def dispatch_rows(facts, hot, rows, crossed, away, near, capacity):
    tokens, width = rows.shape
    out = jax.ShapeDtypeStruct((2 * capacity, width), jnp.bfloat16)
    return pl.pallas_call(
        functools.partial(dispatch_rows_kernel, capacity),
        in_specs=[SMEM] + [VMEM] * 4,
        out_specs=[VMEM] * near,
        out_shape=[out] * near,
        compiler_params=params(FULL),
        cost_estimate=cost(4 * near * capacity * tokens * width, 4 << 20),
        name="dispatch_rows",
    )(facts, hot, rows, crossed, away)


def combine_kernel(near, capacity, facts_ref, hot_ref, *refs):
    blocks = refs[:near]
    outs = refs[near : near + 4]
    gathered, sems = refs[near + 4 :]
    plane = facts_ref[0]
    width = gathered.shape[2]

    def copies(which):
        return [
            pltpu.make_async_copy(
                block.at[pl.ds(which * capacity, capacity)],
                gathered.at[which, pl.ds(j * capacity, capacity)],
                sems.at[which, j],
            )
            for j, block in enumerate(blocks)
        ]

    pending = [copies(0), copies(1)]
    for which in (1, 0):
        for copy in pending[which]:
            copy.start()
    for which in (1, 0):
        for copy in pending[which]:
            copy.wait()
        own_ref, away_ref = outs[2 * which : 2 * which + 2]
        for own, out_ref in ((True, own_ref), (False, away_ref)):
            columns = columns_of(plane, width, own)
            out_ref[...] = dot(hot_ref[which], gathered[which, :, columns], 0, 0).astype(
                out_ref.dtype
            )


def combine_rows(facts, hot, blocks, capacity):
    near = len(blocks)
    tokens, width = hot.shape[2], blocks[0].shape[1]
    own = jax.ShapeDtypeStruct((tokens, width // 2), jnp.float32)
    away = jax.ShapeDtypeStruct((tokens, width // 2), jnp.bfloat16)
    return pl.pallas_call(
        functools.partial(combine_kernel, near, capacity),
        in_specs=[SMEM, VMEM] + [ANY] * near,
        out_specs=[VMEM] * 4,
        out_shape=[own, away, own, away],
        scratch_shapes=[
            pltpu.VMEM((2, near * capacity, width), jnp.bfloat16),
            pltpu.SemaphoreType.DMA((2, near)),
        ],
        compiler_params=params(FULL),
        cost_estimate=cost(4 * near * capacity * tokens * width, 4 << 20),
        name="combine_rows",
    )(facts, hot, *blocks)


def expert_kernel(near, facts_ref, weights_ref, router_ref, *refs):
    row_blocks, cot_blocks = refs[:near], refs[near : 2 * near]
    refs = refs[2 * near :]
    back_blocks, moe_blocks = refs[:near], refs[near : 2 * near]
    rows_ref, hidden_ref, gate_grad_ref, up_grad_ref, slot_grad_ref, logits_ref = refs[
        2 * near : 2 * near + 6
    ]
    cot_all, back_all, moe_all, in_sems, out_sems = refs[2 * near + 6 :]
    index = pl.program_id(0)
    steps = pl.num_programs(0)
    block = row_blocks[0].shape[0]
    step = hidden_ref.shape[0]
    per_step = step // block

    def loads(j):
        place = pl.ds(j * block, block)
        return (
            pltpu.make_async_copy(row_blocks[j], rows_ref.at[place], in_sems.at[0, j]),
            pltpu.make_async_copy(cot_blocks[j], cot_all.at[place], in_sems.at[1, j]),
        )

    def stores(j):
        place = pl.ds(j * block, block)
        return (
            pltpu.make_async_copy(back_all.at[place], back_blocks[j], out_sems.at[0, j]),
            pltpu.make_async_copy(moe_all.at[place], moe_blocks[j], out_sems.at[1, j]),
        )

    @pl.when(index == 0)
    def _():
        for j in range(near):
            for copy in loads(j):
                copy.start()

    for s in range(near // per_step):

        @pl.when(index == s)
        def _():
            for j in range(s * per_step, (s + 1) * per_step):
                for copy in loads(j):
                    copy.wait()

    here = pl.ds(pl.multiple_of(index * step, step), step)
    width = rows_ref.shape[1]
    expert_count = router_ref.shape[0]
    rows = rows_ref[here, :]
    cot = cot_all[here, :width].astype(jnp.float32)
    picked = cot_all[here, width : width + 128][:, :expert_count]
    router = router_ref[...]
    logits = jnp.where(picked.astype(jnp.float32) > 0.5, dot(rows, router, 1, 1), NEGATIVE)
    terms = jnp.exp(logits - jnp.max(logits, axis=1, keepdims=True))
    gates = terms / jnp.sum(terms, axis=1, keepdims=True)
    expert = 2 * facts_ref[1] + facts_ref[0]
    own = (lax.broadcasted_iota(jnp.int32, gates.shape, 1) == expert).astype(jnp.float32)
    gate = jnp.sum(gates * own, axis=1, keepdims=True)

    def weight(f, i):
        value = weights_ref[:, f, i]
        return value.reshape(width, value.shape[-1])

    halves = range(weights_ref.shape[1])
    columns = weights_ref.shape[-1]
    kept = []
    out = 0.0
    for f in halves:
        gate_pre = dot(rows, weight(f, 0))
        up_pre = dot(rows, weight(f, 1))
        sigma = 1.0 / (1.0 + jnp.exp(-gate_pre))
        hidden = (gate_pre * sigma * up_pre).astype(jnp.bfloat16)
        hidden_ref[:, f * columns : (f + 1) * columns] = hidden
        out = out + dot(hidden, weight(f, 2), 1, 1)
        kept.append((gate_pre, up_pre, sigma))
    gate_grad = jnp.sum(out * cot, axis=1, keepdims=True)
    moe_all[here, :] = (gate * out).astype(jnp.bfloat16)
    slot_grad = (gate * cot).astype(jnp.bfloat16)
    slot_grad_ref[...] = slot_grad
    logits_grad = gate_grad * gate * (own - gates)
    upper = logits_grad.astype(jnp.bfloat16)
    lower = (logits_grad - upper.astype(jnp.float32)).astype(jnp.bfloat16)
    logits_ref[0] = upper
    logits_ref[1] = lower
    back = dot(upper, router) + dot(lower, router)
    for f in halves:
        gate_pre, up_pre, sigma = kept[f]
        hidden_grad = dot(slot_grad, weight(f, 2))
        gate_pre_grad = hidden_grad * up_pre * sigma * (1.0 + gate_pre * (1.0 - sigma))
        gate_pre_grad = gate_pre_grad.astype(jnp.bfloat16)
        up_pre_grad = (hidden_grad * gate_pre * sigma).astype(jnp.bfloat16)
        gate_grad_ref[:, f * columns : (f + 1) * columns] = gate_pre_grad
        up_grad_ref[:, f * columns : (f + 1) * columns] = up_pre_grad
        back = back + dot(gate_pre_grad, weight(f, 0), 1, 1)
        back = back + dot(up_pre_grad, weight(f, 1), 1, 1)
    back_all[here, :] = back.astype(jnp.bfloat16)

    for s in range(near // per_step):

        @pl.when(index == s)
        def _():
            for j in range(s * per_step, (s + 1) * per_step):
                for copy in stores(j):
                    copy.start()

    @pl.when(index == steps - 1)
    def _():
        for j in range(near):
            for copy in stores(j):
                copy.wait()


def run_expert(facts, row_blocks, cot_blocks, weights, router_t):
    near = len(row_blocks)
    block, width = row_blocks[0].shape
    count = near * block
    cot_width = cot_blocks[0].shape[1]
    hidden = 2 * weights.shape[-1]
    steps = 2
    step = count // steps
    bf16 = jnp.bfloat16
    row_block = lambda columns: pl.BlockSpec((step, columns), lambda i: (i, 0))
    whole = lambda value: pl.BlockSpec(value.shape, lambda i: (0,) * value.ndim)
    experts = router_t.shape[0]
    block_shape = jax.ShapeDtypeStruct((block, width), bf16)
    results = pl.pallas_call(
        functools.partial(expert_kernel, near),
        grid=(steps,),
        in_specs=[SMEM, whole(weights), whole(router_t)] + [ANY] * (2 * near),
        out_specs=[ANY] * (2 * near)
        + [
            pl.BlockSpec((count, width), lambda i: (0, 0)),
            row_block(hidden),
            row_block(hidden),
            row_block(hidden),
            row_block(width),
            pl.BlockSpec((2, step, experts), lambda i: (0, i, 0)),
        ],
        out_shape=[block_shape] * (2 * near)
        + [
            jax.ShapeDtypeStruct((count, width), bf16),
            jax.ShapeDtypeStruct((count, hidden), bf16),
            jax.ShapeDtypeStruct((count, hidden), bf16),
            jax.ShapeDtypeStruct((count, hidden), bf16),
            jax.ShapeDtypeStruct((count, width), bf16),
            jax.ShapeDtypeStruct((2, count, experts), bf16),
        ],
        scratch_shapes=[
            pltpu.VMEM((count, cot_width), bf16),
            pltpu.VMEM((count, width), bf16),
            pltpu.VMEM((count, width), bf16),
            pltpu.SemaphoreType.DMA((2, near)),
            pltpu.SemaphoreType.DMA((2, near)),
        ],
        compiler_params=params(FULL),
        cost_estimate=cost(12 * count * width * hidden, 16 << 20, count * hidden),
        name="expert_rows",
    )(facts, weights, router_t, *row_blocks, *cot_blocks)
    return results[:near], results[near : 2 * near], results[2 * near :]


def put_grad(piece, out_ref, place=()):
    blocks, planes, block_rows, columns = (
        out_ref.shape[0],
        out_ref.shape[1],
        out_ref.shape[-2],
        out_ref.shape[-1],
    )
    piece = piece.astype(jnp.bfloat16)
    for f in range(planes):
        out_ref[(slice(None), f) + place] = piece[:, f * columns : (f + 1) * columns].reshape(
            blocks, block_rows, columns
        )


def grads_kernel(
    rows_ref,
    hidden_ref,
    gate_grad_ref,
    up_grad_ref,
    slot_grad_ref,
    logits_ref,
    pair_ref,
    down_ref,
    router_ref,
):
    rows = rows_ref[...]
    put_grad(dot(slot_grad_ref[...], hidden_ref[...], 0, 0), down_ref)
    put_grad(dot(rows, gate_grad_ref[...], 0, 0), pair_ref, (0,))
    put_grad(dot(rows, up_grad_ref[...], 0, 0), pair_ref, (1,))
    router_ref[...] = dot(logits_ref[0], rows, 0, 0) + dot(logits_ref[1], rows, 0, 0)


def run_grads(rows, hidden, gate_grad, up_grad, slot_grad, logits, shape):
    count, width = rows.shape
    steps = 4
    step = width // steps
    experts = logits.shape[2]
    blocks, planes, tail = shape[0] // steps, shape[1], shape[2:]
    column = pl.BlockSpec((count, step), lambda i: (0, i))
    whole = lambda value: pl.BlockSpec(value.shape, lambda i: (0,) * value.ndim)
    return pl.pallas_call(
        grads_kernel,
        grid=(steps,),
        in_specs=[column, whole(hidden), whole(gate_grad), whole(up_grad), column, whole(logits)],
        out_specs=[
            pl.BlockSpec((blocks, planes, 2) + tail, lambda i: (i, 0, 0, 0, 0)),
            pl.BlockSpec((blocks, planes) + tail, lambda i: (i, 0, 0, 0)),
            pl.BlockSpec((experts, step), lambda i: (0, i)),
        ],
        out_shape=[
            jax.ShapeDtypeStruct(shape[:2] + (2,) + tail, jnp.bfloat16),
            jax.ShapeDtypeStruct(shape, jnp.bfloat16),
            jax.ShapeDtypeStruct((experts, width), jnp.float32),
        ],
        compiler_params=params(FULL),
        cost_estimate=cost(6 * count * math.prod(shape), 12 << 20),
        name="expert_grads",
    )(rows, hidden, gate_grad, up_grad, slot_grad, logits)


def tables_kernel(place_ref, placement_ref, lengths_ref, facts_ref, cos_ref, sin_ref):
    holder = lax.fori_loop(
        0,
        placement_ref.shape[0],
        lambda i, total: total + jnp.where(placement_ref[i] == place_ref[1], i, 0),
        jnp.int32(0),
    )
    facts_ref[0] = place_ref[0]
    facts_ref[1] = place_ref[2]
    rows, lanes = cos_ref.shape
    row = lax.broadcasted_iota(jnp.int32, (rows, lanes), 0)
    start = jnp.zeros((rows, lanes), jnp.int32)
    end = jnp.int32(0)
    count = lengths_ref.shape[0]
    for j in range(count):
        end = end + lengths_ref[j, holder]
        facts_ref[3 + j] = end
        start = jnp.where(row >= end, end, start)
    facts_ref[2] = end
    half = HEAD_DIM // 2
    lane = lax.broadcasted_iota(jnp.int32, (rows, lanes), 1)
    index = jnp.bitwise_and(lane, half - 1).astype(jnp.float32)
    frequency = jnp.exp(-(2.0 * index / (2.0 * half)) * math.log(ROPE_BASE))
    angles = (row - start).astype(jnp.float32) * frequency
    cos_ref[...] = jnp.cos(angles)
    sine = jnp.sin(angles)
    sin_ref[...] = jnp.where(jnp.bitwise_and(lane, half) == 0, -sine, sine)


def make_tables(place, placement, lengths_t, rows):
    table = jax.ShapeDtypeStruct((rows, 128), jnp.float32)
    return pl.pallas_call(
        tables_kernel,
        in_specs=[SMEM, SMEM, SMEM],
        out_specs=[SMEM, VMEM, VMEM],
        out_shape=[
            jax.ShapeDtypeStruct((3 + lengths_t.shape[0],), jnp.int32),
            table,
            table,
        ],
        compiler_params=params(FULL),
        cost_estimate=cost(1 << 20, 1 << 18, rows * 256),
        name="tables",
    )(place, placement, lengths_t)


def turn(values, cos, sine):
    half = HEAD_DIM // 2
    lane = lax.broadcasted_iota(jnp.int32, cos.shape, 1)
    first = jnp.bitwise_and(lane, half) == 0
    pieces = []
    for c in range(values.shape[1] // 128):
        piece = values[:, c * 128 : (c + 1) * 128]
        other = jnp.where(first, pltpu.roll(piece, 128 - half, 1), pltpu.roll(piece, half, 1))
        pieces.append(piece * cos + other * sine)
    return jnp.concatenate(pieces, axis=1)


def allowed_pairs(facts_ref, rows):
    query = lax.broadcasted_iota(jnp.int32, (rows, rows), 0)
    key = lax.broadcasted_iota(jnp.int32, (rows, rows), 1)
    start = jnp.zeros((rows, rows), jnp.int32)
    for j in range(3, facts_ref.shape[0]):
        start = jnp.where(query >= facts_ref[j], facts_ref[j], start)
    return (key <= query) & (key >= start)


def pair_heads(values, g):
    chunk = values[:, 2 * g * HEAD_DIM : 2 * (g + 1) * HEAD_DIM]
    return jnp.concatenate([chunk[:, :HEAD_DIM], chunk[:, HEAD_DIM:]], axis=0)


def unpair_heads(values):
    rows = values.shape[0] // 2
    return jnp.concatenate([values[:rows], values[rows:]], axis=1)


def pair_scores(query, key, allowed):
    scores = dot(query, key, 1, 1) * (1.0 / HEAD_DIM)
    return jnp.where(jnp.concatenate([allowed, allowed], axis=0), scores, NEGATIVE)


def put_halves(ref, plane, own, away):
    width = ref.shape[1]
    ref[:, columns_of(plane, width, True)] = own
    ref[:, columns_of(plane, width, False)] = away


def inverse_norm(values):
    mean = jnp.mean(values * values, axis=1, keepdims=True)
    return lax.rsqrt(mean + EPSILON)


def attend_kernel(
    facts_ref,
    own_ref,
    away_ref,
    gain_ref,
    query_w_ref,
    key_w_ref,
    value_w_ref,
    output_w_ref,
    cos_ref,
    sin_ref,
    part_ref,
    normed_ref,
    query_ref,
    key_ref,
    value_ref,
    context_ref,
    total_ref,
    wide,
):
    put_halves(
        wide, facts_ref[0], own_ref[...].astype(jnp.float32), away_ref[...].astype(jnp.float32)
    )
    values = wide[...]
    rows = values.shape[0]
    normed = (values * inverse_norm(values) * gain_ref[...]).astype(jnp.bfloat16)
    normed_ref[...] = normed
    cos, sine = cos_ref[...], sin_ref[...]
    query = turn(dot(normed, query_w_ref[...]), cos, sine).astype(jnp.bfloat16)
    key = turn(dot(normed, key_w_ref[...]), cos, sine).astype(jnp.bfloat16)
    value = dot(normed, value_w_ref[...]).astype(jnp.bfloat16)
    query_ref[...] = query
    key_ref[...] = key
    value_ref[...] = value
    allowed = allowed_pairs(facts_ref, rows)
    live = lax.broadcasted_iota(jnp.int32, (rows, 2 * HEAD_DIM), 0) < facts_ref[2]
    pieces, totals = [], []
    for g in range(key.shape[1] // HEAD_DIM):
        place = slice(g * HEAD_DIM, (g + 1) * HEAD_DIM)
        scores = pair_scores(pair_heads(query, g), key[:, place], allowed)
        top = jnp.max(scores, axis=1, keepdims=True)
        terms = jnp.exp(scores - top)
        total = jnp.sum(terms, axis=1, keepdims=True)
        probs = (terms / total).astype(jnp.bfloat16)
        context = unpair_heads(dot(probs, value[:, place]))
        pieces.append(jnp.where(live, context, 0.0).astype(jnp.bfloat16))
        log_total = top + jnp.log(total)
        totals += [log_total[:rows], log_total[rows:]]
    context = jnp.concatenate(pieces, axis=1)
    context_ref[...] = context
    lane = lax.broadcasted_iota(jnp.int32, (rows, 128), 1)
    packed = jnp.zeros((rows, 128), jnp.float32)
    for h, log_total in enumerate(totals):
        packed = jnp.where(lane == h, log_total, packed)
    total_ref[...] = packed
    part_ref[...] = dot(context, output_w_ref[...]).astype(jnp.bfloat16)


def attend(facts, own, away, gain, query_w, key_w, value_w, output_w, cos, sine):
    rows = own.shape[0]
    width = 2 * own.shape[1]
    low = lambda columns: jax.ShapeDtypeStruct((rows, columns), jnp.bfloat16)
    return pl.pallas_call(
        attend_kernel,
        in_specs=[SMEM] + [VMEM] * 9,
        out_specs=[VMEM] * 7,
        out_shape=[
            low(width),
            low(width),
            low(query_w.shape[1]),
            low(key_w.shape[1]),
            low(value_w.shape[1]),
            low(query_w.shape[1]),
            jax.ShapeDtypeStruct((rows, 128), jnp.float32),
        ],
        scratch_shapes=[pltpu.VMEM((rows, width), jnp.float32)],
        compiler_params=params(FULL),
        cost_estimate=cost(8 * rows * width * width // 2, 8 << 20, rows * rows * 8),
        name="attend",
    )(facts, own, away, gain, query_w, key_w, value_w, output_w, cos, sine)


def mix_kernel(
    facts_ref, own_ref, away_ref, part_ref, recv_ref, gain_ref, residual_ref, mixed_ref, half_ref
):
    plane = facts_ref[0]
    put_halves(
        residual_ref, plane, own_ref[...].astype(jnp.float32), away_ref[...].astype(jnp.float32)
    )
    residual = residual_ref[...] + (
        part_ref[...].astype(jnp.float32) + recv_ref[...].astype(jnp.float32)
    )
    residual_ref[...] = residual
    mixed_ref[...] = (residual * inverse_norm(residual) * gain_ref[...]).astype(jnp.bfloat16)
    half_ref[...] = mixed_ref[:, columns_of(plane, residual.shape[1], True)]


def mix(facts, own, away, part, recv, gain):
    rows, width = part.shape
    return pl.pallas_call(
        mix_kernel,
        in_specs=[SMEM] + [VMEM] * 5,
        out_specs=[VMEM] * 3,
        out_shape=[
            jax.ShapeDtypeStruct((rows, width), jnp.float32),
            jax.ShapeDtypeStruct((rows, width), jnp.bfloat16),
            jax.ShapeDtypeStruct((rows, width // 2), jnp.bfloat16),
        ],
        compiler_params=params(FULL),
        cost_estimate=cost(rows * width * 8, 3 << 20),
        name="mix",
    )(facts, own, away, part, recv, gain)


def attend_back_kernel(
    facts_ref,
    mixed_ref,
    mixed_away_ref,
    cot_ref,
    cot_away_ref,
    residual_ref,
    own_ref,
    away_ref,
    gain_ref,
    expert_gain_ref,
    normed_ref,
    query_ref,
    key_ref,
    value_ref,
    context_ref,
    total_ref,
    query_w_ref,
    key_w_ref,
    value_w_ref,
    output_w_ref,
    cos_ref,
    sin_ref,
    router_ref,
    parts_ref,
    normed_own_ref,
    normed_away_ref,
    base_ref,
    inner_ref,
    wide,
):
    plane = facts_ref[0]
    own_columns = columns_of(plane, wide.shape[1], True)
    away_columns = columns_of(plane, wide.shape[1], False)
    rows, width = wide.shape

    put_halves(
        wide, plane, mixed_ref[...].astype(jnp.float32), mixed_away_ref[...].astype(jnp.float32)
    )
    mixed_grad = wide[...]
    put_halves(
        wide, plane, cot_ref[...].astype(jnp.float32), cot_away_ref[...].astype(jnp.float32)
    )
    residual = residual_ref[...]
    inverse = inverse_norm(residual)
    scaled = mixed_grad * expert_gain_ref[...]
    mean = jnp.mean(scaled * residual, axis=1, keepdims=True)
    residual_grad = (
        wide[...] + inverse * scaled - residual * (inverse * inverse * inverse * mean)
    )
    expert_gain_grad = 0.5 * jnp.sum(mixed_grad * residual * inverse, axis=0, keepdims=True)
    wide[...] = residual_grad
    base_ref[...] = wide[:, own_columns]
    low = residual_grad.astype(jnp.bfloat16)
    context = context_ref[...]
    columns = context.shape[1]
    parts_ref[:, :columns] = dot(low, context, 0, 0).astype(parts_ref.dtype)
    live = lax.broadcasted_iota(jnp.int32, (rows, columns), 0) < facts_ref[2]
    context_grad = jnp.where(live, dot(low, output_w_ref[...], 1, 1), 0.0).astype(jnp.bfloat16)

    query, key, value = query_ref[...], key_ref[...], value_ref[...]
    totals = total_ref[...]
    allowed = allowed_pairs(facts_ref, rows)
    scale = 1.0 / HEAD_DIM
    query_grads, key_grads, value_grads = [], [], []
    for g in range(key.shape[1] // HEAD_DIM):
        place = slice(g * HEAD_DIM, (g + 1) * HEAD_DIM)
        pair = pair_heads(query, g)
        pair_grad = pair_heads(context_grad, g)
        total = jnp.concatenate([totals[:, 2 * g : 2 * g + 1], totals[:, 2 * g + 1 : 2 * g + 2]])
        probs = jnp.exp(pair_scores(pair, key[:, place], allowed) - total)
        prob_grad = dot(pair_grad, value[:, place], 1, 1)
        inner = jnp.sum(probs * prob_grad, axis=1, keepdims=True)
        score_grad = (probs * (prob_grad - inner)).astype(jnp.bfloat16)
        query_grads.append(unpair_heads(dot(score_grad, key[:, place]) * scale))
        key_grads.append(dot(score_grad, pair, 0, 0) * scale)
        value_grads.append(dot(probs.astype(jnp.bfloat16), pair_grad, 0, 0))
    cos, sine = cos_ref[...], -sin_ref[...]
    query_grad = turn(jnp.concatenate(query_grads, axis=1), cos, sine).astype(jnp.bfloat16)
    key_grad = turn(jnp.concatenate(key_grads, axis=1), cos, sine).astype(jnp.bfloat16)
    value_grad = jnp.concatenate(value_grads, axis=1).astype(jnp.bfloat16)
    normed_t = normed_ref[...]
    start = columns
    for grad in (query_grad, key_grad, value_grad):
        size = grad.shape[1]
        parts_ref[:, start : start + size] = dot(normed_t, grad, 0, 0).astype(parts_ref.dtype)
        start += size
    normed_grad = (
        dot(query_grad, query_w_ref[...], 1, 1)
        + dot(key_grad, key_w_ref[...], 1, 1)
        + dot(value_grad, value_w_ref[...], 1, 1)
    )
    put_halves(
        wide, plane, own_ref[...].astype(jnp.float32), away_ref[...].astype(jnp.float32)
    )
    values = wide[...]
    product = normed_grad * values
    gain_grad = jnp.sum(product * inverse_norm(values), axis=0, keepdims=True)
    inner = jnp.sum(product * gain_ref[...], axis=1, keepdims=True)
    inner_ref[...] = jnp.broadcast_to(inner, (rows, 128)).T[: inner_ref.shape[0]]
    wide[...] = normed_grad
    normed_own_ref[...] = wide[:, own_columns]
    normed_away_ref[...] = wide[:, away_columns].astype(jnp.bfloat16)
    experts = router_ref.shape[0]
    rest = jnp.zeros((128 - experts - 2, width), jnp.float32)
    packed = jnp.concatenate([router_ref[...], gain_grad, expert_gain_grad, rest], axis=0)
    parts_ref[:, start : start + 128] = packed.T.astype(parts_ref.dtype)


def attend_back(facts, *values):
    mixed, query_w, key_w, value_w = values[0], values[15], values[16], values[17]
    rows, half = mixed.shape
    width = 2 * half
    columns = 2 * query_w.shape[1] + key_w.shape[1] + value_w.shape[1] + 128
    wide = lambda columns, kind: jax.ShapeDtypeStruct((rows, columns), kind)
    return pl.pallas_call(
        attend_back_kernel,
        in_specs=[SMEM] + [VMEM] * len(values),
        out_specs=[VMEM] * 5,
        out_shape=[
            jax.ShapeDtypeStruct((width, columns), jnp.bfloat16),
            wide(half, jnp.float32),
            wide(half, jnp.bfloat16),
            wide(half, jnp.float32),
            jax.ShapeDtypeStruct((8, rows), jnp.float32),
        ],
        scratch_shapes=[pltpu.VMEM((rows, width), jnp.float32)],
        compiler_params=params(FULL),
        cost_estimate=cost(16 * rows * width * half * 2, 14 << 20, rows * rows * 8),
        name="attend_back",
    )(facts, *values)


def finish_kernel(
    facts_ref,
    own_ref,
    away_ref,
    gain_ref,
    residual_ref,
    moe_ref,
    moe_recv_ref,
    moe_cross_ref,
    base_ref,
    normed_ref,
    normed_recv_ref,
    inner_ref,
    inner_recv_ref,
    out_ref,
):
    rows, half = own_ref.shape
    own_columns = columns_of(facts_ref[0], 2 * half, True)
    own = own_ref[...].astype(jnp.float32)
    away = away_ref[...].astype(jnp.float32)
    total = jnp.sum(own * own, axis=1, keepdims=True) + jnp.sum(away * away, axis=1, keepdims=True)
    inverse = lax.rsqrt(total / (2 * half) + EPSILON)
    inner = (inner_ref[0:1, :] + inner_recv_ref[0:1, :]) / (2 * half)
    inner = jnp.broadcast_to(inner, (128, rows)).T[:, :1]
    normed = normed_ref[...] + normed_recv_ref[...].astype(jnp.float32)
    grad = (
        base_ref[...]
        + inverse * normed * gain_ref[:, own_columns]
        - own * (inverse * inverse * inverse * inner)
    )
    moe = (
        moe_ref[...]
        + moe_recv_ref[...].astype(jnp.float32)
        + moe_cross_ref[...].astype(jnp.float32)
    )
    out_ref[:, :half] = (residual_ref[:, own_columns] + moe).astype(out_ref.dtype)
    out_ref[:, half:] = grad.astype(out_ref.dtype)


def finish(facts, *values):
    rows, half = values[0].shape
    return pl.pallas_call(
        finish_kernel,
        in_specs=[SMEM] + [VMEM] * len(values),
        out_specs=VMEM,
        out_shape=jax.ShapeDtypeStruct((rows, 2 * half), jnp.bfloat16),
        compiler_params=params(FULL),
        cost_estimate=cost(rows * half * 16, 4 << 20),
        name="finish",
    )(facts, *values)


def local(
    inputs,
    cotangent,
    attn_gain,
    expert_gain,
    query_weight,
    key_weight,
    value_weight,
    output_weight,
    router_weight,
    gate_weight,
    up_weight,
    down_weight,
    routes,
    lengths,
    placement,
):
    row_count, top_count = routes.shape
    expert_count = router_weight.shape[1]
    capacity = row_count * top_count // expert_count
    kv_local = key_weight.shape[1] // HEAD_DIM
    heads_local = query_weight.shape[1] // HEAD_DIM
    group = heads_local // kv_local
    scale = 1.0 / HEAD_DIM
    width_half = inputs.shape[1]
    width = 2 * width_half
    plane = lax.axis_index("tensor")
    devices = lax.axis_size("dp")
    dp_index = lax.axis_index("dp")
    members = expert_count // 2
    near = members // 2
    clusters = devices // members
    member = dp_index % members
    expert = 2 * member + plane
    inside = [[c * members + m for m in range(members)] for c in range(clusters)]
    across = [[c * members + m for c in range(clusters)] for m in range(members)]

    def cross(values):
        return lax.ppermute(values, "dp", [(i, i ^ near) for i in range(devices)])

    def spread(blocks):
        return [blocks[0]] + [
            lax.ppermute(blocks[s], "dp", [(i, i ^ s) for i in range(devices)])
            for s in range(1, near)
        ]

    def halves(values, axis):
        size = values.shape[axis] // 2
        return (
            lax.dynamic_slice_in_dim(values, plane * size, size, axis),
            lax.dynamic_slice_in_dim(values, (1 - plane) * size, size, axis),
        )

    def join(own, other, axis):
        first = jnp.where(plane == 0, own, other)
        second = jnp.where(plane == 0, other, own)
        return jnp.concatenate([first, second], axis=axis)

    def add_planes(part):
        low = part.astype(jnp.bfloat16)
        return low.astype(jnp.float32) + swap_tensor(low).astype(jnp.float32)

    routes_t = routes.T
    away = swap_tensor(inputs)
    partner_t = cross(routes_t)
    cot_cross = cross(cotangent)
    cot_away = swap_tensor(cotangent)
    cot_cross_away = swap_tensor(cot_cross)
    place = jnp.stack([plane, dp_index, member]).astype(jnp.int32)
    facts, cos_table, sin_table = make_tables(place, placement, lengths.T, row_count)
    gain_one, gain_two = attn_gain[None], expert_gain[None]
    attn_part, normed, query, key, value, context, log_total = attend(
        facts,
        inputs,
        away,
        gain_one,
        query_weight,
        key_weight,
        value_weight,
        output_weight,
        cos_table,
        sin_table,
    )

    def to_owner(values):
        if clusters == 1:
            owned = lax.all_to_all(
                values, ("dp", "tensor"), split_axis=0, concat_axis=0, tiled=True
            )
            return owned.reshape((devices, 2) + owned.shape[1:])
        by_plane = values.reshape((members, 2) + values.shape[1:])
        own_w = lax.dynamic_index_in_dim(by_plane, plane, 1, keepdims=False)
        other_w = swap_tensor(lax.dynamic_index_in_dim(by_plane, 1 - plane, 1, keepdims=False))
        owned = jnp.stack(
            [jnp.where(plane == 0, own_w, other_w), jnp.where(plane == 0, other_w, own_w)], axis=1
        )
        owned = lax.all_to_all(
            owned, "dp", split_axis=0, concat_axis=0, tiled=True, axis_index_groups=inside
        )
        owned = lax.all_gather(owned, "dp", axis=0, tiled=True, axis_index_groups=across)
        owned = owned.reshape((members, clusters) + owned.shape[1:])
        owned = jnp.moveaxis(owned, 1, -3)
        return owned.reshape(owned.shape[:-3] + (-1, owned.shape[-1]))

    def from_owner(values):
        if clusters == 1:
            return lax.all_to_all(
                values.reshape((2 * devices,) + values.shape[2:]),
                ("dp", "tensor"),
                split_axis=0,
                concat_axis=0,
                tiled=True,
            )
        values = values.reshape(values.shape[:-2] + (clusters, -1, values.shape[-1]))
        values = jnp.moveaxis(values, -3, 1)
        values = values.reshape((devices,) + values.shape[2:])
        values = lax.psum_scatter(
            values, "dp", scatter_dimension=0, tiled=True, axis_index_groups=across
        )
        values = lax.all_to_all(
            values, "dp", split_axis=0, concat_axis=0, tiled=True, axis_index_groups=inside
        )
        own_g = lax.dynamic_index_in_dim(values, plane, 1, keepdims=False)
        other_g = swap_tensor(lax.dynamic_index_in_dim(values, 1 - plane, 1, keepdims=False))
        values = jnp.stack(
            [jnp.where(plane == 0, own_g, other_g), jnp.where(plane == 0, other_g, own_g)], axis=1
        )
        return values.reshape((expert_count,) + values.shape[2:])

    owned = to_owner(
        after(
            jnp.stack([gate_weight, up_weight, jnp.swapaxes(down_weight, 1, 2)], axis=1),
            away,
            partner_t,
            cot_away,
            cot_cross,
        )
    )

    hot, cot_blocks = dispatch_cot(
        facts,
        routes_t,
        partner_t,
        cotangent,
        cot_cross,
        cot_away,
        cot_cross_away,
        near,
        capacity,
        expert_count,
    )
    cot_blocks = spread(cot_blocks)

    def combine(hot, blocks):
        mine, mine_away, others, others_away = combine_rows(facts, hot, blocks, capacity)
        others = others + swap_tensor(others_away).astype(jnp.float32)
        return mine, swap_tensor(mine_away), cross(others.astype(jnp.bfloat16))

    residual, mixed_rows, mixed_half = mix(
        facts, inputs, away, attn_part, swap_tensor(attn_part), gain_two
    )
    mixed_cross = cross(mixed_half)
    mixed_away = swap_tensor(mixed_cross)
    row_blocks = spread(
        dispatch_rows(
            facts, after(hot, *cot_blocks[1:7]), mixed_rows, mixed_cross, mixed_away, near, capacity
        )
    )

    back_blocks, moe_blocks, kept = run_expert(
        facts, row_blocks, cot_blocks, owned, router_weight.T
    )
    back_blocks = spread(back_blocks)
    pair_part, down_part, router_part = run_grads(
        *kept, (members, 2, width // members, gate_weight.shape[2])
    )
    down_share = from_owner(down_part)
    moe_blocks = spread(moe_blocks)
    mine, mine_recv, mine_cross = combine(after(hot, down_share), back_blocks)
    mixed_half = mine + mine_recv.astype(jnp.float32) + mine_cross.astype(jnp.float32)
    mixed_half = mixed_half.astype(jnp.bfloat16)
    mixed_away = swap_tensor(mixed_half)
    pair_share = from_owner(after(pair_part, mixed_half))
    moe_parts = combine(hot, moe_blocks)

    parts, normed_own, normed_away, base_half, inner = attend_back(
        facts,
        mixed_half,
        mixed_away,
        cotangent,
        cot_away,
        after(residual, *moe_blocks),
        inputs,
        away,
        gain_one,
        gain_two,
        normed,
        query,
        key,
        value,
        context,
        log_total,
        query_weight,
        key_weight,
        value_weight,
        output_weight,
        cos_table,
        sin_table,
        router_part,
    )
    share = lax.psum_scatter(parts, "dp", scatter_dimension=0, tiled=True)
    cuts = [context.shape[1]]
    for w in (query_weight, key_weight, value_weight):
        cuts.append(cuts[-1] + w.shape[1])
    small = share[:, cuts[3] :]
    small = small.astype(jnp.float32) + swap_tensor(small).astype(jnp.float32)
    share = share.astype(jnp.float32)
    output_part = share[:, : cuts[0]].T
    query_part = share[:, cuts[0] : cuts[1]]
    key_part = share[:, cuts[1] : cuts[2]]
    value_part = share[:, cuts[2] : cuts[3]]
    router_share = small[:, :expert_count]
    attn_gain_part = small[:, expert_count]
    expert_gain_part = small[:, expert_count + 1]

    gate_w_part = pair_share[:, 0].astype(jnp.float32)
    up_w_part = pair_share[:, 1].astype(jnp.float32)
    down_w_part = jnp.swapaxes(down_share, 1, 2).astype(jnp.float32)

    piece_rows = row_count // devices
    moved = finish(
        facts,
        inputs,
        away,
        gain_one,
        residual,
        *moe_parts,
        base_half,
        normed_own,
        swap_tensor(normed_away),
        inner,
        swap_tensor(inner),
    )
    moved = after(moved, pair_share)
    moved = lax.all_to_all(
        moved.reshape(devices, piece_rows, width), "dp", split_axis=0, concat_axis=0, tiled=True
    )
    moved = jnp.take(moved, placement, axis=0)
    moved = lax.all_to_all(moved, "dp", split_axis=0, concat_axis=0, tiled=True)
    moved = moved.reshape(row_count, width)
    outputs = moved[:, :width_half]
    input_result = moved[:, width_half:].astype(jnp.float32)
    return (
        outputs,
        input_result,
        attn_gain_part,
        expert_gain_part,
        query_part,
        key_part,
        value_part,
        output_part,
        router_share,
        gate_w_part,
        up_w_part,
        down_w_part,
    )


def solution(mesh):
    in_specs = (
        P("dp", "tensor"),
        P("dp", "tensor"),
        P(),
        P(),
        P(None, "tensor"),
        P(None, "tensor"),
        P(None, "tensor"),
        P("tensor", None),
        P(),
        P(None, "dp", "tensor"),
        P(None, "dp", "tensor"),
        P(None, "tensor", "dp"),
        P("dp", None),
        P(),
        P(),
    )
    out_specs = (
        P("dp", "tensor"),
        P("dp", "tensor"),
        P("dp"),
        P("dp"),
        P("dp", "tensor"),
        P("dp", "tensor"),
        P("dp", "tensor"),
        P("tensor", "dp"),
        P("dp", None),
        P(None, "dp", "tensor"),
        P(None, "dp", "tensor"),
        P(None, "tensor", "dp"),
    )
    return jax.shard_map(local, mesh=mesh, in_specs=in_specs, out_specs=out_specs, check_vma=False)
```

time: 430 us -> 407 us (0.947)
  Pallas kernels: 24.2 us -> 70.8 us
  local copies, waits for them, and re-layouts: 52.5 us -> 14 us
  matrix products: 22 us -> 0 us
  other arithmetic: 29.6 us -> 15.5 us
  waiting for transfers between devices: 210 us -> 222 us
    pallas_call x2 -> x11, Pallas kernels: 24.2 us -> 70.8 us  [the longest x1 20.9 us: run_expert(): pl.pallas_call(functools.partial(expert_kernel, near), grid=(steps,), in_...]
    unnamed x164 -> x75, local copies, waits for them, and re-layouts: 34.3 us -> 7.41 us
    ppermute x28, waiting for transfers between devices: 115 us -> 89.8 us  [spread(): lax.ppermute(blocks[s], 'dp', [(i, i ^ s) for i in range(devices)])]
    dot_general x23 -> x0, matrix products: 22 us -> none  [the longest x12 15.1 us: mm(): lax.dot_general(left, right, ((contract[:1], contract[1:]), ((), ())), pr...]
    reduce_scatter x0 -> x1, waiting for transfers between devices: none -> 13.6 us  [local(): share = lax.psum_scatter(parts, 'dp', scatter_dimension=0, tiled=True)]
    ppermute x5, waiting for transfers between devices: 25.1 us -> 37.7 us  [cross(): return lax.ppermute(values, 'dp', [(i, i ^ near) for i in range(devices)])]
    split x4 -> x0, local copies, waits for them, and re-layouts: 9.25 us -> none  [the longest x2 5.37 us: combine(): rows = jnp.concatenate(spread(jnp.split(rows, near, axis=0)), axis=0)]
    all_to_all x1 -> x2, waiting for transfers between devices: 0.01 us -> 7.3 us  [from_owner(): lax.all_to_all(values.reshape((2 * devices,) + values.shape[2:]), ('dp',...]
  transfers between devices with their start and end apart: 50 -> 52, of which waited for: 32 -> 26; matrix products, arithmetic and copies ran while one was open for 21% -> 5% of each run, Pallas kernels for 2% -> 9%
where the time goes in v3:
time: 407 us; the launch traced here: 406 us
  waiting for transfers between devices  222 us (55%)
  Pallas kernels  70.8 us (17%)
  starting transfers between devices  68.6 us (17%)
  other arithmetic  15.5 us (4%)
  between operations  14.5 us (4%)
  local copies, waits for them, and re-layouts  14 us (3%)
    ppermute x28, waiting for transfers between devices, spread(): lax.ppermute(blocks[s], 'dp', [(i, i ^ s) for i in range(devices)])  89.8 us
    ppermute x13, waiting for transfers between devices, swap_tensor(): return lax.ppermute(values, 'tensor', [(0, 1), (1, 0)])  55.8 us
    ppermute x5, waiting for transfers between devices, cross(): return lax.ppermute(values, 'dp', [(i, i ^ near) for i in range(devices)])  37.7 us
    pallas_call x1, Pallas kernels, run_expert(): pl.pallas_call(functools.partial(expert_kernel, near), grid=(steps,), in_...  20.9 us
    ppermute x28, starting transfers between devices, spread(): lax.ppermute(blocks[s], 'dp', [(i, i ^ s) for i in range(devices)])  20.5 us
    all_to_all x1, waiting for transfers between devices, local(): lax.all_to_all(moved.reshape(devices, piece_rows, width), 'dp', split_axi...  18 us
    ppermute x13, starting transfers between devices, swap_tensor(): return lax.ppermute(values, 'tensor', [(0, 1), (1, 0)])  16.4 us
    reduce_scatter x1, waiting for transfers between devices, local(): share = lax.psum_scatter(parts, 'dp', scatter_dimension=0, tiled=True)  13.6 us
  transfers between devices with their start and end apart: 52, of which 26 were waited for; matrix products, arithmetic and copies ran while one was open for 5% of the time, Pallas kernels for 9%

profile of v3, /device:TPU:0, one launch (start us, length us, event | category | flops | bytes accessed | tf_op | source)
XLA Modules:
  0.0 405.7 jit_solution(13225782012182981543)
XLA Ops:
  7.2 3.0 collective-permute-start
  10.2 2.6 collective-permute-start.3
  13.3 3.8 pad_maximum_fusion
  17.1 7.9 %collective-permute-done.2.partner_ref = s32[8,256]{1,0:T(8,128)S(1)} collective-permute-done((s32[8,256]{1,0:T(8,128)}, s32[8,256]{1,0:T(8,128)S(1)}, u32[]{:S(2)}, u32[]{:S(2)}) %collective-permute-start.2) | collective-permute-done | bytes 8224 | tf_op jit(solution)/shard_map/ppermute | solution.py:853
  25.8 4.8 %all-to-all-start = ((bf16[32,3,64,256]{3,2,1,0:T(8,128)(2,1)}), bf16[32,3,64,256]{3,2,1,0:T(8,128)(2,1)S(1)}, u32[]{:S(2)}, u32[]{:S(2)}) async-start(bf16[32,3,64,256]{3,2,1,0:T(8,128)(2,1)} %pad_maximum_fusion), calls=%async_computation | async-start | bytes 6291456 | tf_op jit(solution)/shard_map/all_to_all | solution.py:901
  31.2 2.1 tables.1
  33.3 6.8 %attend.1 = (bf16[256,1024]{1,0:T(8,128)(2,1)}, bf16[256,1024]{1,0:T(8,128)(2,1)}, bf16[256,512]{1,0:T(8,128)(2,1)}, bf16[256,256]{1,0:T(8,128)(2,1)}, bf16[256,...) custom-call(s32[7]{0:T(128)} %get-tuple-element.86.facts_ref, bf16[256,512]{1,0:T(8,128)(2,1)} %own_ref.7, ...), custom_call_target="tpu_custom_call" | custom-call | flops 1073741824 | bytes 8388608 | tf_op jit(solution)/shard_map/attend/pallas_call | solution.py:578
  40.1 1.8 collective-permute-start.1
  42.2 38.4 %collective-permute-done.5.refs_3_ = bf16[256,512]{1,0:T(8,128)(2,1)S(1)} collective-permute-done((bf16[256,512]{1,0:T(8,128)(2,1)}, bf16[256,512]{1,0:T(8,128)(2,1)S(1)}, u32[]{:S(2)}, u32[]{:S(2)}) %collective-permute-start.5) | collective-permute-done | bytes 262176 | tf_op jit(solution)/shard_map/ppermute | solution.py:20
  81.3 3.9 dispatch_cot.1
  86.0 2.9 mix.1
  88.9 4.9 %collective-permute-start.12 = (bf16[256,512]{1,0:T(8,128)(2,1)}, bf16[256,512]{1,0:T(8,128)(2,1)S(1)}, u32[]{:S(2)}, u32[]{:S(2)}) collective-permute-start(bf16[256,512]{1,0:T(8,128)(2,1)} %get-tuple-element.101), channel_id=1, source_target_pairs={{0,16},{2,18},{4,20},{6,22},{8,24},{10,26},{12,28},{14,30},{16,0},... | collective-permute-start | bytes 786440 | tf_op jit(solution)/shard_map/ppermute | solution.py:853
  95.3 2.0 collective-permute-start.10
  97.8 15.4 %collective-permute-done.12.cross_ref = bf16[256,512]{1,0:T(8,128)(2,1)S(1)} collective-permute-done((bf16[256,512]{1,0:T(8,128)(2,1)}, bf16[256,512]{1,0:T(8,128)(2,1)S(1)}, u32[]{:S(2)}, u32[]{:S(2)}) %collective-permute-start.12) | collective-permute-done | bytes 262176 | tf_op jit(solution)/shard_map/ppermute | solution.py:853
  115.4 5.6 %collective-permute-done.10.refs_13_ = bf16[128,1152]{1,0:T(8,128)(2,1)} collective-permute-done((bf16[128,1152]{1,0:T(8,128)(2,1)}, bf16[128,1152]{1,0:T(8,128)(2,1)}, u32[]{:S(2)}, u32[]{:S(2)}) %collective-permute-start.10) | collective-permute-done | bytes 294944 | tf_op jit(solution)/shard_map/ppermute | solution.py:857
  121.0 6.6 %collective-permute-done.11.refs_14_ = bf16[128,1152]{1,0:T(8,128)(2,1)} collective-permute-done((bf16[128,1152]{1,0:T(8,128)(2,1)}, bf16[128,1152]{1,0:T(8,128)(2,1)}, u32[]{:S(2)}, u32[]{:S(2)}) %collective-permute-start.11) | collective-permute-done | bytes 294944 | tf_op jit(solution)/shard_map/ppermute | solution.py:857
  128.3 3.3 dispatch_rows.1
  131.6 1.9 collective-permute-start.15
  133.6 1.5 collective-permute-start.18
  135.1 1.7 collective-permute-start.19
  136.9 4.1 %collective-permute-done.15.refs_2_ = bf16[128,1024]{1,0:T(8,128)(2,1)S(1)} collective-permute-done((bf16[128,1024]{1,0:T(8,128)(2,1)}, bf16[128,1024]{1,0:T(8,128)(2,1)S(1)}, u32[]{:S(2)}, u32[]{:S(2)}) %collective-permute-start.15) | collective-permute-done | bytes 262176 | tf_op jit(solution)/shard_map/ppermute | solution.py:857
  140.9 5.0 %collective-permute-done.16.refs_3_ = bf16[128,1024]{1,0:T(8,128)(2,1)S(1)} collective-permute-done((bf16[128,1024]{1,0:T(8,128)(2,1)}, bf16[128,1024]{1,0:T(8,128)(2,1)S(1)}, u32[]{:S(2)}, u32[]{:S(2)}) %collective-permute-start.16) | collective-permute-done | bytes 262176 | tf_op jit(solution)/shard_map/ppermute | solution.py:857
  147.1 8.2 %collective-permute-done.19.refs_6_ = bf16[128,1024]{1,0:T(8,128)(2,1)S(1)} collective-permute-done((bf16[128,1024]{1,0:T(8,128)(2,1)}, bf16[128,1024]{1,0:T(8,128)(2,1)S(1)}, u32[]{:S(2)}, u32[]{:S(2)}) %collective-permute-start.19) | collective-permute-done | bytes 262176 | tf_op jit(solution)/shard_map/ppermute | solution.py:857
  156.0 3.8 collective-permute-done.20.refs_7_
  159.8 1.6 copy-done
  161.5 20.9 %expert_rows.1 = (bf16[128,1024]{1,0:T(8,128)(2,1)}, bf16[128,1024]{1,0:T(8,128)(2,1)}, bf16[128,1024]{1,0:T(8,128)(2,1)}, bf16[128,1024]{1,0:T(8,128)(2,1)}, bf...) custom-call(s32[7]{0:T(128)} %get-tuple-element.86.facts_ref, ...), custom_call_target="tpu_custom_call" | custom-call | flops 6442450944 | bytes 16777216 | tf_op jit(solution)/shard_map/expert_rows/pallas_call | solution.py:327
  182.4 8.1 %expert_grads.1 = (bf16[16,2,2,64,256]{4,3,2,1,0:T(8,128)(2,1)}, bf16[16,2,64,256]{3,2,1,0:T(8,128)(2,1)}, f32[32,1024]{1,0:T(8,128)}) custom-call(bf16[1024,1024]{1,0:T(8,128)(2,1)} %get-tuple-element.124.rows_ref, bf16[1024,512]{1,0:T(8,128)(2,1)} %get-tuple-element.125.hidden_ref, bf16[1024,512]{1,0:T(8,128)(2,1)} %get-tuple-element.126.gate_grad_ref, ...), custom_call_target="tpu_custom_call" | custom-call | flops 3221225472 | bytes 12582912 | tf_op jit(solution)/shard_map/expert_grads/pallas_call | solution.py:403
  190.5 2.8 all-to-all-start.1
  193.5 1.7 collective-permute-start.33
  195.2 1.7 collective-permute-start.35
  197.0 2.6 collective-permute-start.37
  199.6 12.0 %collective-permute-done.33.refs_2_ = bf16[128,1024]{1,0:T(8,128)(2,1)S(1)} collective-permute-done((bf16[128,1024]{1,0:T(8,128)(2,1)S(1)}, bf16[128,1024]{1,0:T(8,128)(2,1)S(1)}, u32[]{:S(2)}, u32[]{:S(2)}) %collective-permute-start.33) | collective-permute-done | bytes 262176 | tf_op jit(solution)/shard_map/ppermute | solution.py:857
  212.3 7.3 %all-to-all-done.1 = bf16[32,64,256]{2,1,0:T(8,128)(2,1)S(1)} async-done(((bf16[32,64,256]{2,1,0:T(8,128)(2,1)}), bf16[32,64,256]{2,1,0:T(8,128)(2,1)S(1)}, u32[]{:S(2)}, u32[]{:S(2)}) %all-to-all-start.1) | async-done | bytes 1048608 | tf_op jit(solution)/shard_map/all_to_all | solution.py:921
  219.6 4.0 collective-permute-done.36.refs_5_
  223.7 7.5 %collective-permute-done.37.refs_6_ = bf16[128,1024]{1,0:T(8,128)(2,1)S(1)} collective-permute-done((bf16[128,1024]{1,0:T(8,128)(2,1)}, bf16[128,1024]{1,0:T(8,128)(2,1)S(1)}, u32[]{:S(2)}, u32[]{:S(2)}) %collective-permute-start.37) | collective-permute-done | bytes 262176 | tf_op jit(solution)/shard_map/ppermute | solution.py:857
  231.2 4.7 %collective-permute-done.38.refs_7_ = bf16[128,1024]{1,0:T(8,128)(2,1)S(1)} collective-permute-done((bf16[128,1024]{1,0:T(8,128)(2,1)}, bf16[128,1024]{1,0:T(8,128)(2,1)S(1)}, u32[]{:S(2)}, u32[]{:S(2)}) %collective-permute-start.38) | collective-permute-done | bytes 262176 | tf_op jit(solution)/shard_map/ppermute | solution.py:857
  236.5 4.3 %combine_rows.3 = (f32[256,512]{1,0:T(8,128)}, bf16[256,512]{1,0:T(8,128)(2,1)}, f32[256,512]{1,0:T(8,128)}, bf16[256,512]{1,0:T(8,128)(2,1)}) custom-call(s32[7]{0:T(128)} %get-tuple-element.86.facts_ref, bf16[2,512,256]{2,1,0:T(8,128)(2,1)} %get-tuple-element.131.hot_ref, bf16[128,1024]{1,0:T(8,128)(2,1)} %get-tuple-element.132.refs_0_, ...), custom_call_target="tpu_custom_call" | custom-call | flops 536870912 | bytes 4194304 | tf_op jit(solution)/shard_map/combine_rows/pallas_call | solution.py:190
  240.9 1.6 collective-permute-start.40
  243.6 6.7 %collective-permute-done.40 = bf16[256,512]{1,0:T(8,128)(2,1)S(1)} collective-permute-done((bf16[256,512]{1,0:T(8,128)(2,1)}, bf16[256,512]{1,0:T(8,128)(2,1)S(1)}, u32[]{:S(2)}, u32[]{:S(2)}) %collective-permute-start.40) | collective-permute-done | bytes 262176 | tf_op jit(solution)/shard_map/ppermute | solution.py:20
  251.4 2.6 collective-permute-start.41
  256.0 1.6 collective-permute-start.27
  257.6 7.6 %collective-permute-done.41 = bf16[256,512]{1,0:T(8,128)(2,1)S(1)} collective-permute-done((bf16[256,512]{1,0:T(8,128)(2,1)S(1)}, bf16[256,512]{1,0:T(8,128)(2,1)S(1)}, u32[]{:S(2)}, u32[]{:S(2)}) %collective-permute-start.41) | collective-permute-done | bytes 262176 | tf_op jit(solution)/shard_map/ppermute | solution.py:853
  266.3 1.6 collective-permute-start.42
  268.0 3.9 all-to-all-start.2
  272.2 1.9 collective-permute-done.26.refs_5_
  274.1 11.2 %collective-permute-done.27.refs_6_ = bf16[128,1024]{1,0:T(8,128)(2,1)} collective-permute-done((bf16[128,1024]{1,0:T(8,128)(2,1)}, bf16[128,1024]{1,0:T(8,128)(2,1)}, u32[]{:S(2)}, u32[]{:S(2)}) %collective-permute-start.27) | collective-permute-done | bytes 262176 | tf_op jit(solution)/shard_map/ppermute | solution.py:857
  285.3 13.3 %collective-permute-done.28.refs_7_ = bf16[128,1024]{1,0:T(8,128)(2,1)} collective-permute-done((bf16[128,1024]{1,0:T(8,128)(2,1)}, bf16[128,1024]{1,0:T(8,128)(2,1)}, u32[]{:S(2)}, u32[]{:S(2)}) %collective-permute-start.28) | collective-permute-done | bytes 262176 | tf_op jit(solution)/shard_map/ppermute | solution.py:857
  298.6 10.9 %attend_back.1 = (bf16[1024,1664]{1,0:T(8,128)(2,1)}, f32[256,512]{1,0:T(8,128)}, bf16[256,512]{1,0:T(8,128)(2,1)}, f32[256,512]{1,0:T(8,128)}, f32[8,256]{1,0:T(8,128)}) custom-call(s32[7]{0:T(128)} %get-tuple-element.86.facts_ref, bf16[256,512]{1,0:T(8,128)(2,1)} %copy-done.3, bf16[256,512]{1,0:T(8,128)(2,1)} %collective-permute-done.42.mixed_away_ref, ...), custom_call_target="tpu_custom_call" | custom-call | flops 4294967296 | bytes 14680064 | tf_op jit(solution)/shard_map/attend_back/pallas_call | solution.py:745
  309.5 4.3 %combine_rows.2 = (f32[256,512]{1,0:T(8,128)}, bf16[256,512]{1,0:T(8,128)(2,1)}, f32[256,512]{1,0:T(8,128)}, bf16[256,512]{1,0:T(8,128)(2,1)}) custom-call(s32[7]{0:T(128)} %get-tuple-element.86.facts_ref, bf16[2,512,256]{2,1,0:T(8,128)(2,1)} %get-tuple-element.131.hot_ref, bf16[128,1024]{1,0:T(8,128)(2,1)} %get-tuple-element.112.refs_0_, ...), custom_call_target="tpu_custom_call" | custom-call | flops 536870912 | bytes 4194304 | tf_op jit(solution)/shard_map/combine_rows/pallas_call | solution.py:190
  313.9 2.0 collective-permute-start.29
  316.0 8.3 %collective-permute-done.30 = bf16[256,512]{1,0:T(8,128)(2,1)S(1)} collective-permute-done((bf16[256,512]{1,0:T(8,128)(2,1)}, bf16[256,512]{1,0:T(8,128)(2,1)S(1)}, u32[]{:S(2)}, u32[]{:S(2)}) %collective-permute-start.30) | collective-permute-done | bytes 262176 | tf_op jit(solution)/shard_map/ppermute | solution.py:20
  325.6 1.9 collective-permute-start.44
  327.6 2.3 collective-permute-done.29.moe_recv_ref
  329.9 6.8 %collective-permute-done.31.moe_cross_ref = bf16[256,512]{1,0:T(8,128)(2,1)S(1)} collective-permute-done((bf16[256,512]{1,0:T(8,128)(2,1)S(1)}, bf16[256,512]{1,0:T(8,128)(2,1)S(1)}, u32[]{:S(2)}, u32[]{:S(2)}) %collective-permute-start.31) | collective-permute-done | bytes 262176 | tf_op jit(solution)/shard_map/ppermute | solution.py:853
  337.5 3.4 finish.1
  340.9 5.0 %all-to-all-start.3 = ((bf16[16,16,1024]{2,1,0:T(8,128)(2,1)}), bf16[16,16,1024]{2,1,0:T(8,128)(2,1)}, u32[]{:S(2)}, u32[]{:S(2)}) async-start(bf16[16,16,1024]{2,1,0:T(8,128)(2,1)} %bitcast.36), calls=%async_computation.3 | async-start | bytes 1048576 | tf_op jit(solution)/shard_map/all_to_all | solution.py:1059
  345.9 1.6 convert_bitcast_fusion
  347.5 18.0 %all-to-all-done.3 = bf16[16,16,1024]{2,1,0:T(8,128)(2,1)} async-done(((bf16[16,16,1024]{2,1,0:T(8,128)(2,1)}), bf16[16,16,1024]{2,1,0:T(8,128)(2,1)}, u32[]{:S(2)}, u32[]{:S(2)}) %all-to-all-start.3) | async-done | bytes 524320 | tf_op jit(solution)/shard_map/all_to_all | solution.py:1059
  365.5 1.6 gather_fusion
  368.1 4.8 %all-to-all-start.4 = ((bf16[16,16,1024]{2,1,0:T(8,128)(2,1)}), bf16[16,16,1024]{2,1,0:T(8,128)(2,1)S(1)}, u32[]{:S(2)}, u32[]{:S(2)}) async-start(bf16[16,16,1024]{2,1,0:T(8,128)(2,1)} %broadcast_select_fusion), calls=%async_computation.4 | async-start | bytes 1048576 | tf_op jit(solution)/shard_map/all_to_all | solution.py:1063
  372.9 2.6 fusion
  375.4 13.6 %reduce-scatter.2.cloned.1.call-done = bf16[64,1664]{1,0:T(8,128)(2,1)} async-done(((bf16[1024,1664]{1,0:T(8,128)(2,1)}), bf16[64,1664]{1,0:T(8,128)(2,1)}) %reduce-scatter.2.cloned.1.call-update) | async-done | bytes 213008 | tf_op jit(solution)/shard_map/reduce_scatter | solution.py:1025
  389.8 1.5 collective-permute-start.45
  394.3 1.5 slice.55
  (147 shorter events, 27.9 us)
Async XLA Ops:
  7.2 17.9 %collective-permute-start = (bf16[256,512]{1,0:T(8,128)(2,1)}, bf16[256,512]{1,0:T(8,128)(2,1)S(1)}, u32[]{:S(2)}, u32[]{:S(2)}) collective-permute-start(bf16[256,512]{1,0:T(8,128)(2,1)} %own_ref.7), channel_id=1, source_target_pairs={{0,1},{1,0},{2,3},{3,2},{4,5},{5,4},{6,7},{7,6},{8,9},{9,8},{10,11... | collective-permute-start | bytes 786440 | tf_op jit(solution)/shard_map/ppermute | solution.py:20
  10.2 14.9 %collective-permute-start.3 = (bf16[256,512]{1,0:T(8,128)(2,1)}, bf16[256,512]{1,0:T(8,128)(2,1)}, u32[]{:S(2)}, u32[]{:S(2)}) collective-permute-start(bf16[256,512]{1,0:T(8,128)(2,1)} %cot_ref.1), channel_id=1, source_target_pairs={{0,16},{2,18},{4,20},{6,22},{8,24},{10,26},{12,28},{14,30},{16,0},... | collective-permute-start | bytes 786440 | tf_op jit(solution)/shard_map/ppermute | solution.py:853
  12.8 12.3 %collective-permute-start.4 = (bf16[256,512]{1,0:T(8,128)(2,1)}, bf16[256,512]{1,0:T(8,128)(2,1)}, u32[]{:S(2)}, u32[]{:S(2)}) collective-permute-start(bf16[256,512]{1,0:T(8,128)(2,1)} %cot_ref.1), channel_id=1, source_target_pairs={{0,1},{1,0},{2,3},{3,2},{4,5},{5,4},{6,7},{7,6},{8,9},{9,8},{10,11... | collective-permute-start | bytes 786440 | tf_op jit(solution)/shard_map/ppermute | solution.py:20
  13.3 11.7 %collective-permute-start.2 = (s32[8,256]{1,0:T(8,128)}, s32[8,256]{1,0:T(8,128)S(1)}, u32[]{:S(2)}, u32[]{:S(2)}) collective-permute-start(s32[8,256]{1,0:T(8,128)} %bitcast.48), channel_id=1, source_target_pairs={{0,16},{2,18},{4,20},{6,22},{8,24},{10,26},{12,28},{14,30},{16,0},... | collective-permute-start | bytes 24584 | tf_op jit(solution)/shard_map/ppermute | solution.py:853
  25.8 134.1 %all-to-all-start = ((bf16[32,3,64,256]{3,2,1,0:T(8,128)(2,1)}), bf16[32,3,64,256]{3,2,1,0:T(8,128)(2,1)S(1)}, u32[]{:S(2)}, u32[]{:S(2)}) async-start(bf16[32,3,64,256]{3,2,1,0:T(8,128)(2,1)} %pad_maximum_fusion), calls=%async_computation | async-start | bytes 6291456 | tf_op jit(solution)/shard_map/all_to_all | solution.py:901
  40.1 45.2 %collective-permute-start.1 = (bf16[256,1024]{1,0:T(8,128)(2,1)}, bf16[256,1024]{1,0:T(8,128)(2,1)S(1)}, u32[]{:S(2)}, u32[]{:S(2)}) collective-permute-start(bf16[256,1024]{1,0:T(8,128)(2,1)} %get-tuple-element.89.part_ref), channel_id=1, source_target_pairs={{0,1},{1,0},{2,3},{3,2},{4,5},{5,4},{6,7},{7,6},{8,9},{9,8},{10,11... | collective-permute-start | bytes 1572872 | tf_op jit(solution)/shard_map/ppermute | solution.py:20
  41.9 38.7 %collective-permute-start.5 = (bf16[256,512]{1,0:T(8,128)(2,1)}, bf16[256,512]{1,0:T(8,128)(2,1)S(1)}, u32[]{:S(2)}, u32[]{:S(2)}) collective-permute-start(bf16[256,512]{1,0:T(8,128)(2,1)} %collective-permute-done.3.refs_1_), channel_id=1, source_target_pairs={{0,1},{1,0},{2,3},{3,2},{4,5},{5,4},{6,7},{7,6},{8,9},{9,8},{10,11... | collective-permute-start | bytes 786440 | tf_op jit(solution)/shard_map/ppermute | solution.py:20
  85.1 10.2 %collective-permute-start.6 = (bf16[128,1152]{1,0:T(8,128)(2,1)}, bf16[128,1152]{1,0:T(8,128)(2,1)S(1)}, u32[]{:S(2)}, u32[]{:S(2)}) collective-permute-start(bf16[128,1152]{1,0:T(8,128)(2,1)} %get-tuple-element.93), channel_id=1, source_target_pairs={{0,2},{2,0},{4,6},{6,4},{8,10},{10,8},{12,14},{14,12},{16,18},{18,... | collective-permute-start | bytes 884744 | tf_op jit(solution)/shard_map/ppermute | solution.py:857
  85.1 12.2 %collective-permute-start.7 = (bf16[128,1152]{1,0:T(8,128)(2,1)}, bf16[128,1152]{1,0:T(8,128)(2,1)}, u32[]{:S(2)}, u32[]{:S(2)}) collective-permute-start(bf16[128,1152]{1,0:T(8,128)(2,1)} %get-tuple-element.94), channel_id=1, source_target_pairs={{0,4},{2,6},{4,0},{6,2},{8,12},{10,14},{12,8},{14,10},{16,20},{18,... | collective-permute-start | bytes 884744 | tf_op jit(solution)/shard_map/ppermute | solution.py:857
  88.9 24.3 %collective-permute-start.12 = (bf16[256,512]{1,0:T(8,128)(2,1)}, bf16[256,512]{1,0:T(8,128)(2,1)S(1)}, u32[]{:S(2)}, u32[]{:S(2)}) collective-permute-start(bf16[256,512]{1,0:T(8,128)(2,1)} %get-tuple-element.101), channel_id=1, source_target_pairs={{0,16},{2,18},{4,20},{6,22},{8,24},{10,26},{12,28},{14,30},{16,0},... | collective-permute-start | bytes 786440 | tf_op jit(solution)/shard_map/ppermute | solution.py:853
  93.8 20.8 %collective-permute-start.8 = (bf16[128,1152]{1,0:T(8,128)(2,1)}, bf16[128,1152]{1,0:T(8,128)(2,1)}, u32[]{:S(2)}, u32[]{:S(2)}) collective-permute-start(bf16[128,1152]{1,0:T(8,128)(2,1)} %get-tuple-element.95), channel_id=1, source_target_pairs={{0,6},{2,4},{4,2},{6,0},{8,14},{10,12},{12,10},{14,8},{16,22},{18,... | collective-permute-start | bytes 884744 | tf_op jit(solution)/shard_map/ppermute | solution.py:857
  95.3 20.0 %collective-permute-start.9 = (bf16[128,1152]{1,0:T(8,128)(2,1)}, bf16[128,1152]{1,0:T(8,128)(2,1)}, u32[]{:S(2)}, u32[]{:S(2)}) collective-permute-start(bf16[128,1152]{1,0:T(8,128)(2,1)} %get-tuple-element.96), channel_id=1, source_target_pairs={{0,8},{2,10},{4,12},{6,14},{8,0},{10,2},{12,4},{14,6},{16,24},{18,... | collective-permute-start | bytes 884744 | tf_op jit(solution)/shard_map/ppermute | solution.py:857
  95.3 64.5 %copy-start.19 = (bf16[128,1152]{1,0:T(8,128)(2,1)}, bf16[128,1152]{1,0:T(8,128)(2,1)S(1)}, u32[]{:S(2)}) copy-start(bf16[128,1152]{1,0:T(8,128)(2,1)S(1)} %collective-permute-done.6.refs_9_) | copy-start | bytes 884740
  95.3 25.6 %collective-permute-start.10 = (bf16[128,1152]{1,0:T(8,128)(2,1)}, bf16[128,1152]{1,0:T(8,128)(2,1)}, u32[]{:S(2)}, u32[]{:S(2)}) collective-permute-start(bf16[128,1152]{1,0:T(8,128)(2,1)} %get-tuple-element.97), channel_id=1, source_target_pairs={{0,10},{2,8},{4,14},{6,12},{8,2},{10,0},{12,6},{14,4},{16,26},{18,... | collective-permute-start | bytes 884744 | tf_op jit(solution)/shard_map/ppermute | solution.py:857
  97.3 30.3 %collective-permute-start.11 = (bf16[128,1152]{1,0:T(8,128)(2,1)}, bf16[128,1152]{1,0:T(8,128)(2,1)}, u32[]{:S(2)}, u32[]{:S(2)}) collective-permute-start(bf16[128,1152]{1,0:T(8,128)(2,1)} %get-tuple-element.98), channel_id=1, source_target_pairs={{0,12},{2,14},{4,8},{6,10},{8,4},{10,6},{12,0},{14,2},{16,28},{18,... | collective-permute-start | bytes 884744 | tf_op jit(solution)/shard_map/ppermute | solution.py:857
  113.2 15.1 %copy-start.32 = (bf16[256,512]{1,0:T(8,128)(2,1)}, bf16[256,512]{1,0:T(8,128)(2,1)S(1)}, u32[]{:S(2)}) copy-start(bf16[256,512]{1,0:T(8,128)(2,1)S(1)} %collective-permute-done.12.cross_ref) | copy-start | bytes 786436
  113.2 14.4 %collective-permute-start.13 = (bf16[256,512]{1,0:T(8,128)(2,1)S(1)}, bf16[256,512]{1,0:T(8,128)(2,1)S(1)}, u32[]{:S(2)}, u32[]{:S(2)}) collective-permute-start(bf16[256,512]{1,0:T(8,128)(2,1)S(1)} %collective-permute-done.12.cross_ref), channel_id=1, source_target_pairs={{0,1},{1,0},{2,3},{3,2},{4,5},{5,4},{6,7},{7,6},{8,9},{9,8},{10,11... | collective-permute-start | bytes 786440 | tf_op jit(solution)/shard_map/ppermute | solution.py:20
  114.6 19.0 %collective-permute-start.21 = (bf16[128,1152]{1,0:T(8,128)(2,1)}, bf16[128,1152]{1,0:T(8,128)(2,1)S(1)}, u32[]{:S(2)}, u32[]{:S(2)}) collective-permute-start(bf16[128,1152]{1,0:T(8,128)(2,1)} %get-tuple-element.111), channel_id=1, source_target_pairs={{0,14},{2,12},{4,10},{6,8},{8,6},{10,4},{12,2},{14,0},{16,30},{18,... | collective-permute-start | bytes 884744 | tf_op jit(solution)/shard_map/ppermute | solution.py:857
  131.6 3.5 collective-permute-start.14
  131.6 9.3 %collective-permute-start.15 = (bf16[128,1024]{1,0:T(8,128)(2,1)}, bf16[128,1024]{1,0:T(8,128)(2,1)S(1)}, u32[]{:S(2)}, u32[]{:S(2)}) collective-permute-start(bf16[128,1024]{1,0:T(8,128)(2,1)} %get-tuple-element.104), channel_id=1, source_target_pairs={{0,4},{2,6},{4,0},{6,2},{8,12},{10,14},{12,8},{14,10},{16,20},{18,... | collective-permute-start | bytes 786440 | tf_op jit(solution)/shard_map/ppermute | solution.py:857
  133.5 12.4 %collective-permute-start.16 = (bf16[128,1024]{1,0:T(8,128)(2,1)}, bf16[128,1024]{1,0:T(8,128)(2,1)S(1)}, u32[]{:S(2)}, u32[]{:S(2)}) collective-permute-start(bf16[128,1024]{1,0:T(8,128)(2,1)} %get-tuple-element.105), channel_id=1, source_target_pairs={{0,6},{2,4},{4,2},{6,0},{8,14},{10,12},{12,10},{14,8},{16,22},{18,... | collective-permute-start | bytes 786440 | tf_op jit(solution)/shard_map/ppermute | solution.py:857
  133.6 12.3 %collective-permute-start.17 = (bf16[128,1024]{1,0:T(8,128)(2,1)}, bf16[128,1024]{1,0:T(8,128)(2,1)S(1)}, u32[]{:S(2)}, u32[]{:S(2)}) collective-permute-start(bf16[128,1024]{1,0:T(8,128)(2,1)} %get-tuple-element.106), channel_id=1, source_target_pairs={{0,8},{2,10},{4,12},{6,14},{8,0},{10,2},{12,4},{14,6},{16,24},{18,... | collective-permute-start | bytes 786440 | tf_op jit(solution)/shard_map/ppermute | solution.py:857
  133.6 21.7 %copy-start.20 = (bf16[128,1152]{1,0:T(8,128)(2,1)}, bf16[128,1152]{1,0:T(8,128)(2,1)S(1)}, u32[]{:S(2)}) copy-start(bf16[128,1152]{1,0:T(8,128)(2,1)S(1)} %collective-permute-done.21.refs_15_) | copy-start | bytes 884740
  133.6 13.5 %collective-permute-start.18 = (bf16[128,1024]{1,0:T(8,128)(2,1)}, bf16[128,1024]{1,0:T(8,128)(2,1)S(1)}, u32[]{:S(2)}, u32[]{:S(2)}) collective-permute-start(bf16[128,1024]{1,0:T(8,128)(2,1)} %get-tuple-element.107), channel_id=1, source_target_pairs={{0,10},{2,8},{4,14},{6,12},{8,2},{10,0},{12,6},{14,4},{16,26},{18,... | collective-permute-start | bytes 786440 | tf_op jit(solution)/shard_map/ppermute | solution.py:857
  135.1 20.2 %copy-start.24 = (bf16[128,1024]{1,0:T(8,128)(2,1)}, bf16[128,1024]{1,0:T(8,128)(2,1)S(1)}, u32[]{:S(2)}) copy-start(bf16[128,1024]{1,0:T(8,128)(2,1)S(1)} %collective-permute-done.14.refs_1_) | copy-start | bytes 786436
  135.1 20.2 %collective-permute-start.19 = (bf16[128,1024]{1,0:T(8,128)(2,1)}, bf16[128,1024]{1,0:T(8,128)(2,1)S(1)}, u32[]{:S(2)}, u32[]{:S(2)}) collective-permute-start(bf16[128,1024]{1,0:T(8,128)(2,1)} %get-tuple-element.108), channel_id=1, source_target_pairs={{0,12},{2,14},{4,8},{6,10},{8,4},{10,6},{12,0},{14,2},{16,28},{18,... | collective-permute-start | bytes 786440 | tf_op jit(solution)/shard_map/ppermute | solution.py:857
  140.9 18.9 %collective-permute-start.20 = (bf16[128,1024]{1,0:T(8,128)(2,1)}, bf16[128,1024]{1,0:T(8,128)(2,1)}, u32[]{:S(2)}, u32[]{:S(2)}) collective-permute-start(bf16[128,1024]{1,0:T(8,128)(2,1)} %get-tuple-element.109), channel_id=1, source_target_pairs={{0,14},{2,12},{4,10},{6,8},{8,6},{10,4},{12,2},{14,0},{16,30},{18,... | collective-permute-start | bytes 786440 | tf_op jit(solution)/shard_map/ppermute | solution.py:857
  190.5 52.0 %copy-start.22 = (bf16[128,1024]{1,0:T(8,128)(2,1)S(1)}, bf16[128,1024]{1,0:T(8,128)(2,1)}, u32[]{:S(2)}) copy-start(bf16[128,1024]{1,0:T(8,128)(2,1)} %get-tuple-element.114) | copy-start | bytes 786436
  190.5 29.1 %all-to-all-start.1 = ((bf16[32,64,256]{2,1,0:T(8,128)(2,1)}), bf16[32,64,256]{2,1,0:T(8,128)(2,1)S(1)}, u32[]{:S(2)}, u32[]{:S(2)}) async-start(bf16[32,64,256]{2,1,0:T(8,128)(2,1)} %bitcast.37), calls=%async_computation.1 | async-start | bytes 2097152 | tf_op jit(solution)/shard_map/all_to_all | solution.py:921
  193.3 60.7 %copy-start.21 = (bf16[128,1024]{1,0:T(8,128)(2,1)S(1)}, bf16[128,1024]{1,0:T(8,128)(2,1)}, u32[]{:S(2)}) copy-start(bf16[128,1024]{1,0:T(8,128)(2,1)} %get-tuple-element.115) | copy-start | bytes 786436
  193.3 3.7 collective-permute-start.32
  193.5 18.1 %collective-permute-start.33 = (bf16[128,1024]{1,0:T(8,128)(2,1)S(1)}, bf16[128,1024]{1,0:T(8,128)(2,1)S(1)}, u32[]{:S(2)}, u32[]{:S(2)}) collective-permute-start(bf16[128,1024]{1,0:T(8,128)(2,1)S(1)} %copy-done.29), channel_id=1, source_target_pairs={{0,4},{2,6},{4,0},{6,2},{8,12},{10,14},{12,8},{14,10},{16,20},{18,... | collective-permute-start | bytes 786440 | tf_op jit(solution)/shard_map/ppermute | solution.py:857
  195.2 24.4 %collective-permute-start.34 = (bf16[128,1024]{1,0:T(8,128)(2,1)}, bf16[128,1024]{1,0:T(8,128)(2,1)S(1)}, u32[]{:S(2)}, u32[]{:S(2)}) collective-permute-start(bf16[128,1024]{1,0:T(8,128)(2,1)} %get-tuple-element.135), channel_id=1, source_target_pairs={{0,6},{2,4},{4,2},{6,0},{8,14},{10,12},{12,10},{14,8},{16,22},{18,... | collective-permute-start | bytes 786440 | tf_op jit(solution)/shard_map/ppermute | solution.py:857
  195.2 24.4 %collective-permute-start.35 = (bf16[128,1024]{1,0:T(8,128)(2,1)}, bf16[128,1024]{1,0:T(8,128)(2,1)S(1)}, u32[]{:S(2)}, u32[]{:S(2)}) collective-permute-start(bf16[128,1024]{1,0:T(8,128)(2,1)} %get-tuple-element.136), channel_id=1, source_target_pairs={{0,8},{2,10},{4,12},{6,14},{8,0},{10,2},{12,4},{14,6},{16,24},{18,... | collective-permute-start | bytes 786440 | tf_op jit(solution)/shard_map/ppermute | solution.py:857
  196.9 26.8 %collective-permute-start.36 = (bf16[128,1024]{1,0:T(8,128)(2,1)}, bf16[128,1024]{1,0:T(8,128)(2,1)S(1)}, u32[]{:S(2)}, u32[]{:S(2)}) collective-permute-start(bf16[128,1024]{1,0:T(8,128)(2,1)} %get-tuple-element.137), channel_id=1, source_target_pairs={{0,10},{2,8},{4,14},{6,12},{8,2},{10,0},{12,6},{14,4},{16,26},{18,... | collective-permute-start | bytes 786440 | tf_op jit(solution)/shard_map/ppermute | solution.py:857
  197.0 38.8 %copy-start.7 = (bf16[128,1024]{1,0:T(8,128)(2,1)}, bf16[128,1024]{1,0:T(8,128)(2,1)S(1)}, u32[]{:S(2)}) copy-start(bf16[128,1024]{1,0:T(8,128)(2,1)S(1)} %collective-permute-done.32.refs_1_) | copy-start | bytes 786436
  197.0 34.1 %collective-permute-start.37 = (bf16[128,1024]{1,0:T(8,128)(2,1)}, bf16[128,1024]{1,0:T(8,128)(2,1)S(1)}, u32[]{:S(2)}, u32[]{:S(2)}) collective-permute-start(bf16[128,1024]{1,0:T(8,128)(2,1)} %get-tuple-element.138), channel_id=1, source_target_pairs={{0,12},{2,14},{4,8},{6,10},{8,4},{10,6},{12,0},{14,2},{16,28},{18,... | collective-permute-start | bytes 786440 | tf_op jit(solution)/shard_map/ppermute | solution.py:857
  211.6 24.2 %copy-start.8 = (bf16[128,1024]{1,0:T(8,128)(2,1)}, bf16[128,1024]{1,0:T(8,128)(2,1)S(1)}, u32[]{:S(2)}) copy-start(bf16[128,1024]{1,0:T(8,128)(2,1)S(1)} %collective-permute-done.33.refs_2_) | copy-start | bytes 786436
  211.6 24.2 %collective-permute-start.38 = (bf16[128,1024]{1,0:T(8,128)(2,1)}, bf16[128,1024]{1,0:T(8,128)(2,1)S(1)}, u32[]{:S(2)}, u32[]{:S(2)}) collective-permute-start(bf16[128,1024]{1,0:T(8,128)(2,1)} %get-tuple-element.139), channel_id=1, source_target_pairs={{0,14},{2,12},{4,10},{6,8},{8,6},{10,4},{12,2},{14,0},{16,30},{18,... | collective-permute-start | bytes 786440 | tf_op jit(solution)/shard_map/ppermute | solution.py:857
  219.6 22.8 %copy-start.23 = (bf16[128,1024]{1,0:T(8,128)(2,1)S(1)}, bf16[128,1024]{1,0:T(8,128)(2,1)}, u32[]{:S(2)}) copy-start(bf16[128,1024]{1,0:T(8,128)(2,1)} %get-tuple-element.113) | copy-start | bytes 786436
  219.6 16.2 %copy-start.9 = (bf16[128,1024]{1,0:T(8,128)(2,1)}, bf16[128,1024]{1,0:T(8,128)(2,1)S(1)}, u32[]{:S(2)}) copy-start(bf16[128,1024]{1,0:T(8,128)(2,1)S(1)} %collective-permute-done.34.refs_3_) | copy-start | bytes 786436
  219.6 16.2 %copy-start.10 = (bf16[128,1024]{1,0:T(8,128)(2,1)}, bf16[128,1024]{1,0:T(8,128)(2,1)S(1)}, u32[]{:S(2)}) copy-start(bf16[128,1024]{1,0:T(8,128)(2,1)S(1)} %collective-permute-done.35.refs_4_) | copy-start | bytes 786436
  240.9 9.4 %collective-permute-start.40 = (bf16[256,512]{1,0:T(8,128)(2,1)}, bf16[256,512]{1,0:T(8,128)(2,1)S(1)}, u32[]{:S(2)}, u32[]{:S(2)}) collective-permute-start(bf16[256,512]{1,0:T(8,128)(2,1)} %get-tuple-element.143), channel_id=1, source_target_pairs={{0,1},{1,0},{2,3},{3,2},{4,5},{5,4},{6,7},{7,6},{8,9},{9,8},{10,11... | collective-permute-start | bytes 786440 | tf_op jit(solution)/shard_map/ppermute | solution.py:20
  242.4 11.5 %collective-permute-start.22 = (bf16[128,1024]{1,0:T(8,128)(2,1)S(1)}, bf16[128,1024]{1,0:T(8,128)(2,1)S(1)}, u32[]{:S(2)}, u32[]{:S(2)}) collective-permute-start(bf16[128,1024]{1,0:T(8,128)(2,1)S(1)} %copy-done.23), channel_id=1, source_target_pairs={{0,2},{2,0},{4,6},{6,4},{8,10},{10,8},{12,14},{14,12},{16,18},{18,... | collective-permute-start | bytes 786440 | tf_op jit(solution)/shard_map/ppermute | solution.py:857
  242.5 12.3 %collective-permute-start.23 = (bf16[128,1024]{1,0:T(8,128)(2,1)S(1)}, bf16[128,1024]{1,0:T(8,128)(2,1)S(1)}, u32[]{:S(2)}, u32[]{:S(2)}) collective-permute-start(bf16[128,1024]{1,0:T(8,128)(2,1)S(1)} %copy-done.22), channel_id=1, source_target_pairs={{0,4},{2,6},{4,0},{6,2},{8,12},{10,14},{12,8},{14,10},{16,20},{18,... | collective-permute-start | bytes 786440 | tf_op jit(solution)/shard_map/ppermute | solution.py:857
  243.0 12.9 %collective-permute-start.39 = (bf16[256,512]{1,0:T(8,128)(2,1)}, bf16[256,512]{1,0:T(8,128)(2,1)S(1)}, u32[]{:S(2)}, u32[]{:S(2)}) collective-permute-start(bf16[256,512]{1,0:T(8,128)(2,1)} %get-tuple-element.141), channel_id=1, source_target_pairs={{0,1},{1,0},{2,3},{3,2},{4,5},{5,4},{6,7},{7,6},{8,9},{9,8},{10,11... | collective-permute-start | bytes 786440 | tf_op jit(solution)/shard_map/ppermute | solution.py:20
  251.4 13.7 %collective-permute-start.41 = (bf16[256,512]{1,0:T(8,128)(2,1)S(1)}, bf16[256,512]{1,0:T(8,128)(2,1)S(1)}, u32[]{:S(2)}, u32[]{:S(2)}) collective-permute-start(bf16[256,512]{1,0:T(8,128)(2,1)S(1)} %add_convert_fusion.1), channel_id=1, source_target_pairs={{0,16},{2,18},{4,20},{6,22},{8,24},{10,26},{12,28},{14,30},{16,0},... | collective-permute-start | bytes 786440 | tf_op jit(solution)/shard_map/ppermute | solution.py:853
  254.0 12.4 %collective-permute-start.24 = (bf16[128,1024]{1,0:T(8,128)(2,1)S(1)}, bf16[128,1024]{1,0:T(8,128)(2,1)S(1)}, u32[]{:S(2)}, u32[]{:S(2)}) collective-permute-start(bf16[128,1024]{1,0:T(8,128)(2,1)S(1)} %copy-done.21), channel_id=1, source_target_pairs={{0,6},{2,4},{4,2},{6,0},{8,14},{10,12},{12,10},{14,8},{16,22},{18,... | collective-permute-start | bytes 786440 | tf_op jit(solution)/shard_map/ppermute | solution.py:857
  254.0 18.2 %collective-permute-start.25 = (bf16[128,1024]{1,0:T(8,128)(2,1)}, bf16[128,1024]{1,0:T(8,128)(2,1)}, u32[]{:S(2)}, u32[]{:S(2)}) collective-permute-start(bf16[128,1024]{1,0:T(8,128)(2,1)} %get-tuple-element.116), channel_id=1, source_target_pairs={{0,8},{2,10},{4,12},{6,14},{8,0},{10,2},{12,4},{14,6},{16,24},{18,... | collective-permute-start | bytes 786440 | tf_op jit(solution)/shard_map/ppermute | solution.py:857
  254.7 19.3 %collective-permute-start.26 = (bf16[128,1024]{1,0:T(8,128)(2,1)}, bf16[128,1024]{1,0:T(8,128)(2,1)}, u32[]{:S(2)}, u32[]{:S(2)}) collective-permute-start(bf16[128,1024]{1,0:T(8,128)(2,1)} %get-tuple-element.117), channel_id=1, source_target_pairs={{0,10},{2,8},{4,14},{6,12},{8,2},{10,0},{12,6},{14,4},{16,26},{18,... | collective-permute-start | bytes 786440 | tf_op jit(solution)/shard_map/ppermute | solution.py:857
  256.0 29.3 %collective-permute-start.27 = (bf16[128,1024]{1,0:T(8,128)(2,1)}, bf16[128,1024]{1,0:T(8,128)(2,1)}, u32[]{:S(2)}, u32[]{:S(2)}) collective-permute-start(bf16[128,1024]{1,0:T(8,128)(2,1)} %get-tuple-element.118), channel_id=1, source_target_pairs={{0,12},{2,14},{4,8},{6,10},{8,4},{10,6},{12,0},{14,2},{16,28},{18,... | collective-permute-start | bytes 786440 | tf_op jit(solution)/shard_map/ppermute | solution.py:857
  265.1 33.4 %collective-permute-start.28 = (bf16[128,1024]{1,0:T(8,128)(2,1)}, bf16[128,1024]{1,0:T(8,128)(2,1)}, u32[]{:S(2)}, u32[]{:S(2)}) collective-permute-start(bf16[128,1024]{1,0:T(8,128)(2,1)} %get-tuple-element.119), channel_id=1, source_target_pairs={{0,14},{2,12},{4,10},{6,8},{8,6},{10,4},{12,2},{14,0},{16,30},{18,... | collective-permute-start | bytes 786440 | tf_op jit(solution)/shard_map/ppermute | solution.py:857
  266.3 32.2 %collective-permute-start.42 = (bf16[256,512]{1,0:T(8,128)(2,1)S(1)}, bf16[256,512]{1,0:T(8,128)(2,1)}, u32[]{:S(2)}, u32[]{:S(2)}) collective-permute-start(bf16[256,512]{1,0:T(8,128)(2,1)S(1)} %add_convert_fusion.mixed_ref), channel_id=1, source_target_pairs={{0,1},{1,0},{2,3},{3,2},{4,5},{5,4},{6,7},{7,6},{8,9},{9,8},{10,11... | collective-permute-start | bytes 786440 | tf_op jit(solution)/shard_map/ppermute | solution.py:20
  268.0 72.9 %all-to-all-start.2 = ((bf16[32,2,64,256]{3,2,1,0:T(8,128)(2,1)}), bf16[32,2,64,256]{3,2,1,0:T(8,128)(2,1)S(1)}, u32[]{:S(2)}, u32[]{:S(2)}) async-start(bf16[32,2,64,256]{3,2,1,0:T(8,128)(2,1)} %bitcast.34), calls=%async_computation.2 | async-start | bytes 4194304 | tf_op jit(solution)/shard_map/all_to_all | solution.py:921
  271.9 117.2 %reduce-scatter.2.cloned.1.call-start = ((), (), s32[]{:S(2)}) async-start(), calls=%async_computation.6 | async-start | bytes 3620864 | tf_op jit(solution)/shard_map/reduce_scatter | solution.py:1025
  309.5 16.1 %copy-start.17 = (f32[8,256]{1,0:T(8,128)S(1)}, f32[8,256]{1,0:T(8,128)}, u32[]{:S(2)}) copy-start(f32[8,256]{1,0:T(8,128)} %get-tuple-element.155.inner_ref) | copy-start | bytes 24580
  313.9 10.4 %collective-permute-start.30 = (bf16[256,512]{1,0:T(8,128)(2,1)}, bf16[256,512]{1,0:T(8,128)(2,1)S(1)}, u32[]{:S(2)}, u32[]{:S(2)}) collective-permute-start(bf16[256,512]{1,0:T(8,128)(2,1)} %get-tuple-element.123), channel_id=1, source_target_pairs={{0,1},{1,0},{2,3},{3,2},{4,5},{5,4},{6,7},{7,6},{8,9},{9,8},{10,11... | collective-permute-start | bytes 786440 | tf_op jit(solution)/shard_map/ppermute | solution.py:20
  313.9 15.9 %collective-permute-start.29 = (bf16[256,512]{1,0:T(8,128)(2,1)}, bf16[256,512]{1,0:T(8,128)(2,1)S(1)}, u32[]{:S(2)}, u32[]{:S(2)}) collective-permute-start(bf16[256,512]{1,0:T(8,128)(2,1)} %get-tuple-element.121), channel_id=1, source_target_pairs={{0,1},{1,0},{2,3},{3,2},{4,5},{5,4},{6,7},{7,6},{8,9},{9,8},{10,11... | collective-permute-start | bytes 786440 | tf_op jit(solution)/shard_map/ppermute | solution.py:20
  325.4 11.3 %collective-permute-start.31 = (bf16[256,512]{1,0:T(8,128)(2,1)S(1)}, bf16[256,512]{1,0:T(8,128)(2,1)S(1)}, u32[]{:S(2)}, u32[]{:S(2)}) collective-permute-start(bf16[256,512]{1,0:T(8,128)(2,1)S(1)} %add_convert_fusion.2), channel_id=1, source_target_pairs={{0,16},{2,18},{4,20},{6,22},{8,24},{10,26},{12,28},{14,30},{16,0},... | collective-permute-start | bytes 786440 | tf_op jit(solution)/shard_map/ppermute | solution.py:853
  325.5 11.2 %collective-permute-start.43 = (bf16[256,512]{1,0:T(8,128)(2,1)}, bf16[256,512]{1,0:T(8,128)(2,1)S(1)}, u32[]{:S(2)}, u32[]{:S(2)}) collective-permute-start(bf16[256,512]{1,0:T(8,128)(2,1)} %get-tuple-element.154), channel_id=1, source_target_pairs={{0,1},{1,0},{2,3},{3,2},{4,5},{5,4},{6,7},{7,6},{8,9},{9,8},{10,11... | collective-permute-start | bytes 786440 | tf_op jit(solution)/shard_map/ppermute | solution.py:20
  325.6 11.1 %collective-permute-start.44 = (f32[8,256]{1,0:T(8,128)S(1)}, f32[8,256]{1,0:T(8,128)S(1)}, u32[]{:S(2)}, u32[]{:S(2)}) collective-permute-start(f32[8,256]{1,0:T(8,128)S(1)} %copy-done.17), channel_id=1, source_target_pairs={{0,1},{1,0},{2,3},{3,2},{4,5},{5,4},{6,7},{7,6},{8,9},{9,8},{10,11... | collective-permute-start | bytes 24584 | tf_op jit(solution)/shard_map/ppermute | solution.py:20
  340.9 24.7 %all-to-all-start.3 = ((bf16[16,16,1024]{2,1,0:T(8,128)(2,1)}), bf16[16,16,1024]{2,1,0:T(8,128)(2,1)}, u32[]{:S(2)}, u32[]{:S(2)}) async-start(bf16[16,16,1024]{2,1,0:T(8,128)(2,1)} %bitcast.36), calls=%async_computation.3 | async-start | bytes 1048576 | tf_op jit(solution)/shard_map/all_to_all | solution.py:1059
  368.1 29.9 %all-to-all-start.4 = ((bf16[16,16,1024]{2,1,0:T(8,128)(2,1)}), bf16[16,16,1024]{2,1,0:T(8,128)(2,1)S(1)}, u32[]{:S(2)}, u32[]{:S(2)}) async-start(bf16[16,16,1024]{2,1,0:T(8,128)(2,1)} %broadcast_select_fusion), calls=%async_computation.4 | async-start | bytes 1048576 | tf_op jit(solution)/shard_map/all_to_all | solution.py:1063
  389.8 6.1 %collective-permute-start.45 = (bf16[64,128]{1,0:T(8,128)(2,1)S(1)}, bf16[64,128]{1,0:T(8,128)(2,1)S(1)}, u32[]{:S(2)}, u32[]{:S(2)}) collective-permute-start(bf16[64,128]{1,0:T(8,128)(2,1)S(1)} %slice.52), channel_id=1, source_target_pairs={{0,1},{1,0},{2,3},{3,2},{4,5},{5,4},{6,7},{7,6},{8,9},{9,8},{10,11... | collective-permute-start | bytes 49160 | tf_op jit(solution)/shard_map/ppermute | solution.py:20
  (25 other events, 115.5 us)
Sparse Core Ops, SparseCore 0:
  309.6 79.3 reduce-scatter.1

commit v4 on v3

--- a/solution.py
+++ b/solution.py
@@ -209,7 +209,7 @@
     rows_ref, hidden_ref, gate_grad_ref, up_grad_ref, slot_grad_ref, logits_ref = refs[
         2 * near : 2 * near + 6
     ]
-    cot_all, back_all, moe_all, in_sems, out_sems = refs[2 * near + 6 :]
+    cot_all, back_all, moe_all, weights, in_sems, out_sems = refs[2 * near + 6 :]
     index = pl.program_id(0)
     steps = pl.num_programs(0)
     block = row_blocks[0].shape[0]
@@ -223,12 +223,10 @@
             pltpu.make_async_copy(cot_blocks[j], cot_all.at[place], in_sems.at[1, j]),
         )
 
-    def stores(j):
+    def store(which, j):
+        source, targets = ((back_all, back_blocks), (moe_all, moe_blocks))[which]
         place = pl.ds(j * block, block)
-        return (
-            pltpu.make_async_copy(back_all.at[place], back_blocks[j], out_sems.at[0, j]),
-            pltpu.make_async_copy(moe_all.at[place], moe_blocks[j], out_sems.at[1, j]),
-        )
+        return pltpu.make_async_copy(source.at[place], targets[j], out_sems.at[which, j])
 
     @pl.when(index == 0)
     def _():
@@ -258,24 +256,33 @@
     own = (lax.broadcasted_iota(jnp.int32, gates.shape, 1) == expert).astype(jnp.float32)
     gate = jnp.sum(gates * own, axis=1, keepdims=True)
 
-    def weight(f, i):
-        value = weights_ref[:, f, i]
-        return value.reshape(width, value.shape[-1])
-
-    halves = range(weights_ref.shape[1])
-    columns = weights_ref.shape[-1]
-    kept = []
-    out = 0.0
-    for f in halves:
-        gate_pre = dot(rows, weight(f, 0))
-        up_pre = dot(rows, weight(f, 1))
-        sigma = 1.0 / (1.0 + jnp.exp(-gate_pre))
-        hidden = (gate_pre * sigma * up_pre).astype(jnp.bfloat16)
-        hidden_ref[:, f * columns : (f + 1) * columns] = hidden
-        out = out + dot(hidden, weight(f, 2), 1, 1)
-        kept.append((gate_pre, up_pre, sigma))
+    @pl.when(index == 0)
+    def _():
+        columns = weights_ref.shape[-1]
+        for i in range(3):
+            for f in range(2):
+                weights[i, :, f * columns : (f + 1) * columns] = weights_ref[:, f, i].reshape(
+                    width, columns
+                )
+
+    gate_pre = dot(rows, weights[0])
+    up_pre = dot(rows, weights[1])
+    sigma = 1.0 / (1.0 + jnp.exp(-gate_pre))
+    hidden = (gate_pre * sigma * up_pre).astype(jnp.bfloat16)
+    hidden_ref[...] = hidden
+    out = dot(hidden, weights[2], 1, 1)
     gate_grad = jnp.sum(out * cot, axis=1, keepdims=True)
     moe_all[here, :] = (gate * out).astype(jnp.bfloat16)
+
+    def start_stores(which):
+        for s in range(near // per_step):
+
+            @pl.when(index == s)
+            def _():
+                for j in range(s * per_step, (s + 1) * per_step):
+                    store(which, j).start()
+
+    start_stores(1)
     slot_grad = (gate * cot).astype(jnp.bfloat16)
     slot_grad_ref[...] = slot_grad
     logits_grad = gate_grad * gate * (own - gates)
@@ -283,32 +290,22 @@
     lower = (logits_grad - upper.astype(jnp.float32)).astype(jnp.bfloat16)
     logits_ref[0] = upper
     logits_ref[1] = lower
+    hidden_grad = dot(slot_grad, weights[2])
+    gate_pre_grad = hidden_grad * up_pre * sigma * (1.0 + gate_pre * (1.0 - sigma))
+    gate_pre_grad = gate_pre_grad.astype(jnp.bfloat16)
+    up_pre_grad = (hidden_grad * gate_pre * sigma).astype(jnp.bfloat16)
+    gate_grad_ref[...] = gate_pre_grad
+    up_grad_ref[...] = up_pre_grad
     back = dot(upper, router) + dot(lower, router)
-    for f in halves:
-        gate_pre, up_pre, sigma = kept[f]
-        hidden_grad = dot(slot_grad, weight(f, 2))
-        gate_pre_grad = hidden_grad * up_pre * sigma * (1.0 + gate_pre * (1.0 - sigma))
-        gate_pre_grad = gate_pre_grad.astype(jnp.bfloat16)
-        up_pre_grad = (hidden_grad * gate_pre * sigma).astype(jnp.bfloat16)
-        gate_grad_ref[:, f * columns : (f + 1) * columns] = gate_pre_grad
-        up_grad_ref[:, f * columns : (f + 1) * columns] = up_pre_grad
-        back = back + dot(gate_pre_grad, weight(f, 0), 1, 1)
-        back = back + dot(up_pre_grad, weight(f, 1), 1, 1)
+    back = back + dot(gate_pre_grad, weights[0], 1, 1) + dot(up_pre_grad, weights[1], 1, 1)
     back_all[here, :] = back.astype(jnp.bfloat16)
-
-    for s in range(near // per_step):
-
-        @pl.when(index == s)
-        def _():
-            for j in range(s * per_step, (s + 1) * per_step):
-                for copy in stores(j):
-                    copy.start()
+    start_stores(0)
 
     @pl.when(index == steps - 1)
     def _():
         for j in range(near):
-            for copy in stores(j):
-                copy.wait()
+            store(0, j).wait()
+            store(1, j).wait()
 
 
 def run_expert(facts, row_blocks, cot_blocks, weights, router_t):
@@ -350,6 +347,7 @@
             pltpu.VMEM((count, cot_width), bf16),
             pltpu.VMEM((count, width), bf16),
             pltpu.VMEM((count, width), bf16),
+            pltpu.VMEM((3, width, hidden), bf16),
             pltpu.SemaphoreType.DMA((2, near)),
             pltpu.SemaphoreType.DMA((2, near)),
         ],

time: 407 us -> 405 us (level)
  no operation moved by 1% of the time
where the time goes in v4:
time: 405 us; the launch traced here: 404 us
  waiting for transfers between devices  219 us (54%)
  starting transfers between devices  71.5 us (18%)
  Pallas kernels  68.5 us (17%)
  other arithmetic  15.5 us (4%)
  between operations  14.5 us (4%)
  local copies, waits for them, and re-layouts  14 us (3%)
    ppermute x28, waiting for transfers between devices, spread(): lax.ppermute(blocks[s], 'dp', [(i, i ^ s) for i in range(devices)])  89.9 us
    ppermute x13, waiting for transfers between devices, swap_tensor(): return lax.ppermute(values, 'tensor', [(0, 1), (1, 0)])  55.7 us
    ppermute x5, waiting for transfers between devices, cross(): return lax.ppermute(values, 'dp', [(i, i ^ near) for i in range(devices)])  37.7 us
    ppermute x28, starting transfers between devices, spread(): lax.ppermute(blocks[s], 'dp', [(i, i ^ s) for i in range(devices)])  20.5 us
    ppermute x13, starting transfers between devices, swap_tensor(): return lax.ppermute(values, 'tensor', [(0, 1), (1, 0)])  18.9 us
    pallas_call x1, Pallas kernels, run_expert(): pl.pallas_call(functools.partial(expert_kernel, near), grid=(steps,), in_...  18.6 us
    all_to_all x1, waiting for transfers between devices, local(): lax.all_to_all(moved.reshape(devices, piece_rows, width), 'dp', split_axi...  17.9 us
    pallas_call x1, Pallas kernels, attend_back(): pl.pallas_call(attend_back_kernel, in_specs=[SMEM] + [VMEM] * len(values)...  10.9 us
  transfers between devices with their start and end apart: 52, of which 26 were waited for; matrix products, arithmetic and copies ran while one was open for 5% of the time, Pallas kernels for 9%

profile of v4, /device:TPU:0, one launch (start us, length us, event | category | flops | bytes accessed | tf_op | source)
XLA Modules:
  0.0 403.5 jit_solution(13455509925068080845)
XLA Ops:
  7.2 3.0 collective-permute-start
  10.2 2.6 collective-permute-start.3
  13.3 3.8 pad_maximum_fusion
  17.1 7.9 %collective-permute-done.2.partner_ref = s32[8,256]{1,0:T(8,128)S(1)} collective-permute-done((s32[8,256]{1,0:T(8,128)}, s32[8,256]{1,0:T(8,128)S(1)}, u32[]{:S(2)}, u32[]{:S(2)}) %collective-permute-start.2) | collective-permute-done | bytes 8224 | tf_op jit(solution)/shard_map/ppermute | solution.py:851
  25.8 4.8 %all-to-all-start = ((bf16[32,3,64,256]{3,2,1,0:T(8,128)(2,1)}), bf16[32,3,64,256]{3,2,1,0:T(8,128)(2,1)S(1)}, u32[]{:S(2)}, u32[]{:S(2)}) async-start(bf16[32,3,64,256]{3,2,1,0:T(8,128)(2,1)} %pad_maximum_fusion), calls=%async_computation | async-start | bytes 6291456 | tf_op jit(solution)/shard_map/all_to_all | solution.py:899
  31.2 2.1 tables.1
  33.3 6.8 %attend.1 = (bf16[256,1024]{1,0:T(8,128)(2,1)}, bf16[256,1024]{1,0:T(8,128)(2,1)}, bf16[256,512]{1,0:T(8,128)(2,1)}, bf16[256,256]{1,0:T(8,128)(2,1)}, bf16[256,...) custom-call(s32[7]{0:T(128)} %get-tuple-element.86.facts_ref, bf16[256,512]{1,0:T(8,128)(2,1)} %own_ref.7, ...), custom_call_target="tpu_custom_call" | custom-call | flops 1073741824 | bytes 8388608 | tf_op jit(solution)/shard_map/attend/pallas_call | solution.py:576
  40.1 1.8 collective-permute-start.1
  42.2 38.4 %collective-permute-done.5.refs_3_ = bf16[256,512]{1,0:T(8,128)(2,1)S(1)} collective-permute-done((bf16[256,512]{1,0:T(8,128)(2,1)}, bf16[256,512]{1,0:T(8,128)(2,1)S(1)}, u32[]{:S(2)}, u32[]{:S(2)}) %collective-permute-start.5) | collective-permute-done | bytes 262176 | tf_op jit(solution)/shard_map/ppermute | solution.py:20
  81.3 3.9 dispatch_cot.1
  86.0 2.9 mix.1
  88.9 4.9 %collective-permute-start.12 = (bf16[256,512]{1,0:T(8,128)(2,1)}, bf16[256,512]{1,0:T(8,128)(2,1)S(1)}, u32[]{:S(2)}, u32[]{:S(2)}) collective-permute-start(bf16[256,512]{1,0:T(8,128)(2,1)} %get-tuple-element.101), channel_id=1, source_target_pairs={{0,16},{2,18},{4,20},{6,22},{8,24},{10,26},{12,28},{14,30},{16,0},... | collective-permute-start | bytes 786440 | tf_op jit(solution)/shard_map/ppermute | solution.py:851
  95.3 2.0 collective-permute-start.10
  97.8 15.4 %collective-permute-done.12.cross_ref = bf16[256,512]{1,0:T(8,128)(2,1)S(1)} collective-permute-done((bf16[256,512]{1,0:T(8,128)(2,1)}, bf16[256,512]{1,0:T(8,128)(2,1)S(1)}, u32[]{:S(2)}, u32[]{:S(2)}) %collective-permute-start.12) | collective-permute-done | bytes 262176 | tf_op jit(solution)/shard_map/ppermute | solution.py:851
  115.4 5.6 %collective-permute-done.10.refs_13_ = bf16[128,1152]{1,0:T(8,128)(2,1)} collective-permute-done((bf16[128,1152]{1,0:T(8,128)(2,1)}, bf16[128,1152]{1,0:T(8,128)(2,1)}, u32[]{:S(2)}, u32[]{:S(2)}) %collective-permute-start.10) | collective-permute-done | bytes 294944 | tf_op jit(solution)/shard_map/ppermute | solution.py:855
  121.0 6.6 %collective-permute-done.11.refs_14_ = bf16[128,1152]{1,0:T(8,128)(2,1)} collective-permute-done((bf16[128,1152]{1,0:T(8,128)(2,1)}, bf16[128,1152]{1,0:T(8,128)(2,1)}, u32[]{:S(2)}, u32[]{:S(2)}) %collective-permute-start.11) | collective-permute-done | bytes 294944 | tf_op jit(solution)/shard_map/ppermute | solution.py:855
  128.3 3.3 dispatch_rows.1
  131.6 1.9 collective-permute-start.15
  133.6 1.5 collective-permute-start.18
  135.1 1.7 collective-permute-start.19
  136.9 4.1 %collective-permute-done.15.refs_2_ = bf16[128,1024]{1,0:T(8,128)(2,1)S(1)} collective-permute-done((bf16[128,1024]{1,0:T(8,128)(2,1)}, bf16[128,1024]{1,0:T(8,128)(2,1)S(1)}, u32[]{:S(2)}, u32[]{:S(2)}) %collective-permute-start.15) | collective-permute-done | bytes 262176 | tf_op jit(solution)/shard_map/ppermute | solution.py:855
  140.9 5.0 %collective-permute-done.16.refs_3_ = bf16[128,1024]{1,0:T(8,128)(2,1)S(1)} collective-permute-done((bf16[128,1024]{1,0:T(8,128)(2,1)}, bf16[128,1024]{1,0:T(8,128)(2,1)S(1)}, u32[]{:S(2)}, u32[]{:S(2)}) %collective-permute-start.16) | collective-permute-done | bytes 262176 | tf_op jit(solution)/shard_map/ppermute | solution.py:855
  147.1 8.2 %collective-permute-done.19.refs_6_ = bf16[128,1024]{1,0:T(8,128)(2,1)S(1)} collective-permute-done((bf16[128,1024]{1,0:T(8,128)(2,1)}, bf16[128,1024]{1,0:T(8,128)(2,1)S(1)}, u32[]{:S(2)}, u32[]{:S(2)}) %collective-permute-start.19) | collective-permute-done | bytes 262176 | tf_op jit(solution)/shard_map/ppermute | solution.py:855
  156.0 3.8 collective-permute-done.20.refs_7_
  159.8 1.6 copy-done
  161.5 18.6 %expert_rows.1 = (bf16[128,1024]{1,0:T(8,128)(2,1)}, bf16[128,1024]{1,0:T(8,128)(2,1)}, bf16[128,1024]{1,0:T(8,128)(2,1)}, bf16[128,1024]{1,0:T(8,128)(2,1)}, bf...) custom-call(s32[7]{0:T(128)} %get-tuple-element.86.facts_ref, ...), custom_call_target="tpu_custom_call" | custom-call | flops 6442450944 | bytes 16777216 | tf_op jit(solution)/shard_map/expert_rows/pallas_call | solution.py:324
  180.0 8.1 %expert_grads.1 = (bf16[16,2,2,64,256]{4,3,2,1,0:T(8,128)(2,1)}, bf16[16,2,64,256]{3,2,1,0:T(8,128)(2,1)}, f32[32,1024]{1,0:T(8,128)}) custom-call(bf16[1024,1024]{1,0:T(8,128)(2,1)} %get-tuple-element.124.rows_ref, bf16[1024,512]{1,0:T(8,128)(2,1)} %get-tuple-element.125.hidden_ref, bf16[1024,512]{1,0:T(8,128)(2,1)} %get-tuple-element.126.gate_grad_ref, ...), custom_call_target="tpu_custom_call" | custom-call | flops 3221225472 | bytes 12582912 | tf_op jit(solution)/shard_map/expert_grads/pallas_call | solution.py:401
  188.1 2.8 all-to-all-start.1
  191.2 1.6 collective-permute-start.33
  192.9 1.7 collective-permute-start.35
  194.7 2.6 collective-permute-start.37
  197.3 12.0 %collective-permute-done.33.refs_2_ = bf16[128,1024]{1,0:T(8,128)(2,1)S(1)} collective-permute-done((bf16[128,1024]{1,0:T(8,128)(2,1)S(1)}, bf16[128,1024]{1,0:T(8,128)(2,1)S(1)}, u32[]{:S(2)}, u32[]{:S(2)}) %collective-permute-start.33) | collective-permute-done | bytes 262176 | tf_op jit(solution)/shard_map/ppermute | solution.py:855
  210.0 7.3 %all-to-all-done.1 = bf16[32,64,256]{2,1,0:T(8,128)(2,1)S(1)} async-done(((bf16[32,64,256]{2,1,0:T(8,128)(2,1)}), bf16[32,64,256]{2,1,0:T(8,128)(2,1)S(1)}, u32[]{:S(2)}, u32[]{:S(2)}) %all-to-all-start.1) | async-done | bytes 1048608 | tf_op jit(solution)/shard_map/all_to_all | solution.py:919
  217.3 4.0 %collective-permute-done.36.refs_5_ = bf16[128,1024]{1,0:T(8,128)(2,1)S(1)} collective-permute-done((bf16[128,1024]{1,0:T(8,128)(2,1)}, bf16[128,1024]{1,0:T(8,128)(2,1)S(1)}, u32[]{:S(2)}, u32[]{:S(2)}) %collective-permute-start.36) | collective-permute-done | bytes 262176 | tf_op jit(solution)/shard_map/ppermute | solution.py:855
  221.3 7.5 %collective-permute-done.37.refs_6_ = bf16[128,1024]{1,0:T(8,128)(2,1)S(1)} collective-permute-done((bf16[128,1024]{1,0:T(8,128)(2,1)}, bf16[128,1024]{1,0:T(8,128)(2,1)S(1)}, u32[]{:S(2)}, u32[]{:S(2)}) %collective-permute-start.37) | collective-permute-done | bytes 262176 | tf_op jit(solution)/shard_map/ppermute | solution.py:855
  228.8 4.7 %collective-permute-done.38.refs_7_ = bf16[128,1024]{1,0:T(8,128)(2,1)S(1)} collective-permute-done((bf16[128,1024]{1,0:T(8,128)(2,1)}, bf16[128,1024]{1,0:T(8,128)(2,1)S(1)}, u32[]{:S(2)}, u32[]{:S(2)}) %collective-permute-start.38) | collective-permute-done | bytes 262176 | tf_op jit(solution)/shard_map/ppermute | solution.py:855
  234.2 4.3 %combine_rows.3 = (f32[256,512]{1,0:T(8,128)}, bf16[256,512]{1,0:T(8,128)(2,1)}, f32[256,512]{1,0:T(8,128)}, bf16[256,512]{1,0:T(8,128)(2,1)}) custom-call(s32[7]{0:T(128)} %get-tuple-element.86.facts_ref, bf16[2,512,256]{2,1,0:T(8,128)(2,1)} %get-tuple-element.131.hot_ref, bf16[128,1024]{1,0:T(8,128)(2,1)} %get-tuple-element.132.refs_0_, ...), custom_call_target="tpu_custom_call" | custom-call | flops 536870912 | bytes 4194304 | tf_op jit(solution)/shard_map/combine_rows/pallas_call | solution.py:190
  238.5 1.6 collective-permute-start.40
  241.2 6.7 %collective-permute-done.40 = bf16[256,512]{1,0:T(8,128)(2,1)S(1)} collective-permute-done((bf16[256,512]{1,0:T(8,128)(2,1)}, bf16[256,512]{1,0:T(8,128)(2,1)S(1)}, u32[]{:S(2)}, u32[]{:S(2)}) %collective-permute-start.40) | collective-permute-done | bytes 262176 | tf_op jit(solution)/shard_map/ppermute | solution.py:20
  249.1 2.6 collective-permute-start.41
  253.6 1.6 collective-permute-start.27
  255.2 7.6 %collective-permute-done.41 = bf16[256,512]{1,0:T(8,128)(2,1)S(1)} collective-permute-done((bf16[256,512]{1,0:T(8,128)(2,1)S(1)}, bf16[256,512]{1,0:T(8,128)(2,1)S(1)}, u32[]{:S(2)}, u32[]{:S(2)}) %collective-permute-start.41) | collective-permute-done | bytes 262176 | tf_op jit(solution)/shard_map/ppermute | solution.py:851
  264.0 1.6 collective-permute-start.42
  265.6 3.9 all-to-all-start.2
  269.8 1.9 collective-permute-done.26.refs_5_
  271.7 11.3 %collective-permute-done.27.refs_6_ = bf16[128,1024]{1,0:T(8,128)(2,1)} collective-permute-done((bf16[128,1024]{1,0:T(8,128)(2,1)}, bf16[128,1024]{1,0:T(8,128)(2,1)}, u32[]{:S(2)}, u32[]{:S(2)}) %collective-permute-start.27) | collective-permute-done | bytes 262176 | tf_op jit(solution)/shard_map/ppermute | solution.py:855
  283.0 13.2 %collective-permute-done.28.refs_7_ = bf16[128,1024]{1,0:T(8,128)(2,1)} collective-permute-done((bf16[128,1024]{1,0:T(8,128)(2,1)}, bf16[128,1024]{1,0:T(8,128)(2,1)}, u32[]{:S(2)}, u32[]{:S(2)}) %collective-permute-start.28) | collective-permute-done | bytes 262176 | tf_op jit(solution)/shard_map/ppermute | solution.py:855
  296.2 10.9 %attend_back.1 = (bf16[1024,1664]{1,0:T(8,128)(2,1)}, f32[256,512]{1,0:T(8,128)}, bf16[256,512]{1,0:T(8,128)(2,1)}, f32[256,512]{1,0:T(8,128)}, f32[8,256]{1,0:T(8,128)}) custom-call(s32[7]{0:T(128)} %get-tuple-element.86.facts_ref, bf16[256,512]{1,0:T(8,128)(2,1)} %copy-done.3, bf16[256,512]{1,0:T(8,128)(2,1)} %collective-permute-done.42.mixed_away_ref, ...), custom_call_target="tpu_custom_call" | custom-call | flops 4294967296 | bytes 14680064 | tf_op jit(solution)/shard_map/attend_back/pallas_call | solution.py:743
  307.2 4.3 %combine_rows.2 = (f32[256,512]{1,0:T(8,128)}, bf16[256,512]{1,0:T(8,128)(2,1)}, f32[256,512]{1,0:T(8,128)}, bf16[256,512]{1,0:T(8,128)(2,1)}) custom-call(s32[7]{0:T(128)} %get-tuple-element.86.facts_ref, bf16[2,512,256]{2,1,0:T(8,128)(2,1)} %get-tuple-element.131.hot_ref, bf16[128,1024]{1,0:T(8,128)(2,1)} %get-tuple-element.112.refs_0_, ...), custom_call_target="tpu_custom_call" | custom-call | flops 536870912 | bytes 4194304 | tf_op jit(solution)/shard_map/combine_rows/pallas_call | solution.py:190
  311.6 2.0 collective-permute-start.29
  313.7 8.3 %collective-permute-done.30 = bf16[256,512]{1,0:T(8,128)(2,1)S(1)} collective-permute-done((bf16[256,512]{1,0:T(8,128)(2,1)}, bf16[256,512]{1,0:T(8,128)(2,1)S(1)}, u32[]{:S(2)}, u32[]{:S(2)}) %collective-permute-start.30) | collective-permute-done | bytes 262176 | tf_op jit(solution)/shard_map/ppermute | solution.py:20
  323.2 2.0 collective-permute-start.44
  325.2 2.3 collective-permute-done.29.moe_recv_ref
  327.5 6.8 %collective-permute-done.31.moe_cross_ref = bf16[256,512]{1,0:T(8,128)(2,1)S(1)} collective-permute-done((bf16[256,512]{1,0:T(8,128)(2,1)S(1)}, bf16[256,512]{1,0:T(8,128)(2,1)S(1)}, u32[]{:S(2)}, u32[]{:S(2)}) %collective-permute-start.31) | collective-permute-done | bytes 262176 | tf_op jit(solution)/shard_map/ppermute | solution.py:851
  335.1 3.4 finish.1
  338.5 5.3 %all-to-all-start.3 = ((bf16[16,16,1024]{2,1,0:T(8,128)(2,1)}), bf16[16,16,1024]{2,1,0:T(8,128)(2,1)}, u32[]{:S(2)}, u32[]{:S(2)}) async-start(bf16[16,16,1024]{2,1,0:T(8,128)(2,1)} %bitcast.36), calls=%async_computation.3 | async-start | bytes 1048576 | tf_op jit(solution)/shard_map/all_to_all | solution.py:1057
  343.8 1.6 convert_bitcast_fusion
  345.4 17.9 %all-to-all-done.3 = bf16[16,16,1024]{2,1,0:T(8,128)(2,1)} async-done(((bf16[16,16,1024]{2,1,0:T(8,128)(2,1)}), bf16[16,16,1024]{2,1,0:T(8,128)(2,1)}, u32[]{:S(2)}, u32[]{:S(2)}) %all-to-all-start.3) | async-done | bytes 524320 | tf_op jit(solution)/shard_map/all_to_all | solution.py:1057
  363.3 1.6 gather_fusion
  365.9 4.9 %all-to-all-start.4 = ((bf16[16,16,1024]{2,1,0:T(8,128)(2,1)}), bf16[16,16,1024]{2,1,0:T(8,128)(2,1)S(1)}, u32[]{:S(2)}, u32[]{:S(2)}) async-start(bf16[16,16,1024]{2,1,0:T(8,128)(2,1)} %broadcast_select_fusion), calls=%async_computation.4 | async-start | bytes 1048576 | tf_op jit(solution)/shard_map/all_to_all | solution.py:1061
  370.8 2.6 fusion
  373.4 10.9 %reduce-scatter.2.cloned.1.call-done = bf16[64,1664]{1,0:T(8,128)(2,1)} async-done(((bf16[1024,1664]{1,0:T(8,128)(2,1)}), bf16[64,1664]{1,0:T(8,128)(2,1)}) %reduce-scatter.2.cloned.1.call-update) | async-done | bytes 213008 | tf_op jit(solution)/shard_map/reduce_scatter | solution.py:1023
  385.0 4.0 %collective-permute-start.45 = (bf16[64,128]{1,0:T(8,128)(2,1)S(1)}, bf16[64,128]{1,0:T(8,128)(2,1)S(1)}, u32[]{:S(2)}, u32[]{:S(2)}) collective-permute-start(bf16[64,128]{1,0:T(8,128)(2,1)S(1)} %slice.52), channel_id=1, source_target_pairs={{0,1},{1,0},{2,3},{3,2},{4,5},{5,4},{6,7},{7,6},{8,9},{9,8},{10,11... | collective-permute-start | bytes 49160 | tf_op jit(solution)/shard_map/ppermute | solution.py:20
  392.1 1.5 slice.55
  (147 shorter events, 27.8 us)
Async XLA Ops:
  7.2 17.9 %collective-permute-start = (bf16[256,512]{1,0:T(8,128)(2,1)}, bf16[256,512]{1,0:T(8,128)(2,1)S(1)}, u32[]{:S(2)}, u32[]{:S(2)}) collective-permute-start(bf16[256,512]{1,0:T(8,128)(2,1)} %own_ref.7), channel_id=1, source_target_pairs={{0,1},{1,0},{2,3},{3,2},{4,5},{5,4},{6,7},{7,6},{8,9},{9,8},{10,11... | collective-permute-start | bytes 786440 | tf_op jit(solution)/shard_map/ppermute | solution.py:20
  10.2 14.9 %collective-permute-start.3 = (bf16[256,512]{1,0:T(8,128)(2,1)}, bf16[256,512]{1,0:T(8,128)(2,1)}, u32[]{:S(2)}, u32[]{:S(2)}) collective-permute-start(bf16[256,512]{1,0:T(8,128)(2,1)} %cot_ref.1), channel_id=1, source_target_pairs={{0,16},{2,18},{4,20},{6,22},{8,24},{10,26},{12,28},{14,30},{16,0},... | collective-permute-start | bytes 786440 | tf_op jit(solution)/shard_map/ppermute | solution.py:851
  12.8 12.3 %collective-permute-start.4 = (bf16[256,512]{1,0:T(8,128)(2,1)}, bf16[256,512]{1,0:T(8,128)(2,1)}, u32[]{:S(2)}, u32[]{:S(2)}) collective-permute-start(bf16[256,512]{1,0:T(8,128)(2,1)} %cot_ref.1), channel_id=1, source_target_pairs={{0,1},{1,0},{2,3},{3,2},{4,5},{5,4},{6,7},{7,6},{8,9},{9,8},{10,11... | collective-permute-start | bytes 786440 | tf_op jit(solution)/shard_map/ppermute | solution.py:20
  13.3 11.7 %collective-permute-start.2 = (s32[8,256]{1,0:T(8,128)}, s32[8,256]{1,0:T(8,128)S(1)}, u32[]{:S(2)}, u32[]{:S(2)}) collective-permute-start(s32[8,256]{1,0:T(8,128)} %bitcast.48), channel_id=1, source_target_pairs={{0,16},{2,18},{4,20},{6,22},{8,24},{10,26},{12,28},{14,30},{16,0},... | collective-permute-start | bytes 24584 | tf_op jit(solution)/shard_map/ppermute | solution.py:851
  25.8 134.1 %all-to-all-start = ((bf16[32,3,64,256]{3,2,1,0:T(8,128)(2,1)}), bf16[32,3,64,256]{3,2,1,0:T(8,128)(2,1)S(1)}, u32[]{:S(2)}, u32[]{:S(2)}) async-start(bf16[32,3,64,256]{3,2,1,0:T(8,128)(2,1)} %pad_maximum_fusion), calls=%async_computation | async-start | bytes 6291456 | tf_op jit(solution)/shard_map/all_to_all | solution.py:899
  40.1 45.2 %collective-permute-start.1 = (bf16[256,1024]{1,0:T(8,128)(2,1)}, bf16[256,1024]{1,0:T(8,128)(2,1)S(1)}, u32[]{:S(2)}, u32[]{:S(2)}) collective-permute-start(bf16[256,1024]{1,0:T(8,128)(2,1)} %get-tuple-element.89.part_ref), channel_id=1, source_target_pairs={{0,1},{1,0},{2,3},{3,2},{4,5},{5,4},{6,7},{7,6},{8,9},{9,8},{10,11... | collective-permute-start | bytes 1572872 | tf_op jit(solution)/shard_map/ppermute | solution.py:20
  41.9 38.7 %collective-permute-start.5 = (bf16[256,512]{1,0:T(8,128)(2,1)}, bf16[256,512]{1,0:T(8,128)(2,1)S(1)}, u32[]{:S(2)}, u32[]{:S(2)}) collective-permute-start(bf16[256,512]{1,0:T(8,128)(2,1)} %collective-permute-done.3.refs_1_), channel_id=1, source_target_pairs={{0,1},{1,0},{2,3},{3,2},{4,5},{5,4},{6,7},{7,6},{8,9},{9,8},{10,11... | collective-permute-start | bytes 786440 | tf_op jit(solution)/shard_map/ppermute | solution.py:20
  85.1 10.2 %collective-permute-start.6 = (bf16[128,1152]{1,0:T(8,128)(2,1)}, bf16[128,1152]{1,0:T(8,128)(2,1)S(1)}, u32[]{:S(2)}, u32[]{:S(2)}) collective-permute-start(bf16[128,1152]{1,0:T(8,128)(2,1)} %get-tuple-element.93), channel_id=1, source_target_pairs={{0,2},{2,0},{4,6},{6,4},{8,10},{10,8},{12,14},{14,12},{16,18},{18,... | collective-permute-start | bytes 884744 | tf_op jit(solution)/shard_map/ppermute | solution.py:855
  85.1 12.2 %collective-permute-start.7 = (bf16[128,1152]{1,0:T(8,128)(2,1)}, bf16[128,1152]{1,0:T(8,128)(2,1)}, u32[]{:S(2)}, u32[]{:S(2)}) collective-permute-start(bf16[128,1152]{1,0:T(8,128)(2,1)} %get-tuple-element.94), channel_id=1, source_target_pairs={{0,4},{2,6},{4,0},{6,2},{8,12},{10,14},{12,8},{14,10},{16,20},{18,... | collective-permute-start | bytes 884744 | tf_op jit(solution)/shard_map/ppermute | solution.py:855
  88.9 24.3 %collective-permute-start.12 = (bf16[256,512]{1,0:T(8,128)(2,1)}, bf16[256,512]{1,0:T(8,128)(2,1)S(1)}, u32[]{:S(2)}, u32[]{:S(2)}) collective-permute-start(bf16[256,512]{1,0:T(8,128)(2,1)} %get-tuple-element.101), channel_id=1, source_target_pairs={{0,16},{2,18},{4,20},{6,22},{8,24},{10,26},{12,28},{14,30},{16,0},... | collective-permute-start | bytes 786440 | tf_op jit(solution)/shard_map/ppermute | solution.py:851
  93.8 20.8 %collective-permute-start.8 = (bf16[128,1152]{1,0:T(8,128)(2,1)}, bf16[128,1152]{1,0:T(8,128)(2,1)}, u32[]{:S(2)}, u32[]{:S(2)}) collective-permute-start(bf16[128,1152]{1,0:T(8,128)(2,1)} %get-tuple-element.95), channel_id=1, source_target_pairs={{0,6},{2,4},{4,2},{6,0},{8,14},{10,12},{12,10},{14,8},{16,22},{18,... | collective-permute-start | bytes 884744 | tf_op jit(solution)/shard_map/ppermute | solution.py:855
  95.3 20.0 %collective-permute-start.9 = (bf16[128,1152]{1,0:T(8,128)(2,1)}, bf16[128,1152]{1,0:T(8,128)(2,1)}, u32[]{:S(2)}, u32[]{:S(2)}) collective-permute-start(bf16[128,1152]{1,0:T(8,128)(2,1)} %get-tuple-element.96), channel_id=1, source_target_pairs={{0,8},{2,10},{4,12},{6,14},{8,0},{10,2},{12,4},{14,6},{16,24},{18,... | collective-permute-start | bytes 884744 | tf_op jit(solution)/shard_map/ppermute | solution.py:855
  95.3 64.5 %copy-start.19 = (bf16[128,1152]{1,0:T(8,128)(2,1)}, bf16[128,1152]{1,0:T(8,128)(2,1)S(1)}, u32[]{:S(2)}) copy-start(bf16[128,1152]{1,0:T(8,128)(2,1)S(1)} %collective-permute-done.6.refs_9_) | copy-start | bytes 884740
  95.3 25.6 %collective-permute-start.10 = (bf16[128,1152]{1,0:T(8,128)(2,1)}, bf16[128,1152]{1,0:T(8,128)(2,1)}, u32[]{:S(2)}, u32[]{:S(2)}) collective-permute-start(bf16[128,1152]{1,0:T(8,128)(2,1)} %get-tuple-element.97), channel_id=1, source_target_pairs={{0,10},{2,8},{4,14},{6,12},{8,2},{10,0},{12,6},{14,4},{16,26},{18,... | collective-permute-start | bytes 884744 | tf_op jit(solution)/shard_map/ppermute | solution.py:855
  97.3 30.3 %collective-permute-start.11 = (bf16[128,1152]{1,0:T(8,128)(2,1)}, bf16[128,1152]{1,0:T(8,128)(2,1)}, u32[]{:S(2)}, u32[]{:S(2)}) collective-permute-start(bf16[128,1152]{1,0:T(8,128)(2,1)} %get-tuple-element.98), channel_id=1, source_target_pairs={{0,12},{2,14},{4,8},{6,10},{8,4},{10,6},{12,0},{14,2},{16,28},{18,... | collective-permute-start | bytes 884744 | tf_op jit(solution)/shard_map/ppermute | solution.py:855
  113.2 15.1 %copy-start.32 = (bf16[256,512]{1,0:T(8,128)(2,1)}, bf16[256,512]{1,0:T(8,128)(2,1)S(1)}, u32[]{:S(2)}) copy-start(bf16[256,512]{1,0:T(8,128)(2,1)S(1)} %collective-permute-done.12.cross_ref) | copy-start | bytes 786436
  113.2 14.4 %collective-permute-start.13 = (bf16[256,512]{1,0:T(8,128)(2,1)S(1)}, bf16[256,512]{1,0:T(8,128)(2,1)S(1)}, u32[]{:S(2)}, u32[]{:S(2)}) collective-permute-start(bf16[256,512]{1,0:T(8,128)(2,1)S(1)} %collective-permute-done.12.cross_ref), channel_id=1, source_target_pairs={{0,1},{1,0},{2,3},{3,2},{4,5},{5,4},{6,7},{7,6},{8,9},{9,8},{10,11... | collective-permute-start | bytes 786440 | tf_op jit(solution)/shard_map/ppermute | solution.py:20
  114.6 19.0 %collective-permute-start.21 = (bf16[128,1152]{1,0:T(8,128)(2,1)}, bf16[128,1152]{1,0:T(8,128)(2,1)S(1)}, u32[]{:S(2)}, u32[]{:S(2)}) collective-permute-start(bf16[128,1152]{1,0:T(8,128)(2,1)} %get-tuple-element.111), channel_id=1, source_target_pairs={{0,14},{2,12},{4,10},{6,8},{8,6},{10,4},{12,2},{14,0},{16,30},{18,... | collective-permute-start | bytes 884744 | tf_op jit(solution)/shard_map/ppermute | solution.py:855
  131.6 3.5 collective-permute-start.14
  131.6 9.3 %collective-permute-start.15 = (bf16[128,1024]{1,0:T(8,128)(2,1)}, bf16[128,1024]{1,0:T(8,128)(2,1)S(1)}, u32[]{:S(2)}, u32[]{:S(2)}) collective-permute-start(bf16[128,1024]{1,0:T(8,128)(2,1)} %get-tuple-element.104), channel_id=1, source_target_pairs={{0,4},{2,6},{4,0},{6,2},{8,12},{10,14},{12,8},{14,10},{16,20},{18,... | collective-permute-start | bytes 786440 | tf_op jit(solution)/shard_map/ppermute | solution.py:855
  133.5 12.4 %collective-permute-start.16 = (bf16[128,1024]{1,0:T(8,128)(2,1)}, bf16[128,1024]{1,0:T(8,128)(2,1)S(1)}, u32[]{:S(2)}, u32[]{:S(2)}) collective-permute-start(bf16[128,1024]{1,0:T(8,128)(2,1)} %get-tuple-element.105), channel_id=1, source_target_pairs={{0,6},{2,4},{4,2},{6,0},{8,14},{10,12},{12,10},{14,8},{16,22},{18,... | collective-permute-start | bytes 786440 | tf_op jit(solution)/shard_map/ppermute | solution.py:855
  133.6 12.3 %collective-permute-start.17 = (bf16[128,1024]{1,0:T(8,128)(2,1)}, bf16[128,1024]{1,0:T(8,128)(2,1)S(1)}, u32[]{:S(2)}, u32[]{:S(2)}) collective-permute-start(bf16[128,1024]{1,0:T(8,128)(2,1)} %get-tuple-element.106), channel_id=1, source_target_pairs={{0,8},{2,10},{4,12},{6,14},{8,0},{10,2},{12,4},{14,6},{16,24},{18,... | collective-permute-start | bytes 786440 | tf_op jit(solution)/shard_map/ppermute | solution.py:855
  133.6 21.7 %copy-start.20 = (bf16[128,1152]{1,0:T(8,128)(2,1)}, bf16[128,1152]{1,0:T(8,128)(2,1)S(1)}, u32[]{:S(2)}) copy-start(bf16[128,1152]{1,0:T(8,128)(2,1)S(1)} %collective-permute-done.21.refs_15_) | copy-start | bytes 884740
  133.6 13.5 %collective-permute-start.18 = (bf16[128,1024]{1,0:T(8,128)(2,1)}, bf16[128,1024]{1,0:T(8,128)(2,1)S(1)}, u32[]{:S(2)}, u32[]{:S(2)}) collective-permute-start(bf16[128,1024]{1,0:T(8,128)(2,1)} %get-tuple-element.107), channel_id=1, source_target_pairs={{0,10},{2,8},{4,14},{6,12},{8,2},{10,0},{12,6},{14,4},{16,26},{18,... | collective-permute-start | bytes 786440 | tf_op jit(solution)/shard_map/ppermute | solution.py:855
  135.1 20.2 %copy-start.24 = (bf16[128,1024]{1,0:T(8,128)(2,1)}, bf16[128,1024]{1,0:T(8,128)(2,1)S(1)}, u32[]{:S(2)}) copy-start(bf16[128,1024]{1,0:T(8,128)(2,1)S(1)} %collective-permute-done.14.refs_1_) | copy-start | bytes 786436
  135.1 20.2 %collective-permute-start.19 = (bf16[128,1024]{1,0:T(8,128)(2,1)}, bf16[128,1024]{1,0:T(8,128)(2,1)S(1)}, u32[]{:S(2)}, u32[]{:S(2)}) collective-permute-start(bf16[128,1024]{1,0:T(8,128)(2,1)} %get-tuple-element.108), channel_id=1, source_target_pairs={{0,12},{2,14},{4,8},{6,10},{8,4},{10,6},{12,0},{14,2},{16,28},{18,... | collective-permute-start | bytes 786440 | tf_op jit(solution)/shard_map/ppermute | solution.py:855
  140.9 18.9 %collective-permute-start.20 = (bf16[128,1024]{1,0:T(8,128)(2,1)}, bf16[128,1024]{1,0:T(8,128)(2,1)}, u32[]{:S(2)}, u32[]{:S(2)}) collective-permute-start(bf16[128,1024]{1,0:T(8,128)(2,1)} %get-tuple-element.109), channel_id=1, source_target_pairs={{0,14},{2,12},{4,10},{6,8},{8,6},{10,4},{12,2},{14,0},{16,30},{18,... | collective-permute-start | bytes 786440 | tf_op jit(solution)/shard_map/ppermute | solution.py:855
  188.1 52.0 %copy-start.22 = (bf16[128,1024]{1,0:T(8,128)(2,1)S(1)}, bf16[128,1024]{1,0:T(8,128)(2,1)}, u32[]{:S(2)}) copy-start(bf16[128,1024]{1,0:T(8,128)(2,1)} %get-tuple-element.114) | copy-start | bytes 786436
  188.1 29.1 %all-to-all-start.1 = ((bf16[32,64,256]{2,1,0:T(8,128)(2,1)}), bf16[32,64,256]{2,1,0:T(8,128)(2,1)S(1)}, u32[]{:S(2)}, u32[]{:S(2)}) async-start(bf16[32,64,256]{2,1,0:T(8,128)(2,1)} %bitcast.37), calls=%async_computation.1 | async-start | bytes 2097152 | tf_op jit(solution)/shard_map/all_to_all | solution.py:919
  190.9 60.7 %copy-start.21 = (bf16[128,1024]{1,0:T(8,128)(2,1)S(1)}, bf16[128,1024]{1,0:T(8,128)(2,1)}, u32[]{:S(2)}) copy-start(bf16[128,1024]{1,0:T(8,128)(2,1)} %get-tuple-element.115) | copy-start | bytes 786436
  191.0 3.7 collective-permute-start.32
  191.2 18.1 %collective-permute-start.33 = (bf16[128,1024]{1,0:T(8,128)(2,1)S(1)}, bf16[128,1024]{1,0:T(8,128)(2,1)S(1)}, u32[]{:S(2)}, u32[]{:S(2)}) collective-permute-start(bf16[128,1024]{1,0:T(8,128)(2,1)S(1)} %copy-done.29), channel_id=1, source_target_pairs={{0,4},{2,6},{4,0},{6,2},{8,12},{10,14},{12,8},{14,10},{16,20},{18,... | collective-permute-start | bytes 786440 | tf_op jit(solution)/shard_map/ppermute | solution.py:855
  192.9 24.4 %collective-permute-start.34 = (bf16[128,1024]{1,0:T(8,128)(2,1)}, bf16[128,1024]{1,0:T(8,128)(2,1)S(1)}, u32[]{:S(2)}, u32[]{:S(2)}) collective-permute-start(bf16[128,1024]{1,0:T(8,128)(2,1)} %get-tuple-element.135), channel_id=1, source_target_pairs={{0,6},{2,4},{4,2},{6,0},{8,14},{10,12},{12,10},{14,8},{16,22},{18,... | collective-permute-start | bytes 786440 | tf_op jit(solution)/shard_map/ppermute | solution.py:855
  192.9 24.4 %collective-permute-start.35 = (bf16[128,1024]{1,0:T(8,128)(2,1)}, bf16[128,1024]{1,0:T(8,128)(2,1)S(1)}, u32[]{:S(2)}, u32[]{:S(2)}) collective-permute-start(bf16[128,1024]{1,0:T(8,128)(2,1)} %get-tuple-element.136), channel_id=1, source_target_pairs={{0,8},{2,10},{4,12},{6,14},{8,0},{10,2},{12,4},{14,6},{16,24},{18,... | collective-permute-start | bytes 786440 | tf_op jit(solution)/shard_map/ppermute | solution.py:855
  194.6 26.8 %collective-permute-start.36 = (bf16[128,1024]{1,0:T(8,128)(2,1)}, bf16[128,1024]{1,0:T(8,128)(2,1)S(1)}, u32[]{:S(2)}, u32[]{:S(2)}) collective-permute-start(bf16[128,1024]{1,0:T(8,128)(2,1)} %get-tuple-element.137), channel_id=1, source_target_pairs={{0,10},{2,8},{4,14},{6,12},{8,2},{10,0},{12,6},{14,4},{16,26},{18,... | collective-permute-start | bytes 786440 | tf_op jit(solution)/shard_map/ppermute | solution.py:855
  194.7 38.8 %copy-start.7 = (bf16[128,1024]{1,0:T(8,128)(2,1)}, bf16[128,1024]{1,0:T(8,128)(2,1)S(1)}, u32[]{:S(2)}) copy-start(bf16[128,1024]{1,0:T(8,128)(2,1)S(1)} %collective-permute-done.32.refs_1_) | copy-start | bytes 786436
  194.7 34.1 %collective-permute-start.37 = (bf16[128,1024]{1,0:T(8,128)(2,1)}, bf16[128,1024]{1,0:T(8,128)(2,1)S(1)}, u32[]{:S(2)}, u32[]{:S(2)}) collective-permute-start(bf16[128,1024]{1,0:T(8,128)(2,1)} %get-tuple-element.138), channel_id=1, source_target_pairs={{0,12},{2,14},{4,8},{6,10},{8,4},{10,6},{12,0},{14,2},{16,28},{18,... | collective-permute-start | bytes 786440 | tf_op jit(solution)/shard_map/ppermute | solution.py:855
  209.3 24.2 %copy-start.8 = (bf16[128,1024]{1,0:T(8,128)(2,1)}, bf16[128,1024]{1,0:T(8,128)(2,1)S(1)}, u32[]{:S(2)}) copy-start(bf16[128,1024]{1,0:T(8,128)(2,1)S(1)} %collective-permute-done.33.refs_2_) | copy-start | bytes 786436
  209.3 24.2 %collective-permute-start.38 = (bf16[128,1024]{1,0:T(8,128)(2,1)}, bf16[128,1024]{1,0:T(8,128)(2,1)S(1)}, u32[]{:S(2)}, u32[]{:S(2)}) collective-permute-start(bf16[128,1024]{1,0:T(8,128)(2,1)} %get-tuple-element.139), channel_id=1, source_target_pairs={{0,14},{2,12},{4,10},{6,8},{8,6},{10,4},{12,2},{14,0},{16,30},{18,... | collective-permute-start | bytes 786440 | tf_op jit(solution)/shard_map/ppermute | solution.py:855
  217.3 22.8 %copy-start.23 = (bf16[128,1024]{1,0:T(8,128)(2,1)S(1)}, bf16[128,1024]{1,0:T(8,128)(2,1)}, u32[]{:S(2)}) copy-start(bf16[128,1024]{1,0:T(8,128)(2,1)} %get-tuple-element.113) | copy-start | bytes 786436
  217.3 16.2 %copy-start.9 = (bf16[128,1024]{1,0:T(8,128)(2,1)}, bf16[128,1024]{1,0:T(8,128)(2,1)S(1)}, u32[]{:S(2)}) copy-start(bf16[128,1024]{1,0:T(8,128)(2,1)S(1)} %collective-permute-done.34.refs_3_) | copy-start | bytes 786436
  217.3 16.2 %copy-start.10 = (bf16[128,1024]{1,0:T(8,128)(2,1)}, bf16[128,1024]{1,0:T(8,128)(2,1)S(1)}, u32[]{:S(2)}) copy-start(bf16[128,1024]{1,0:T(8,128)(2,1)S(1)} %collective-permute-done.35.refs_4_) | copy-start | bytes 786436
  238.5 9.4 %collective-permute-start.40 = (bf16[256,512]{1,0:T(8,128)(2,1)}, bf16[256,512]{1,0:T(8,128)(2,1)S(1)}, u32[]{:S(2)}, u32[]{:S(2)}) collective-permute-start(bf16[256,512]{1,0:T(8,128)(2,1)} %get-tuple-element.143), channel_id=1, source_target_pairs={{0,1},{1,0},{2,3},{3,2},{4,5},{5,4},{6,7},{7,6},{8,9},{9,8},{10,11... | collective-permute-start | bytes 786440 | tf_op jit(solution)/shard_map/ppermute | solution.py:20
  240.1 11.5 %collective-permute-start.22 = (bf16[128,1024]{1,0:T(8,128)(2,1)S(1)}, bf16[128,1024]{1,0:T(8,128)(2,1)S(1)}, u32[]{:S(2)}, u32[]{:S(2)}) collective-permute-start(bf16[128,1024]{1,0:T(8,128)(2,1)S(1)} %copy-done.23), channel_id=1, source_target_pairs={{0,2},{2,0},{4,6},{6,4},{8,10},{10,8},{12,14},{14,12},{16,18},{18,... | collective-permute-start | bytes 786440 | tf_op jit(solution)/shard_map/ppermute | solution.py:855
  240.1 12.2 %collective-permute-start.23 = (bf16[128,1024]{1,0:T(8,128)(2,1)S(1)}, bf16[128,1024]{1,0:T(8,128)(2,1)S(1)}, u32[]{:S(2)}, u32[]{:S(2)}) collective-permute-start(bf16[128,1024]{1,0:T(8,128)(2,1)S(1)} %copy-done.22), channel_id=1, source_target_pairs={{0,4},{2,6},{4,0},{6,2},{8,12},{10,14},{12,8},{14,10},{16,20},{18,... | collective-permute-start | bytes 786440 | tf_op jit(solution)/shard_map/ppermute | solution.py:855
  240.7 12.9 %collective-permute-start.39 = (bf16[256,512]{1,0:T(8,128)(2,1)}, bf16[256,512]{1,0:T(8,128)(2,1)S(1)}, u32[]{:S(2)}, u32[]{:S(2)}) collective-permute-start(bf16[256,512]{1,0:T(8,128)(2,1)} %get-tuple-element.141), channel_id=1, source_target_pairs={{0,1},{1,0},{2,3},{3,2},{4,5},{5,4},{6,7},{7,6},{8,9},{9,8},{10,11... | collective-permute-start | bytes 786440 | tf_op jit(solution)/shard_map/ppermute | solution.py:20
  249.1 13.7 %collective-permute-start.41 = (bf16[256,512]{1,0:T(8,128)(2,1)S(1)}, bf16[256,512]{1,0:T(8,128)(2,1)S(1)}, u32[]{:S(2)}, u32[]{:S(2)}) collective-permute-start(bf16[256,512]{1,0:T(8,128)(2,1)S(1)} %add_convert_fusion.1), channel_id=1, source_target_pairs={{0,16},{2,18},{4,20},{6,22},{8,24},{10,26},{12,28},{14,30},{16,0},... | collective-permute-start | bytes 786440 | tf_op jit(solution)/shard_map/ppermute | solution.py:851
  251.6 12.4 %collective-permute-start.24 = (bf16[128,1024]{1,0:T(8,128)(2,1)S(1)}, bf16[128,1024]{1,0:T(8,128)(2,1)S(1)}, u32[]{:S(2)}, u32[]{:S(2)}) collective-permute-start(bf16[128,1024]{1,0:T(8,128)(2,1)S(1)} %copy-done.21), channel_id=1, source_target_pairs={{0,6},{2,4},{4,2},{6,0},{8,14},{10,12},{12,10},{14,8},{16,22},{18,... | collective-permute-start | bytes 786440 | tf_op jit(solution)/shard_map/ppermute | solution.py:855
  251.7 18.1 %collective-permute-start.25 = (bf16[128,1024]{1,0:T(8,128)(2,1)}, bf16[128,1024]{1,0:T(8,128)(2,1)}, u32[]{:S(2)}, u32[]{:S(2)}) collective-permute-start(bf16[128,1024]{1,0:T(8,128)(2,1)} %get-tuple-element.116), channel_id=1, source_target_pairs={{0,8},{2,10},{4,12},{6,14},{8,0},{10,2},{12,4},{14,6},{16,24},{18,... | collective-permute-start | bytes 786440 | tf_op jit(solution)/shard_map/ppermute | solution.py:855
  252.4 19.3 %collective-permute-start.26 = (bf16[128,1024]{1,0:T(8,128)(2,1)}, bf16[128,1024]{1,0:T(8,128)(2,1)}, u32[]{:S(2)}, u32[]{:S(2)}) collective-permute-start(bf16[128,1024]{1,0:T(8,128)(2,1)} %get-tuple-element.117), channel_id=1, source_target_pairs={{0,10},{2,8},{4,14},{6,12},{8,2},{10,0},{12,6},{14,4},{16,26},{18,... | collective-permute-start | bytes 786440 | tf_op jit(solution)/shard_map/ppermute | solution.py:855
  253.6 29.3 %collective-permute-start.27 = (bf16[128,1024]{1,0:T(8,128)(2,1)}, bf16[128,1024]{1,0:T(8,128)(2,1)}, u32[]{:S(2)}, u32[]{:S(2)}) collective-permute-start(bf16[128,1024]{1,0:T(8,128)(2,1)} %get-tuple-element.118), channel_id=1, source_target_pairs={{0,12},{2,14},{4,8},{6,10},{8,4},{10,6},{12,0},{14,2},{16,28},{18,... | collective-permute-start | bytes 786440 | tf_op jit(solution)/shard_map/ppermute | solution.py:855
  262.8 33.4 %collective-permute-start.28 = (bf16[128,1024]{1,0:T(8,128)(2,1)}, bf16[128,1024]{1,0:T(8,128)(2,1)}, u32[]{:S(2)}, u32[]{:S(2)}) collective-permute-start(bf16[128,1024]{1,0:T(8,128)(2,1)} %get-tuple-element.119), channel_id=1, source_target_pairs={{0,14},{2,12},{4,10},{6,8},{8,6},{10,4},{12,2},{14,0},{16,30},{18,... | collective-permute-start | bytes 786440 | tf_op jit(solution)/shard_map/ppermute | solution.py:855
  264.0 32.2 %collective-permute-start.42 = (bf16[256,512]{1,0:T(8,128)(2,1)S(1)}, bf16[256,512]{1,0:T(8,128)(2,1)}, u32[]{:S(2)}, u32[]{:S(2)}) collective-permute-start(bf16[256,512]{1,0:T(8,128)(2,1)S(1)} %add_convert_fusion.mixed_ref), channel_id=1, source_target_pairs={{0,1},{1,0},{2,3},{3,2},{4,5},{5,4},{6,7},{7,6},{8,9},{9,8},{10,11... | collective-permute-start | bytes 786440 | tf_op jit(solution)/shard_map/ppermute | solution.py:20
  265.6 72.8 %all-to-all-start.2 = ((bf16[32,2,64,256]{3,2,1,0:T(8,128)(2,1)}), bf16[32,2,64,256]{3,2,1,0:T(8,128)(2,1)S(1)}, u32[]{:S(2)}, u32[]{:S(2)}) async-start(bf16[32,2,64,256]{3,2,1,0:T(8,128)(2,1)} %bitcast.34), calls=%async_computation.2 | async-start | bytes 4194304 | tf_op jit(solution)/shard_map/all_to_all | solution.py:919
  269.5 114.8 %reduce-scatter.2.cloned.1.call-start = ((), (), s32[]{:S(2)}) async-start(), calls=%async_computation.6 | async-start | bytes 3620864 | tf_op jit(solution)/shard_map/reduce_scatter | solution.py:1023
  307.2 16.0 %copy-start.17 = (f32[8,256]{1,0:T(8,128)S(1)}, f32[8,256]{1,0:T(8,128)}, u32[]{:S(2)}) copy-start(f32[8,256]{1,0:T(8,128)} %get-tuple-element.155.inner_ref) | copy-start | bytes 24580
  311.6 10.3 %collective-permute-start.30 = (bf16[256,512]{1,0:T(8,128)(2,1)}, bf16[256,512]{1,0:T(8,128)(2,1)S(1)}, u32[]{:S(2)}, u32[]{:S(2)}) collective-permute-start(bf16[256,512]{1,0:T(8,128)(2,1)} %get-tuple-element.123), channel_id=1, source_target_pairs={{0,1},{1,0},{2,3},{3,2},{4,5},{5,4},{6,7},{7,6},{8,9},{9,8},{10,11... | collective-permute-start | bytes 786440 | tf_op jit(solution)/shard_map/ppermute | solution.py:20
  311.6 15.9 %collective-permute-start.29 = (bf16[256,512]{1,0:T(8,128)(2,1)}, bf16[256,512]{1,0:T(8,128)(2,1)S(1)}, u32[]{:S(2)}, u32[]{:S(2)}) collective-permute-start(bf16[256,512]{1,0:T(8,128)(2,1)} %get-tuple-element.121), channel_id=1, source_target_pairs={{0,1},{1,0},{2,3},{3,2},{4,5},{5,4},{6,7},{7,6},{8,9},{9,8},{10,11... | collective-permute-start | bytes 786440 | tf_op jit(solution)/shard_map/ppermute | solution.py:20
  323.0 11.2 %collective-permute-start.31 = (bf16[256,512]{1,0:T(8,128)(2,1)S(1)}, bf16[256,512]{1,0:T(8,128)(2,1)S(1)}, u32[]{:S(2)}, u32[]{:S(2)}) collective-permute-start(bf16[256,512]{1,0:T(8,128)(2,1)S(1)} %add_convert_fusion.2), channel_id=1, source_target_pairs={{0,16},{2,18},{4,20},{6,22},{8,24},{10,26},{12,28},{14,30},{16,0},... | collective-permute-start | bytes 786440 | tf_op jit(solution)/shard_map/ppermute | solution.py:851
  323.1 11.2 %collective-permute-start.43 = (bf16[256,512]{1,0:T(8,128)(2,1)}, bf16[256,512]{1,0:T(8,128)(2,1)S(1)}, u32[]{:S(2)}, u32[]{:S(2)}) collective-permute-start(bf16[256,512]{1,0:T(8,128)(2,1)} %get-tuple-element.154), channel_id=1, source_target_pairs={{0,1},{1,0},{2,3},{3,2},{4,5},{5,4},{6,7},{7,6},{8,9},{9,8},{10,11... | collective-permute-start | bytes 786440 | tf_op jit(solution)/shard_map/ppermute | solution.py:20
  323.2 11.1 %collective-permute-start.44 = (f32[8,256]{1,0:T(8,128)S(1)}, f32[8,256]{1,0:T(8,128)S(1)}, u32[]{:S(2)}, u32[]{:S(2)}) collective-permute-start(f32[8,256]{1,0:T(8,128)S(1)} %copy-done.17), channel_id=1, source_target_pairs={{0,1},{1,0},{2,3},{3,2},{4,5},{5,4},{6,7},{7,6},{8,9},{9,8},{10,11... | collective-permute-start | bytes 24584 | tf_op jit(solution)/shard_map/ppermute | solution.py:20
  338.5 24.8 %all-to-all-start.3 = ((bf16[16,16,1024]{2,1,0:T(8,128)(2,1)}), bf16[16,16,1024]{2,1,0:T(8,128)(2,1)}, u32[]{:S(2)}, u32[]{:S(2)}) async-start(bf16[16,16,1024]{2,1,0:T(8,128)(2,1)} %bitcast.36), calls=%async_computation.3 | async-start | bytes 1048576 | tf_op jit(solution)/shard_map/all_to_all | solution.py:1057
  365.9 29.9 %all-to-all-start.4 = ((bf16[16,16,1024]{2,1,0:T(8,128)(2,1)}), bf16[16,16,1024]{2,1,0:T(8,128)(2,1)S(1)}, u32[]{:S(2)}, u32[]{:S(2)}) async-start(bf16[16,16,1024]{2,1,0:T(8,128)(2,1)} %broadcast_select_fusion), calls=%async_computation.4 | async-start | bytes 1048576 | tf_op jit(solution)/shard_map/all_to_all | solution.py:1061
  385.0 8.6 %collective-permute-start.45 = (bf16[64,128]{1,0:T(8,128)(2,1)S(1)}, bf16[64,128]{1,0:T(8,128)(2,1)S(1)}, u32[]{:S(2)}, u32[]{:S(2)}) collective-permute-start(bf16[64,128]{1,0:T(8,128)(2,1)S(1)} %slice.52), channel_id=1, source_target_pairs={{0,1},{1,0},{2,3},{3,2},{4,5},{5,4},{6,7},{7,6},{8,9},{9,8},{10,11... | collective-permute-start | bytes 49160 | tf_op jit(solution)/shard_map/ppermute | solution.py:20
  (25 other events, 115.7 us)
Sparse Core Ops, SparseCore 0:
  307.3 76.9 reduce-scatter.1

commit v5 on v4

--- a/solution.py
+++ b/solution.py
@@ -1026,11 +1026,10 @@
         cuts.append(cuts[-1] + w.shape[1])
     small = share[:, cuts[3] :]
     small = small.astype(jnp.float32) + swap_tensor(small).astype(jnp.float32)
-    share = share.astype(jnp.float32)
-    output_part = share[:, : cuts[0]].T
-    query_part = share[:, cuts[0] : cuts[1]]
-    key_part = share[:, cuts[1] : cuts[2]]
-    value_part = share[:, cuts[2] : cuts[3]]
+    output_part = share[:, : cuts[0]].T.astype(jnp.float32)
+    query_part = share[:, cuts[0] : cuts[1]].astype(jnp.float32)
+    key_part = share[:, cuts[1] : cuts[2]].astype(jnp.float32)
+    value_part = share[:, cuts[2] : cuts[3]].astype(jnp.float32)
     router_share = small[:, :expert_count]
     attn_gain_part = small[:, expert_count]
     expert_gain_part = small[:, expert_count + 1]

time: 405 us -> 403 us (level)
  no operation moved by 1% of the time
where the time goes in v5:
time: 403 us; the launch traced here: 402 us
  waiting for transfers between devices  219 us (54%)
  starting transfers between devices  71.5 us (18%)
  Pallas kernels  68.6 us (17%)
  other arithmetic  17.6 us (4%)
  between operations  14.5 us (4%)
  local copies, waits for them, and re-layouts  10.4 us (3%)
    ppermute x28, waiting for transfers between devices, spread(): lax.ppermute(blocks[s], 'dp', [(i, i ^ s) for i in range(devices)])  89.7 us
    ppermute x13, waiting for transfers between devices, swap_tensor(): return lax.ppermute(values, 'tensor', [(0, 1), (1, 0)])  55.8 us
    ppermute x5, waiting for transfers between devices, cross(): return lax.ppermute(values, 'dp', [(i, i ^ near) for i in range(devices)])  37.5 us
    ppermute x28, starting transfers between devices, spread(): lax.ppermute(blocks[s], 'dp', [(i, i ^ s) for i in range(devices)])  20.5 us
    ppermute x13, starting transfers between devices, swap_tensor(): return lax.ppermute(values, 'tensor', [(0, 1), (1, 0)])  18.9 us
    pallas_call x1, Pallas kernels, run_expert(): pl.pallas_call(functools.partial(expert_kernel, near), grid=(steps,), in_...  18.5 us
    all_to_all x1, waiting for transfers between devices, local(): lax.all_to_all(moved.reshape(devices, piece_rows, width), 'dp', split_axi...  17.9 us
    pallas_call x1, Pallas kernels, attend_back(): pl.pallas_call(attend_back_kernel, in_specs=[SMEM] + [VMEM] * len(values)...  11 us
  transfers between devices with their start and end apart: 52, of which 26 were waited for; matrix products, arithmetic and copies ran while one was open for 5% of the time, Pallas kernels for 9%

profile of v5, /device:TPU:0, one launch (start us, length us, event | category | flops | bytes accessed | tf_op | source)
XLA Modules:
  0.0 401.7 jit_solution(5523046205798951557)
XLA Ops:
  7.2 3.0 collective-permute-start
  10.2 2.6 collective-permute-start.3
  13.3 3.8 pad_maximum_fusion
  17.1 7.9 %collective-permute-done.2.partner_ref = s32[8,256]{1,0:T(8,128)S(1)} collective-permute-done((s32[8,256]{1,0:T(8,128)}, s32[8,256]{1,0:T(8,128)S(1)}, u32[]{:S(2)}, u32[]{:S(2)}) %collective-permute-start.2) | collective-permute-done | bytes 8224 | tf_op jit(solution)/shard_map/ppermute | solution.py:851
  25.8 4.8 %all-to-all-start = ((bf16[32,3,64,256]{3,2,1,0:T(8,128)(2,1)}), bf16[32,3,64,256]{3,2,1,0:T(8,128)(2,1)S(1)}, u32[]{:S(2)}, u32[]{:S(2)}) async-start(bf16[32,3,64,256]{3,2,1,0:T(8,128)(2,1)} %pad_maximum_fusion), calls=%async_computation | async-start | bytes 6291456 | tf_op jit(solution)/shard_map/all_to_all | solution.py:899
  31.2 2.1 tables.1
  33.3 6.8 %attend.1 = (bf16[256,1024]{1,0:T(8,128)(2,1)}, bf16[256,1024]{1,0:T(8,128)(2,1)}, bf16[256,512]{1,0:T(8,128)(2,1)}, bf16[256,256]{1,0:T(8,128)(2,1)}, bf16[256,...) custom-call(s32[7]{0:T(128)} %get-tuple-element.86.facts_ref, bf16[256,512]{1,0:T(8,128)(2,1)} %own_ref.7, ...), custom_call_target="tpu_custom_call" | custom-call | flops 1073741824 | bytes 8388608 | tf_op jit(solution)/shard_map/attend/pallas_call | solution.py:576
  40.1 1.8 collective-permute-start.1
  42.2 38.4 %collective-permute-done.5.refs_3_ = bf16[256,512]{1,0:T(8,128)(2,1)S(1)} collective-permute-done((bf16[256,512]{1,0:T(8,128)(2,1)}, bf16[256,512]{1,0:T(8,128)(2,1)S(1)}, u32[]{:S(2)}, u32[]{:S(2)}) %collective-permute-start.5) | collective-permute-done | bytes 262176 | tf_op jit(solution)/shard_map/ppermute | solution.py:20
  81.3 3.9 dispatch_cot.1
  86.0 2.9 mix.1
  88.9 4.9 %collective-permute-start.12 = (bf16[256,512]{1,0:T(8,128)(2,1)}, bf16[256,512]{1,0:T(8,128)(2,1)S(1)}, u32[]{:S(2)}, u32[]{:S(2)}) collective-permute-start(bf16[256,512]{1,0:T(8,128)(2,1)} %get-tuple-element.101), channel_id=1, source_target_pairs={{0,16},{2,18},{4,20},{6,22},{8,24},{10,26},{12,28},{14,30},{16,0},... | collective-permute-start | bytes 786440 | tf_op jit(solution)/shard_map/ppermute | solution.py:851
  95.4 2.0 collective-permute-start.10
  97.8 15.4 %collective-permute-done.12.cross_ref = bf16[256,512]{1,0:T(8,128)(2,1)S(1)} collective-permute-done((bf16[256,512]{1,0:T(8,128)(2,1)}, bf16[256,512]{1,0:T(8,128)(2,1)S(1)}, u32[]{:S(2)}, u32[]{:S(2)}) %collective-permute-start.12) | collective-permute-done | bytes 262176 | tf_op jit(solution)/shard_map/ppermute | solution.py:851
  115.4 5.6 %collective-permute-done.10.refs_13_ = bf16[128,1152]{1,0:T(8,128)(2,1)} collective-permute-done((bf16[128,1152]{1,0:T(8,128)(2,1)}, bf16[128,1152]{1,0:T(8,128)(2,1)}, u32[]{:S(2)}, u32[]{:S(2)}) %collective-permute-start.10) | collective-permute-done | bytes 294944 | tf_op jit(solution)/shard_map/ppermute | solution.py:855
  121.0 6.6 %collective-permute-done.11.refs_14_ = bf16[128,1152]{1,0:T(8,128)(2,1)} collective-permute-done((bf16[128,1152]{1,0:T(8,128)(2,1)}, bf16[128,1152]{1,0:T(8,128)(2,1)}, u32[]{:S(2)}, u32[]{:S(2)}) %collective-permute-start.11) | collective-permute-done | bytes 294944 | tf_op jit(solution)/shard_map/ppermute | solution.py:855
  128.3 3.3 dispatch_rows.1
  131.6 1.9 collective-permute-start.15
  133.7 1.5 collective-permute-start.18
  135.2 1.8 collective-permute-start.19
  136.9 4.0 %collective-permute-done.15.refs_2_ = bf16[128,1024]{1,0:T(8,128)(2,1)S(1)} collective-permute-done((bf16[128,1024]{1,0:T(8,128)(2,1)}, bf16[128,1024]{1,0:T(8,128)(2,1)S(1)}, u32[]{:S(2)}, u32[]{:S(2)}) %collective-permute-start.15) | collective-permute-done | bytes 262176 | tf_op jit(solution)/shard_map/ppermute | solution.py:855
  141.0 5.0 %collective-permute-done.16.refs_3_ = bf16[128,1024]{1,0:T(8,128)(2,1)S(1)} collective-permute-done((bf16[128,1024]{1,0:T(8,128)(2,1)}, bf16[128,1024]{1,0:T(8,128)(2,1)S(1)}, u32[]{:S(2)}, u32[]{:S(2)}) %collective-permute-start.16) | collective-permute-done | bytes 262176 | tf_op jit(solution)/shard_map/ppermute | solution.py:855
  147.1 8.3 %collective-permute-done.19.refs_6_ = bf16[128,1024]{1,0:T(8,128)(2,1)S(1)} collective-permute-done((bf16[128,1024]{1,0:T(8,128)(2,1)}, bf16[128,1024]{1,0:T(8,128)(2,1)S(1)}, u32[]{:S(2)}, u32[]{:S(2)}) %collective-permute-start.19) | collective-permute-done | bytes 262176 | tf_op jit(solution)/shard_map/ppermute | solution.py:855
  156.1 3.7 collective-permute-done.20.refs_7_
  159.9 1.6 copy-done
  161.5 18.5 %expert_rows.1 = (bf16[128,1024]{1,0:T(8,128)(2,1)}, bf16[128,1024]{1,0:T(8,128)(2,1)}, bf16[128,1024]{1,0:T(8,128)(2,1)}, bf16[128,1024]{1,0:T(8,128)(2,1)}, bf...) custom-call(s32[7]{0:T(128)} %get-tuple-element.86.facts_ref, ...), custom_call_target="tpu_custom_call" | custom-call | flops 6442450944 | bytes 16777216 | tf_op jit(solution)/shard_map/expert_rows/pallas_call | solution.py:324
  180.0 8.1 %expert_grads.1 = (bf16[16,2,2,64,256]{4,3,2,1,0:T(8,128)(2,1)}, bf16[16,2,64,256]{3,2,1,0:T(8,128)(2,1)}, f32[32,1024]{1,0:T(8,128)}) custom-call(bf16[1024,1024]{1,0:T(8,128)(2,1)} %get-tuple-element.124.rows_ref, bf16[1024,512]{1,0:T(8,128)(2,1)} %get-tuple-element.125.hidden_ref, bf16[1024,512]{1,0:T(8,128)(2,1)} %get-tuple-element.126.gate_grad_ref, ...), custom_call_target="tpu_custom_call" | custom-call | flops 3221225472 | bytes 12582912 | tf_op jit(solution)/shard_map/expert_grads/pallas_call | solution.py:401
  188.1 2.8 all-to-all-start.1
  191.2 1.6 collective-permute-start.33
  192.9 1.7 collective-permute-start.35
  194.7 2.6 collective-permute-start.37
  197.3 12.0 %collective-permute-done.33.refs_2_ = bf16[128,1024]{1,0:T(8,128)(2,1)S(1)} collective-permute-done((bf16[128,1024]{1,0:T(8,128)(2,1)S(1)}, bf16[128,1024]{1,0:T(8,128)(2,1)S(1)}, u32[]{:S(2)}, u32[]{:S(2)}) %collective-permute-start.33) | collective-permute-done | bytes 262176 | tf_op jit(solution)/shard_map/ppermute | solution.py:855
  210.0 7.3 %all-to-all-done.1 = bf16[32,64,256]{2,1,0:T(8,128)(2,1)S(1)} async-done(((bf16[32,64,256]{2,1,0:T(8,128)(2,1)}), bf16[32,64,256]{2,1,0:T(8,128)(2,1)S(1)}, u32[]{:S(2)}, u32[]{:S(2)}) %all-to-all-start.1) | async-done | bytes 1048608 | tf_op jit(solution)/shard_map/all_to_all | solution.py:919
  217.3 4.0 %collective-permute-done.36.refs_5_ = bf16[128,1024]{1,0:T(8,128)(2,1)S(1)} collective-permute-done((bf16[128,1024]{1,0:T(8,128)(2,1)}, bf16[128,1024]{1,0:T(8,128)(2,1)S(1)}, u32[]{:S(2)}, u32[]{:S(2)}) %collective-permute-start.36) | collective-permute-done | bytes 262176 | tf_op jit(solution)/shard_map/ppermute | solution.py:855
  221.3 7.5 %collective-permute-done.37.refs_6_ = bf16[128,1024]{1,0:T(8,128)(2,1)S(1)} collective-permute-done((bf16[128,1024]{1,0:T(8,128)(2,1)}, bf16[128,1024]{1,0:T(8,128)(2,1)S(1)}, u32[]{:S(2)}, u32[]{:S(2)}) %collective-permute-start.37) | collective-permute-done | bytes 262176 | tf_op jit(solution)/shard_map/ppermute | solution.py:855
  228.8 4.7 %collective-permute-done.38.refs_7_ = bf16[128,1024]{1,0:T(8,128)(2,1)S(1)} collective-permute-done((bf16[128,1024]{1,0:T(8,128)(2,1)}, bf16[128,1024]{1,0:T(8,128)(2,1)S(1)}, u32[]{:S(2)}, u32[]{:S(2)}) %collective-permute-start.38) | collective-permute-done | bytes 262176 | tf_op jit(solution)/shard_map/ppermute | solution.py:855
  234.2 4.3 %combine_rows.3 = (f32[256,512]{1,0:T(8,128)}, bf16[256,512]{1,0:T(8,128)(2,1)}, f32[256,512]{1,0:T(8,128)}, bf16[256,512]{1,0:T(8,128)(2,1)}) custom-call(s32[7]{0:T(128)} %get-tuple-element.86.facts_ref, bf16[2,512,256]{2,1,0:T(8,128)(2,1)} %get-tuple-element.131.hot_ref, bf16[128,1024]{1,0:T(8,128)(2,1)} %get-tuple-element.132.refs_0_, ...), custom_call_target="tpu_custom_call" | custom-call | flops 536870912 | bytes 4194304 | tf_op jit(solution)/shard_map/combine_rows/pallas_call | solution.py:190
  238.5 1.6 collective-permute-start.40
  241.2 6.7 %collective-permute-done.40 = bf16[256,512]{1,0:T(8,128)(2,1)S(1)} collective-permute-done((bf16[256,512]{1,0:T(8,128)(2,1)}, bf16[256,512]{1,0:T(8,128)(2,1)S(1)}, u32[]{:S(2)}, u32[]{:S(2)}) %collective-permute-start.40) | collective-permute-done | bytes 262176 | tf_op jit(solution)/shard_map/ppermute | solution.py:20
  249.1 2.6 collective-permute-start.41
  253.6 1.6 collective-permute-start.27
  255.2 7.6 %collective-permute-done.41 = bf16[256,512]{1,0:T(8,128)(2,1)S(1)} collective-permute-done((bf16[256,512]{1,0:T(8,128)(2,1)S(1)}, bf16[256,512]{1,0:T(8,128)(2,1)S(1)}, u32[]{:S(2)}, u32[]{:S(2)}) %collective-permute-start.41) | collective-permute-done | bytes 262176 | tf_op jit(solution)/shard_map/ppermute | solution.py:851
  264.0 1.6 collective-permute-start.42
  265.6 3.9 all-to-all-start.2
  269.8 1.9 collective-permute-done.26.refs_5_
  271.7 11.2 %collective-permute-done.27.refs_6_ = bf16[128,1024]{1,0:T(8,128)(2,1)} collective-permute-done((bf16[128,1024]{1,0:T(8,128)(2,1)}, bf16[128,1024]{1,0:T(8,128)(2,1)}, u32[]{:S(2)}, u32[]{:S(2)}) %collective-permute-start.27) | collective-permute-done | bytes 262176 | tf_op jit(solution)/shard_map/ppermute | solution.py:855
  282.9 13.3 %collective-permute-done.28.refs_7_ = bf16[128,1024]{1,0:T(8,128)(2,1)} collective-permute-done((bf16[128,1024]{1,0:T(8,128)(2,1)}, bf16[128,1024]{1,0:T(8,128)(2,1)}, u32[]{:S(2)}, u32[]{:S(2)}) %collective-permute-start.28) | collective-permute-done | bytes 262176 | tf_op jit(solution)/shard_map/ppermute | solution.py:855
  296.2 11.0 %attend_back.1 = (bf16[1024,1664]{1,0:T(8,128)(2,1)}, f32[256,512]{1,0:T(8,128)}, bf16[256,512]{1,0:T(8,128)(2,1)}, f32[256,512]{1,0:T(8,128)}, f32[8,256]{1,0:T(8,128)}) custom-call(s32[7]{0:T(128)} %get-tuple-element.86.facts_ref, bf16[256,512]{1,0:T(8,128)(2,1)} %copy-done.3, bf16[256,512]{1,0:T(8,128)(2,1)} %collective-permute-done.42.mixed_away_ref, ...), custom_call_target="tpu_custom_call" | custom-call | flops 4294967296 | bytes 14680064 | tf_op jit(solution)/shard_map/attend_back/pallas_call | solution.py:743
  307.2 4.3 %combine_rows.2 = (f32[256,512]{1,0:T(8,128)}, bf16[256,512]{1,0:T(8,128)(2,1)}, f32[256,512]{1,0:T(8,128)}, bf16[256,512]{1,0:T(8,128)(2,1)}) custom-call(s32[7]{0:T(128)} %get-tuple-element.86.facts_ref, bf16[2,512,256]{2,1,0:T(8,128)(2,1)} %get-tuple-element.131.hot_ref, bf16[128,1024]{1,0:T(8,128)(2,1)} %get-tuple-element.112.refs_0_, ...), custom_call_target="tpu_custom_call" | custom-call | flops 536870912 | bytes 4194304 | tf_op jit(solution)/shard_map/combine_rows/pallas_call | solution.py:190
  311.6 2.0 collective-permute-start.29
  313.6 8.4 %collective-permute-done.30 = bf16[256,512]{1,0:T(8,128)(2,1)S(1)} collective-permute-done((bf16[256,512]{1,0:T(8,128)(2,1)}, bf16[256,512]{1,0:T(8,128)(2,1)S(1)}, u32[]{:S(2)}, u32[]{:S(2)}) %collective-permute-start.30) | collective-permute-done | bytes 262176 | tf_op jit(solution)/shard_map/ppermute | solution.py:20
  323.3 2.0 collective-permute-start.44
  325.3 2.3 collective-permute-done.29.moe_recv_ref
  327.6 6.6 %collective-permute-done.31.moe_cross_ref = bf16[256,512]{1,0:T(8,128)(2,1)S(1)} collective-permute-done((bf16[256,512]{1,0:T(8,128)(2,1)S(1)}, bf16[256,512]{1,0:T(8,128)(2,1)S(1)}, u32[]{:S(2)}, u32[]{:S(2)}) %collective-permute-start.31) | collective-permute-done | bytes 262176 | tf_op jit(solution)/shard_map/ppermute | solution.py:851
  335.0 3.4 finish.1
  338.4 5.2 %all-to-all-start.3 = ((bf16[16,16,1024]{2,1,0:T(8,128)(2,1)}), bf16[16,16,1024]{2,1,0:T(8,128)(2,1)}, u32[]{:S(2)}, u32[]{:S(2)}) async-start(bf16[16,16,1024]{2,1,0:T(8,128)(2,1)} %bitcast.36), calls=%async_computation.3 | async-start | bytes 1048576 | tf_op jit(solution)/shard_map/all_to_all | solution.py:1056
  343.7 1.6 convert_bitcast_fusion
  345.2 17.9 %all-to-all-done.3 = bf16[16,16,1024]{2,1,0:T(8,128)(2,1)} async-done(((bf16[16,16,1024]{2,1,0:T(8,128)(2,1)}), bf16[16,16,1024]{2,1,0:T(8,128)(2,1)}, u32[]{:S(2)}, u32[]{:S(2)}) %all-to-all-start.3) | async-done | bytes 524320 | tf_op jit(solution)/shard_map/all_to_all | solution.py:1056
  363.1 1.6 gather_fusion
  365.7 5.0 %all-to-all-start.4 = ((bf16[16,16,1024]{2,1,0:T(8,128)(2,1)}), bf16[16,16,1024]{2,1,0:T(8,128)(2,1)S(1)}, u32[]{:S(2)}, u32[]{:S(2)}) async-start(bf16[16,16,1024]{2,1,0:T(8,128)(2,1)} %broadcast_select_fusion), calls=%async_computation.4 | async-start | bytes 1048576 | tf_op jit(solution)/shard_map/all_to_all | solution.py:1060
  370.7 2.6 fusion
  373.2 10.8 %reduce-scatter.2.cloned.1.call-done = bf16[64,1664]{1,0:T(8,128)(2,1)} async-done(((bf16[1024,1664]{1,0:T(8,128)(2,1)}), bf16[64,1664]{1,0:T(8,128)(2,1)}) %reduce-scatter.2.cloned.1.call-update) | async-done | bytes 213008 | tf_op jit(solution)/shard_map/reduce_scatter | solution.py:1023
  384.8 4.0 collective-permute-start.45
  388.8 1.6 convert_bitcast_fusion.1
  (145 shorter events, 26.2 us)
Async XLA Ops:
  7.2 17.9 %collective-permute-start = (bf16[256,512]{1,0:T(8,128)(2,1)}, bf16[256,512]{1,0:T(8,128)(2,1)S(1)}, u32[]{:S(2)}, u32[]{:S(2)}) collective-permute-start(bf16[256,512]{1,0:T(8,128)(2,1)} %own_ref.7), channel_id=1, source_target_pairs={{0,1},{1,0},{2,3},{3,2},{4,5},{5,4},{6,7},{7,6},{8,9},{9,8},{10,11... | collective-permute-start | bytes 786440 | tf_op jit(solution)/shard_map/ppermute | solution.py:20
  10.2 14.9 %collective-permute-start.3 = (bf16[256,512]{1,0:T(8,128)(2,1)}, bf16[256,512]{1,0:T(8,128)(2,1)}, u32[]{:S(2)}, u32[]{:S(2)}) collective-permute-start(bf16[256,512]{1,0:T(8,128)(2,1)} %cot_ref.1), channel_id=1, source_target_pairs={{0,16},{2,18},{4,20},{6,22},{8,24},{10,26},{12,28},{14,30},{16,0},... | collective-permute-start | bytes 786440 | tf_op jit(solution)/shard_map/ppermute | solution.py:851
  12.8 12.3 %collective-permute-start.4 = (bf16[256,512]{1,0:T(8,128)(2,1)}, bf16[256,512]{1,0:T(8,128)(2,1)}, u32[]{:S(2)}, u32[]{:S(2)}) collective-permute-start(bf16[256,512]{1,0:T(8,128)(2,1)} %cot_ref.1), channel_id=1, source_target_pairs={{0,1},{1,0},{2,3},{3,2},{4,5},{5,4},{6,7},{7,6},{8,9},{9,8},{10,11... | collective-permute-start | bytes 786440 | tf_op jit(solution)/shard_map/ppermute | solution.py:20
  13.3 11.7 %collective-permute-start.2 = (s32[8,256]{1,0:T(8,128)}, s32[8,256]{1,0:T(8,128)S(1)}, u32[]{:S(2)}, u32[]{:S(2)}) collective-permute-start(s32[8,256]{1,0:T(8,128)} %bitcast.48), channel_id=1, source_target_pairs={{0,16},{2,18},{4,20},{6,22},{8,24},{10,26},{12,28},{14,30},{16,0},... | collective-permute-start | bytes 24584 | tf_op jit(solution)/shard_map/ppermute | solution.py:851
  25.8 134.1 %all-to-all-start = ((bf16[32,3,64,256]{3,2,1,0:T(8,128)(2,1)}), bf16[32,3,64,256]{3,2,1,0:T(8,128)(2,1)S(1)}, u32[]{:S(2)}, u32[]{:S(2)}) async-start(bf16[32,3,64,256]{3,2,1,0:T(8,128)(2,1)} %pad_maximum_fusion), calls=%async_computation | async-start | bytes 6291456 | tf_op jit(solution)/shard_map/all_to_all | solution.py:899
  40.1 45.2 %collective-permute-start.1 = (bf16[256,1024]{1,0:T(8,128)(2,1)}, bf16[256,1024]{1,0:T(8,128)(2,1)S(1)}, u32[]{:S(2)}, u32[]{:S(2)}) collective-permute-start(bf16[256,1024]{1,0:T(8,128)(2,1)} %get-tuple-element.89.part_ref), channel_id=1, source_target_pairs={{0,1},{1,0},{2,3},{3,2},{4,5},{5,4},{6,7},{7,6},{8,9},{9,8},{10,11... | collective-permute-start | bytes 1572872 | tf_op jit(solution)/shard_map/ppermute | solution.py:20
  41.9 38.7 %collective-permute-start.5 = (bf16[256,512]{1,0:T(8,128)(2,1)}, bf16[256,512]{1,0:T(8,128)(2,1)S(1)}, u32[]{:S(2)}, u32[]{:S(2)}) collective-permute-start(bf16[256,512]{1,0:T(8,128)(2,1)} %collective-permute-done.3.refs_1_), channel_id=1, source_target_pairs={{0,1},{1,0},{2,3},{3,2},{4,5},{5,4},{6,7},{7,6},{8,9},{9,8},{10,11... | collective-permute-start | bytes 786440 | tf_op jit(solution)/shard_map/ppermute | solution.py:20
  85.2 10.2 %collective-permute-start.6 = (bf16[128,1152]{1,0:T(8,128)(2,1)}, bf16[128,1152]{1,0:T(8,128)(2,1)S(1)}, u32[]{:S(2)}, u32[]{:S(2)}) collective-permute-start(bf16[128,1152]{1,0:T(8,128)(2,1)} %get-tuple-element.93), channel_id=1, source_target_pairs={{0,2},{2,0},{4,6},{6,4},{8,10},{10,8},{12,14},{14,12},{16,18},{18,... | collective-permute-start | bytes 884744 | tf_op jit(solution)/shard_map/ppermute | solution.py:855
  85.2 12.2 %collective-permute-start.7 = (bf16[128,1152]{1,0:T(8,128)(2,1)}, bf16[128,1152]{1,0:T(8,128)(2,1)}, u32[]{:S(2)}, u32[]{:S(2)}) collective-permute-start(bf16[128,1152]{1,0:T(8,128)(2,1)} %get-tuple-element.94), channel_id=1, source_target_pairs={{0,4},{2,6},{4,0},{6,2},{8,12},{10,14},{12,8},{14,10},{16,20},{18,... | collective-permute-start | bytes 884744 | tf_op jit(solution)/shard_map/ppermute | solution.py:855
  88.9 24.3 %collective-permute-start.12 = (bf16[256,512]{1,0:T(8,128)(2,1)}, bf16[256,512]{1,0:T(8,128)(2,1)S(1)}, u32[]{:S(2)}, u32[]{:S(2)}) collective-permute-start(bf16[256,512]{1,0:T(8,128)(2,1)} %get-tuple-element.101), channel_id=1, source_target_pairs={{0,16},{2,18},{4,20},{6,22},{8,24},{10,26},{12,28},{14,30},{16,0},... | collective-permute-start | bytes 786440 | tf_op jit(solution)/shard_map/ppermute | solution.py:851
  93.9 20.7 %collective-permute-start.8 = (bf16[128,1152]{1,0:T(8,128)(2,1)}, bf16[128,1152]{1,0:T(8,128)(2,1)}, u32[]{:S(2)}, u32[]{:S(2)}) collective-permute-start(bf16[128,1152]{1,0:T(8,128)(2,1)} %get-tuple-element.95), channel_id=1, source_target_pairs={{0,6},{2,4},{4,2},{6,0},{8,14},{10,12},{12,10},{14,8},{16,22},{18,... | collective-permute-start | bytes 884744 | tf_op jit(solution)/shard_map/ppermute | solution.py:855
  95.4 20.0 %collective-permute-start.9 = (bf16[128,1152]{1,0:T(8,128)(2,1)}, bf16[128,1152]{1,0:T(8,128)(2,1)}, u32[]{:S(2)}, u32[]{:S(2)}) collective-permute-start(bf16[128,1152]{1,0:T(8,128)(2,1)} %get-tuple-element.96), channel_id=1, source_target_pairs={{0,8},{2,10},{4,12},{6,14},{8,0},{10,2},{12,4},{14,6},{16,24},{18,... | collective-permute-start | bytes 884744 | tf_op jit(solution)/shard_map/ppermute | solution.py:855
  95.4 64.5 %copy-start.19 = (bf16[128,1152]{1,0:T(8,128)(2,1)}, bf16[128,1152]{1,0:T(8,128)(2,1)S(1)}, u32[]{:S(2)}) copy-start(bf16[128,1152]{1,0:T(8,128)(2,1)S(1)} %collective-permute-done.6.refs_9_) | copy-start | bytes 884740
  95.4 25.6 %collective-permute-start.10 = (bf16[128,1152]{1,0:T(8,128)(2,1)}, bf16[128,1152]{1,0:T(8,128)(2,1)}, u32[]{:S(2)}, u32[]{:S(2)}) collective-permute-start(bf16[128,1152]{1,0:T(8,128)(2,1)} %get-tuple-element.97), channel_id=1, source_target_pairs={{0,10},{2,8},{4,14},{6,12},{8,2},{10,0},{12,6},{14,4},{16,26},{18,... | collective-permute-start | bytes 884744 | tf_op jit(solution)/shard_map/ppermute | solution.py:855
  97.3 30.3 %collective-permute-start.11 = (bf16[128,1152]{1,0:T(8,128)(2,1)}, bf16[128,1152]{1,0:T(8,128)(2,1)}, u32[]{:S(2)}, u32[]{:S(2)}) collective-permute-start(bf16[128,1152]{1,0:T(8,128)(2,1)} %get-tuple-element.98), channel_id=1, source_target_pairs={{0,12},{2,14},{4,8},{6,10},{8,4},{10,6},{12,0},{14,2},{16,28},{18,... | collective-permute-start | bytes 884744 | tf_op jit(solution)/shard_map/ppermute | solution.py:855
  113.2 15.1 %copy-start.32 = (bf16[256,512]{1,0:T(8,128)(2,1)}, bf16[256,512]{1,0:T(8,128)(2,1)S(1)}, u32[]{:S(2)}) copy-start(bf16[256,512]{1,0:T(8,128)(2,1)S(1)} %collective-permute-done.12.cross_ref) | copy-start | bytes 786436
  113.2 14.4 %collective-permute-start.13 = (bf16[256,512]{1,0:T(8,128)(2,1)S(1)}, bf16[256,512]{1,0:T(8,128)(2,1)S(1)}, u32[]{:S(2)}, u32[]{:S(2)}) collective-permute-start(bf16[256,512]{1,0:T(8,128)(2,1)S(1)} %collective-permute-done.12.cross_ref), channel_id=1, source_target_pairs={{0,1},{1,0},{2,3},{3,2},{4,5},{5,4},{6,7},{7,6},{8,9},{9,8},{10,11... | collective-permute-start | bytes 786440 | tf_op jit(solution)/shard_map/ppermute | solution.py:20
  114.6 19.0 %collective-permute-start.21 = (bf16[128,1152]{1,0:T(8,128)(2,1)}, bf16[128,1152]{1,0:T(8,128)(2,1)S(1)}, u32[]{:S(2)}, u32[]{:S(2)}) collective-permute-start(bf16[128,1152]{1,0:T(8,128)(2,1)} %get-tuple-element.111), channel_id=1, source_target_pairs={{0,14},{2,12},{4,10},{6,8},{8,6},{10,4},{12,2},{14,0},{16,30},{18,... | collective-permute-start | bytes 884744 | tf_op jit(solution)/shard_map/ppermute | solution.py:855
  131.6 3.5 collective-permute-start.14
  131.6 9.3 %collective-permute-start.15 = (bf16[128,1024]{1,0:T(8,128)(2,1)}, bf16[128,1024]{1,0:T(8,128)(2,1)S(1)}, u32[]{:S(2)}, u32[]{:S(2)}) collective-permute-start(bf16[128,1024]{1,0:T(8,128)(2,1)} %get-tuple-element.104), channel_id=1, source_target_pairs={{0,4},{2,6},{4,0},{6,2},{8,12},{10,14},{12,8},{14,10},{16,20},{18,... | collective-permute-start | bytes 786440 | tf_op jit(solution)/shard_map/ppermute | solution.py:855
  133.5 12.5 %collective-permute-start.16 = (bf16[128,1024]{1,0:T(8,128)(2,1)}, bf16[128,1024]{1,0:T(8,128)(2,1)S(1)}, u32[]{:S(2)}, u32[]{:S(2)}) collective-permute-start(bf16[128,1024]{1,0:T(8,128)(2,1)} %get-tuple-element.105), channel_id=1, source_target_pairs={{0,6},{2,4},{4,2},{6,0},{8,14},{10,12},{12,10},{14,8},{16,22},{18,... | collective-permute-start | bytes 786440 | tf_op jit(solution)/shard_map/ppermute | solution.py:855
  133.6 12.4 %collective-permute-start.17 = (bf16[128,1024]{1,0:T(8,128)(2,1)}, bf16[128,1024]{1,0:T(8,128)(2,1)S(1)}, u32[]{:S(2)}, u32[]{:S(2)}) collective-permute-start(bf16[128,1024]{1,0:T(8,128)(2,1)} %get-tuple-element.106), channel_id=1, source_target_pairs={{0,8},{2,10},{4,12},{6,14},{8,0},{10,2},{12,4},{14,6},{16,24},{18,... | collective-permute-start | bytes 786440 | tf_op jit(solution)/shard_map/ppermute | solution.py:855
  133.6 21.8 %copy-start.20 = (bf16[128,1152]{1,0:T(8,128)(2,1)}, bf16[128,1152]{1,0:T(8,128)(2,1)S(1)}, u32[]{:S(2)}) copy-start(bf16[128,1152]{1,0:T(8,128)(2,1)S(1)} %collective-permute-done.21.refs_15_) | copy-start | bytes 884740
  133.7 13.4 %collective-permute-start.18 = (bf16[128,1024]{1,0:T(8,128)(2,1)}, bf16[128,1024]{1,0:T(8,128)(2,1)S(1)}, u32[]{:S(2)}, u32[]{:S(2)}) collective-permute-start(bf16[128,1024]{1,0:T(8,128)(2,1)} %get-tuple-element.107), channel_id=1, source_target_pairs={{0,10},{2,8},{4,14},{6,12},{8,2},{10,0},{12,6},{14,4},{16,26},{18,... | collective-permute-start | bytes 786440 | tf_op jit(solution)/shard_map/ppermute | solution.py:855
  135.2 20.2 %copy-start.24 = (bf16[128,1024]{1,0:T(8,128)(2,1)}, bf16[128,1024]{1,0:T(8,128)(2,1)S(1)}, u32[]{:S(2)}) copy-start(bf16[128,1024]{1,0:T(8,128)(2,1)S(1)} %collective-permute-done.14.refs_1_) | copy-start | bytes 786436
  135.2 20.2 %collective-permute-start.19 = (bf16[128,1024]{1,0:T(8,128)(2,1)}, bf16[128,1024]{1,0:T(8,128)(2,1)S(1)}, u32[]{:S(2)}, u32[]{:S(2)}) collective-permute-start(bf16[128,1024]{1,0:T(8,128)(2,1)} %get-tuple-element.108), channel_id=1, source_target_pairs={{0,12},{2,14},{4,8},{6,10},{8,4},{10,6},{12,0},{14,2},{16,28},{18,... | collective-permute-start | bytes 786440 | tf_op jit(solution)/shard_map/ppermute | solution.py:855
  141.0 18.9 %collective-permute-start.20 = (bf16[128,1024]{1,0:T(8,128)(2,1)}, bf16[128,1024]{1,0:T(8,128)(2,1)}, u32[]{:S(2)}, u32[]{:S(2)}) collective-permute-start(bf16[128,1024]{1,0:T(8,128)(2,1)} %get-tuple-element.109), channel_id=1, source_target_pairs={{0,14},{2,12},{4,10},{6,8},{8,6},{10,4},{12,2},{14,0},{16,30},{18,... | collective-permute-start | bytes 786440 | tf_op jit(solution)/shard_map/ppermute | solution.py:855
  188.1 52.0 %copy-start.22 = (bf16[128,1024]{1,0:T(8,128)(2,1)S(1)}, bf16[128,1024]{1,0:T(8,128)(2,1)}, u32[]{:S(2)}) copy-start(bf16[128,1024]{1,0:T(8,128)(2,1)} %get-tuple-element.114) | copy-start | bytes 786436
  188.1 29.1 %all-to-all-start.1 = ((bf16[32,64,256]{2,1,0:T(8,128)(2,1)}), bf16[32,64,256]{2,1,0:T(8,128)(2,1)S(1)}, u32[]{:S(2)}, u32[]{:S(2)}) async-start(bf16[32,64,256]{2,1,0:T(8,128)(2,1)} %bitcast.37), calls=%async_computation.1 | async-start | bytes 2097152 | tf_op jit(solution)/shard_map/all_to_all | solution.py:919
  190.9 60.7 %copy-start.21 = (bf16[128,1024]{1,0:T(8,128)(2,1)S(1)}, bf16[128,1024]{1,0:T(8,128)(2,1)}, u32[]{:S(2)}) copy-start(bf16[128,1024]{1,0:T(8,128)(2,1)} %get-tuple-element.115) | copy-start | bytes 786436
  191.0 3.8 collective-permute-start.32
  191.2 18.0 %collective-permute-start.33 = (bf16[128,1024]{1,0:T(8,128)(2,1)S(1)}, bf16[128,1024]{1,0:T(8,128)(2,1)S(1)}, u32[]{:S(2)}, u32[]{:S(2)}) collective-permute-start(bf16[128,1024]{1,0:T(8,128)(2,1)S(1)} %copy-done.29), channel_id=1, source_target_pairs={{0,4},{2,6},{4,0},{6,2},{8,12},{10,14},{12,8},{14,10},{16,20},{18,... | collective-permute-start | bytes 786440 | tf_op jit(solution)/shard_map/ppermute | solution.py:855
  192.8 24.4 %collective-permute-start.34 = (bf16[128,1024]{1,0:T(8,128)(2,1)}, bf16[128,1024]{1,0:T(8,128)(2,1)S(1)}, u32[]{:S(2)}, u32[]{:S(2)}) collective-permute-start(bf16[128,1024]{1,0:T(8,128)(2,1)} %get-tuple-element.135), channel_id=1, source_target_pairs={{0,6},{2,4},{4,2},{6,0},{8,14},{10,12},{12,10},{14,8},{16,22},{18,... | collective-permute-start | bytes 786440 | tf_op jit(solution)/shard_map/ppermute | solution.py:855
  192.9 24.4 %collective-permute-start.35 = (bf16[128,1024]{1,0:T(8,128)(2,1)}, bf16[128,1024]{1,0:T(8,128)(2,1)S(1)}, u32[]{:S(2)}, u32[]{:S(2)}) collective-permute-start(bf16[128,1024]{1,0:T(8,128)(2,1)} %get-tuple-element.136), channel_id=1, source_target_pairs={{0,8},{2,10},{4,12},{6,14},{8,0},{10,2},{12,4},{14,6},{16,24},{18,... | collective-permute-start | bytes 786440 | tf_op jit(solution)/shard_map/ppermute | solution.py:855
  194.6 26.8 %collective-permute-start.36 = (bf16[128,1024]{1,0:T(8,128)(2,1)}, bf16[128,1024]{1,0:T(8,128)(2,1)S(1)}, u32[]{:S(2)}, u32[]{:S(2)}) collective-permute-start(bf16[128,1024]{1,0:T(8,128)(2,1)} %get-tuple-element.137), channel_id=1, source_target_pairs={{0,10},{2,8},{4,14},{6,12},{8,2},{10,0},{12,6},{14,4},{16,26},{18,... | collective-permute-start | bytes 786440 | tf_op jit(solution)/shard_map/ppermute | solution.py:855
  194.7 38.8 %copy-start.7 = (bf16[128,1024]{1,0:T(8,128)(2,1)}, bf16[128,1024]{1,0:T(8,128)(2,1)S(1)}, u32[]{:S(2)}) copy-start(bf16[128,1024]{1,0:T(8,128)(2,1)S(1)} %collective-permute-done.32.refs_1_) | copy-start | bytes 786436
  194.7 34.1 %collective-permute-start.37 = (bf16[128,1024]{1,0:T(8,128)(2,1)}, bf16[128,1024]{1,0:T(8,128)(2,1)S(1)}, u32[]{:S(2)}, u32[]{:S(2)}) collective-permute-start(bf16[128,1024]{1,0:T(8,128)(2,1)} %get-tuple-element.138), channel_id=1, source_target_pairs={{0,12},{2,14},{4,8},{6,10},{8,4},{10,6},{12,0},{14,2},{16,28},{18,... | collective-permute-start | bytes 786440 | tf_op jit(solution)/shard_map/ppermute | solution.py:855
  209.3 24.2 %copy-start.8 = (bf16[128,1024]{1,0:T(8,128)(2,1)}, bf16[128,1024]{1,0:T(8,128)(2,1)S(1)}, u32[]{:S(2)}) copy-start(bf16[128,1024]{1,0:T(8,128)(2,1)S(1)} %collective-permute-done.33.refs_2_) | copy-start | bytes 786436
  209.3 24.2 %collective-permute-start.38 = (bf16[128,1024]{1,0:T(8,128)(2,1)}, bf16[128,1024]{1,0:T(8,128)(2,1)S(1)}, u32[]{:S(2)}, u32[]{:S(2)}) collective-permute-start(bf16[128,1024]{1,0:T(8,128)(2,1)} %get-tuple-element.139), channel_id=1, source_target_pairs={{0,14},{2,12},{4,10},{6,8},{8,6},{10,4},{12,2},{14,0},{16,30},{18,... | collective-permute-start | bytes 786440 | tf_op jit(solution)/shard_map/ppermute | solution.py:855
  217.3 22.8 %copy-start.23 = (bf16[128,1024]{1,0:T(8,128)(2,1)S(1)}, bf16[128,1024]{1,0:T(8,128)(2,1)}, u32[]{:S(2)}) copy-start(bf16[128,1024]{1,0:T(8,128)(2,1)} %get-tuple-element.113) | copy-start | bytes 786436
  217.3 16.2 %copy-start.9 = (bf16[128,1024]{1,0:T(8,128)(2,1)}, bf16[128,1024]{1,0:T(8,128)(2,1)S(1)}, u32[]{:S(2)}) copy-start(bf16[128,1024]{1,0:T(8,128)(2,1)S(1)} %collective-permute-done.34.refs_3_) | copy-start | bytes 786436
  217.3 16.2 %copy-start.10 = (bf16[128,1024]{1,0:T(8,128)(2,1)}, bf16[128,1024]{1,0:T(8,128)(2,1)S(1)}, u32[]{:S(2)}) copy-start(bf16[128,1024]{1,0:T(8,128)(2,1)S(1)} %collective-permute-done.35.refs_4_) | copy-start | bytes 786436
  238.5 9.4 %collective-permute-start.40 = (bf16[256,512]{1,0:T(8,128)(2,1)}, bf16[256,512]{1,0:T(8,128)(2,1)S(1)}, u32[]{:S(2)}, u32[]{:S(2)}) collective-permute-start(bf16[256,512]{1,0:T(8,128)(2,1)} %get-tuple-element.143), channel_id=1, source_target_pairs={{0,1},{1,0},{2,3},{3,2},{4,5},{5,4},{6,7},{7,6},{8,9},{9,8},{10,11... | collective-permute-start | bytes 786440 | tf_op jit(solution)/shard_map/ppermute | solution.py:20
  240.1 11.5 %collective-permute-start.22 = (bf16[128,1024]{1,0:T(8,128)(2,1)S(1)}, bf16[128,1024]{1,0:T(8,128)(2,1)S(1)}, u32[]{:S(2)}, u32[]{:S(2)}) collective-permute-start(bf16[128,1024]{1,0:T(8,128)(2,1)S(1)} %copy-done.23), channel_id=1, source_target_pairs={{0,2},{2,0},{4,6},{6,4},{8,10},{10,8},{12,14},{14,12},{16,18},{18,... | collective-permute-start | bytes 786440 | tf_op jit(solution)/shard_map/ppermute | solution.py:855
  240.1 12.3 %collective-permute-start.23 = (bf16[128,1024]{1,0:T(8,128)(2,1)S(1)}, bf16[128,1024]{1,0:T(8,128)(2,1)S(1)}, u32[]{:S(2)}, u32[]{:S(2)}) collective-permute-start(bf16[128,1024]{1,0:T(8,128)(2,1)S(1)} %copy-done.22), channel_id=1, source_target_pairs={{0,4},{2,6},{4,0},{6,2},{8,12},{10,14},{12,8},{14,10},{16,20},{18,... | collective-permute-start | bytes 786440 | tf_op jit(solution)/shard_map/ppermute | solution.py:855
  240.7 12.9 %collective-permute-start.39 = (bf16[256,512]{1,0:T(8,128)(2,1)}, bf16[256,512]{1,0:T(8,128)(2,1)S(1)}, u32[]{:S(2)}, u32[]{:S(2)}) collective-permute-start(bf16[256,512]{1,0:T(8,128)(2,1)} %get-tuple-element.141), channel_id=1, source_target_pairs={{0,1},{1,0},{2,3},{3,2},{4,5},{5,4},{6,7},{7,6},{8,9},{9,8},{10,11... | collective-permute-start | bytes 786440 | tf_op jit(solution)/shard_map/ppermute | solution.py:20
  249.1 13.7 %collective-permute-start.41 = (bf16[256,512]{1,0:T(8,128)(2,1)S(1)}, bf16[256,512]{1,0:T(8,128)(2,1)S(1)}, u32[]{:S(2)}, u32[]{:S(2)}) collective-permute-start(bf16[256,512]{1,0:T(8,128)(2,1)S(1)} %add_convert_fusion.1), channel_id=1, source_target_pairs={{0,16},{2,18},{4,20},{6,22},{8,24},{10,26},{12,28},{14,30},{16,0},... | collective-permute-start | bytes 786440 | tf_op jit(solution)/shard_map/ppermute | solution.py:851
  251.6 12.4 %collective-permute-start.24 = (bf16[128,1024]{1,0:T(8,128)(2,1)S(1)}, bf16[128,1024]{1,0:T(8,128)(2,1)S(1)}, u32[]{:S(2)}, u32[]{:S(2)}) collective-permute-start(bf16[128,1024]{1,0:T(8,128)(2,1)S(1)} %copy-done.21), channel_id=1, source_target_pairs={{0,6},{2,4},{4,2},{6,0},{8,14},{10,12},{12,10},{14,8},{16,22},{18,... | collective-permute-start | bytes 786440 | tf_op jit(solution)/shard_map/ppermute | solution.py:855
  251.6 18.2 %collective-permute-start.25 = (bf16[128,1024]{1,0:T(8,128)(2,1)}, bf16[128,1024]{1,0:T(8,128)(2,1)}, u32[]{:S(2)}, u32[]{:S(2)}) collective-permute-start(bf16[128,1024]{1,0:T(8,128)(2,1)} %get-tuple-element.116), channel_id=1, source_target_pairs={{0,8},{2,10},{4,12},{6,14},{8,0},{10,2},{12,4},{14,6},{16,24},{18,... | collective-permute-start | bytes 786440 | tf_op jit(solution)/shard_map/ppermute | solution.py:855
  252.4 19.3 %collective-permute-start.26 = (bf16[128,1024]{1,0:T(8,128)(2,1)}, bf16[128,1024]{1,0:T(8,128)(2,1)}, u32[]{:S(2)}, u32[]{:S(2)}) collective-permute-start(bf16[128,1024]{1,0:T(8,128)(2,1)} %get-tuple-element.117), channel_id=1, source_target_pairs={{0,10},{2,8},{4,14},{6,12},{8,2},{10,0},{12,6},{14,4},{16,26},{18,... | collective-permute-start | bytes 786440 | tf_op jit(solution)/shard_map/ppermute | solution.py:855
  253.6 29.3 %collective-permute-start.27 = (bf16[128,1024]{1,0:T(8,128)(2,1)}, bf16[128,1024]{1,0:T(8,128)(2,1)}, u32[]{:S(2)}, u32[]{:S(2)}) collective-permute-start(bf16[128,1024]{1,0:T(8,128)(2,1)} %get-tuple-element.118), channel_id=1, source_target_pairs={{0,12},{2,14},{4,8},{6,10},{8,4},{10,6},{12,0},{14,2},{16,28},{18,... | collective-permute-start | bytes 786440 | tf_op jit(solution)/shard_map/ppermute | solution.py:855
  262.8 33.4 %collective-permute-start.28 = (bf16[128,1024]{1,0:T(8,128)(2,1)}, bf16[128,1024]{1,0:T(8,128)(2,1)}, u32[]{:S(2)}, u32[]{:S(2)}) collective-permute-start(bf16[128,1024]{1,0:T(8,128)(2,1)} %get-tuple-element.119), channel_id=1, source_target_pairs={{0,14},{2,12},{4,10},{6,8},{8,6},{10,4},{12,2},{14,0},{16,30},{18,... | collective-permute-start | bytes 786440 | tf_op jit(solution)/shard_map/ppermute | solution.py:855
  264.0 32.2 %collective-permute-start.42 = (bf16[256,512]{1,0:T(8,128)(2,1)S(1)}, bf16[256,512]{1,0:T(8,128)(2,1)}, u32[]{:S(2)}, u32[]{:S(2)}) collective-permute-start(bf16[256,512]{1,0:T(8,128)(2,1)S(1)} %add_convert_fusion.mixed_ref), channel_id=1, source_target_pairs={{0,1},{1,0},{2,3},{3,2},{4,5},{5,4},{6,7},{7,6},{8,9},{9,8},{10,11... | collective-permute-start | bytes 786440 | tf_op jit(solution)/shard_map/ppermute | solution.py:20
  265.6 72.8 %all-to-all-start.2 = ((bf16[32,2,64,256]{3,2,1,0:T(8,128)(2,1)}), bf16[32,2,64,256]{3,2,1,0:T(8,128)(2,1)S(1)}, u32[]{:S(2)}, u32[]{:S(2)}) async-start(bf16[32,2,64,256]{3,2,1,0:T(8,128)(2,1)} %bitcast.34), calls=%async_computation.2 | async-start | bytes 4194304 | tf_op jit(solution)/shard_map/all_to_all | solution.py:919
  269.6 114.5 %reduce-scatter.2.cloned.1.call-start = ((), (), s32[]{:S(2)}) async-start(), calls=%async_computation.6 | async-start | bytes 3620864 | tf_op jit(solution)/shard_map/reduce_scatter | solution.py:1023
  307.2 16.1 %copy-start.17 = (f32[8,256]{1,0:T(8,128)S(1)}, f32[8,256]{1,0:T(8,128)}, u32[]{:S(2)}) copy-start(f32[8,256]{1,0:T(8,128)} %get-tuple-element.155.inner_ref) | copy-start | bytes 24580
  311.6 10.4 %collective-permute-start.30 = (bf16[256,512]{1,0:T(8,128)(2,1)}, bf16[256,512]{1,0:T(8,128)(2,1)S(1)}, u32[]{:S(2)}, u32[]{:S(2)}) collective-permute-start(bf16[256,512]{1,0:T(8,128)(2,1)} %get-tuple-element.123), channel_id=1, source_target_pairs={{0,1},{1,0},{2,3},{3,2},{4,5},{5,4},{6,7},{7,6},{8,9},{9,8},{10,11... | collective-permute-start | bytes 786440 | tf_op jit(solution)/shard_map/ppermute | solution.py:20
  311.6 16.0 %collective-permute-start.29 = (bf16[256,512]{1,0:T(8,128)(2,1)}, bf16[256,512]{1,0:T(8,128)(2,1)S(1)}, u32[]{:S(2)}, u32[]{:S(2)}) collective-permute-start(bf16[256,512]{1,0:T(8,128)(2,1)} %get-tuple-element.121), channel_id=1, source_target_pairs={{0,1},{1,0},{2,3},{3,2},{4,5},{5,4},{6,7},{7,6},{8,9},{9,8},{10,11... | collective-permute-start | bytes 786440 | tf_op jit(solution)/shard_map/ppermute | solution.py:20
  323.2 11.1 %collective-permute-start.31 = (bf16[256,512]{1,0:T(8,128)(2,1)S(1)}, bf16[256,512]{1,0:T(8,128)(2,1)S(1)}, u32[]{:S(2)}, u32[]{:S(2)}) collective-permute-start(bf16[256,512]{1,0:T(8,128)(2,1)S(1)} %add_convert_fusion.2), channel_id=1, source_target_pairs={{0,16},{2,18},{4,20},{6,22},{8,24},{10,26},{12,28},{14,30},{16,0},... | collective-permute-start | bytes 786440 | tf_op jit(solution)/shard_map/ppermute | solution.py:851
  323.2 11.0 %collective-permute-start.43 = (bf16[256,512]{1,0:T(8,128)(2,1)}, bf16[256,512]{1,0:T(8,128)(2,1)S(1)}, u32[]{:S(2)}, u32[]{:S(2)}) collective-permute-start(bf16[256,512]{1,0:T(8,128)(2,1)} %get-tuple-element.154), channel_id=1, source_target_pairs={{0,1},{1,0},{2,3},{3,2},{4,5},{5,4},{6,7},{7,6},{8,9},{9,8},{10,11... | collective-permute-start | bytes 786440 | tf_op jit(solution)/shard_map/ppermute | solution.py:20
  323.3 10.9 %collective-permute-start.44 = (f32[8,256]{1,0:T(8,128)S(1)}, f32[8,256]{1,0:T(8,128)S(1)}, u32[]{:S(2)}, u32[]{:S(2)}) collective-permute-start(f32[8,256]{1,0:T(8,128)S(1)} %copy-done.17), channel_id=1, source_target_pairs={{0,1},{1,0},{2,3},{3,2},{4,5},{5,4},{6,7},{7,6},{8,9},{9,8},{10,11... | collective-permute-start | bytes 24584 | tf_op jit(solution)/shard_map/ppermute | solution.py:20
  338.4 24.7 %all-to-all-start.3 = ((bf16[16,16,1024]{2,1,0:T(8,128)(2,1)}), bf16[16,16,1024]{2,1,0:T(8,128)(2,1)}, u32[]{:S(2)}, u32[]{:S(2)}) async-start(bf16[16,16,1024]{2,1,0:T(8,128)(2,1)} %bitcast.36), calls=%async_computation.3 | async-start | bytes 1048576 | tf_op jit(solution)/shard_map/all_to_all | solution.py:1056
  365.7 28.3 %all-to-all-start.4 = ((bf16[16,16,1024]{2,1,0:T(8,128)(2,1)}), bf16[16,16,1024]{2,1,0:T(8,128)(2,1)S(1)}, u32[]{:S(2)}, u32[]{:S(2)}) async-start(bf16[16,16,1024]{2,1,0:T(8,128)(2,1)} %broadcast_select_fusion), calls=%async_computation.4 | async-start | bytes 1048576 | tf_op jit(solution)/shard_map/all_to_all | solution.py:1060
  384.8 7.0 %collective-permute-start.45 = (bf16[64,128]{1,0:T(8,128)(2,1)S(1)}, bf16[64,128]{1,0:T(8,128)(2,1)S(1)}, u32[]{:S(2)}, u32[]{:S(2)}) collective-permute-start(bf16[64,128]{1,0:T(8,128)(2,1)S(1)} %slice.52), channel_id=1, source_target_pairs={{0,1},{1,0},{2,3},{3,2},{4,5},{5,4},{6,7},{7,6},{8,9},{9,8},{10,11... | collective-permute-start | bytes 49160 | tf_op jit(solution)/shard_map/ppermute | solution.py:20
  (25 other events, 115.6 us)
Sparse Core Ops, SparseCore 0:
  307.3 76.7 reduce-scatter.1
